TPU v7x, 32 devices: a whole 2x2x4 slice. The times are simulated.
32 devices in a mesh: dp: 8 (over z, core), tensor: 4 (over y, x).
Axes of the slice: x: 2, y: 2, z: 4, core: 2. Of those that a mesh axis runs over, the one named last changes fastest.
Arguments:
- layer_input: bfloat16 [8192, 2048], P(('dp', 'tensor')), may hold values from -6 to 6
- norm1_gain: bfloat16 [2048], P('dp'), may hold values from 0.25 to 1.75
- norm1_bias: bfloat16 [2048], P('dp'), may hold values from -3 to 3
- qkv_weight: bfloat16 [3, 2048, 2048], P(None, 'dp', 'tensor'), may hold values from -0.125 to 0.125
- qkv_bias: bfloat16 [3, 2048], P(None, ('tensor', 'dp')), may hold values from -6 to 6
- out_weight: bfloat16 [2048, 2048], P('tensor', 'dp'), may hold values from -0.5 to 0.5
- norm2_gain: bfloat16 [2048], P('dp'), may hold values from 0.25 to 1.75
- norm2_bias: bfloat16 [2048], P('dp'), may hold values from -3 to 3
- gate_up_weight: bfloat16 [2, 2048, 5632], P(None, 'dp', 'tensor'), may hold values from -0.125 to 0.125
- down_weight: bfloat16 [5632, 2048], P('tensor', 'dp'), may hold values from -0.15625 to 0.15625
- out_cotangent: bfloat16 [8192, 2048], P(('dp', 'tensor')), may hold values from -6 to 6
Outputs:
- layer_output: bfloat16 [8192, 2048], P(('dp', 'tensor'))
- grad_input: float32 [8192, 2048], P(('dp', 'tensor'))
- grad_norm1_gain: float32 [2048], P('dp')
- grad_norm1_bias: float32 [2048], P('dp')
- grad_qkv_weight: float32 [3, 2048, 2048], P(None, 'dp', 'tensor')
- grad_qkv_bias: float32 [3, 2048], P(None, ('tensor', 'dp'))
- grad_out_weight: float32 [2048, 2048], P('tensor', 'dp')
- grad_norm2_gain: float32 [2048], P('dp')
- grad_norm2_bias: float32 [2048], P('dp')
- grad_gate_up_weight: float32 [2, 2048, 5632], P(None, 'dp', 'tensor')
- grad_down_weight: float32 [5632, 2048], P('tensor', 'dp')
All inputs are finite; a program needn't handle non-finite values.
Results may differ from a plain program's by a relative error of at most 0.025.
The roundings to bfloat16 on the way count: a program that leaves them out, or rounds other values in their place, can miss the bound.
Values may be sent and summed in bfloat16 or wider, within the bound.
No kernel may reach another device: no remote copies, remote signals or barrier semaphores. Data moves between devices by JAX's collectives and lax.ppermute only.
A program may use at most 192 MiB of HBM per device.

v0:
```python
import jax
import jax.numpy as jnp
from jax import lax
from jax.sharding import PartitionSpec as P

HEAD_DIM = 64
ROT = 16
SEQ_LEN = 512


epsilon = 1e-05


def layer_norm(values):
    row_mean = jnp.mean(values, axis=-1, keepdims=True)
    centered = values - row_mean
    inv_sigma = lax.rsqrt(jnp.mean(centered * centered, axis=-1, keepdims=True) + epsilon)
    return (centered * inv_sigma, inv_sigma)


def norm_back(grad_hat, normed, inv_sigma):
    return inv_sigma * (
        grad_hat
        - jnp.mean(grad_hat, axis=-1, keepdims=True)
        - normed * jnp.mean(grad_hat * normed, axis=-1, keepdims=True)
    )


def rotary_tables(length, rot_dims):
    half_rot = rot_dims // 2
    frequency = 10000.0 ** (-(2.0 * jnp.arange(half_rot, dtype=jnp.float32)) / rot_dims)
    angles = jnp.arange(length, dtype=jnp.float32)[:, None] * frequency[None, :]
    return (jnp.cos(angles)[:, None, :], jnp.sin(angles)[:, None, :])


def rotate(tensor, cosine_table, sine_table, rot_dims):
    half_rot = rot_dims // 2
    lower_half = tensor[..., :half_rot]
    upper_half = tensor[..., half_rot:rot_dims]
    return jnp.concatenate(
        [
            lower_half * cosine_table - upper_half * sine_table,
            upper_half * cosine_table + lower_half * sine_table,
            tensor[..., rot_dims:],
        ],
        axis=-1,
    )


def unrotate(tensor, cosine_table, sine_table, rot_dims):
    half_rot = rot_dims // 2
    lower_half = tensor[..., :half_rot]
    upper_half = tensor[..., half_rot:rot_dims]
    return jnp.concatenate(
        [
            lower_half * cosine_table + upper_half * sine_table,
            upper_half * cosine_table - lower_half * sine_table,
            tensor[..., rot_dims:],
        ],
        axis=-1,
    )


def causal_mask(length):
    places = jnp.arange(length)
    return places[:, None] >= places[None, :]


def attention_params(norm1_gain, norm1_bias, qkv_weight, qkv_bias, out_weight):
    return (
        lax.all_gather(norm1_gain, "dp", axis=0, tiled=True),
        lax.all_gather(norm1_bias, "dp", axis=0, tiled=True),
        lax.all_gather(qkv_weight, "dp", axis=1, tiled=True),
        lax.all_gather(qkv_bias, "dp", axis=1, tiled=True),
        lax.all_gather(out_weight, "dp", axis=1, tiled=True),
    )


def mlp_params(norm2_gain, norm2_bias, gate_up_weight, down_weight):
    return (
        lax.all_gather(norm2_gain, "dp", axis=0, tiled=True),
        lax.all_gather(norm2_bias, "dp", axis=0, tiled=True),
        lax.all_gather(gate_up_weight, "dp", axis=1, tiled=True),
        lax.all_gather(down_weight, "dp", axis=1, tiled=True),
    )


def collect_rows(row_block):
    return lax.all_gather(row_block, "tensor", axis=0, tiled=True)


def spread_rows(term_fn, row_total):
    return lax.psum_scatter(
        term_fn(jnp.int32(0), row_total * lax.axis_size("tensor")).astype(jnp.bfloat16),
        "tensor",
        scatter_dimension=0,
        tiled=True,
    ).astype(jnp.float32)


def shards(
    layer_input,
    norm1_gain,
    norm1_bias,
    qkv_weight,
    qkv_bias,
    out_weight,
    norm2_gain,
    norm2_bias,
    gate_up_weight,
    down_weight,
    out_cotangent,
):
    local_rows = layer_input.shape[0]
    score_scale = HEAD_DIM ** (-0.5)
    cosine_table, sine_table = rotary_tables(SEQ_LEN, ROT)
    causal = causal_mask(SEQ_LEN)
    gain_one, bias_one, qkv_local, bias_local, out_local = attention_params(
        norm1_gain, norm1_bias, qkv_weight, qkv_bias, out_weight
    )
    x_float = layer_input.astype(jnp.float32)
    hat_one, inv_one = layer_norm(x_float)
    normed_one = (hat_one * gain_one.astype(jnp.float32) + bias_one.astype(jnp.float32)).astype(
        jnp.bfloat16
    )
    rows_one = collect_rows(normed_one)
    group_rows = rows_one.shape[0]
    seq_count = group_rows // SEQ_LEN
    head_cols = qkv_local.shape[2]
    heads_here = head_cols // HEAD_DIM
    qkv_all = (
        jnp.einsum("rd,cdk->crk", rows_one, qkv_local, preferred_element_type=jnp.float32)
        + bias_local.astype(jnp.float32)[:, None, :]
    )
    qkv_all = qkv_all.reshape(3, seq_count, SEQ_LEN, heads_here, HEAD_DIM)
    query_rot = rotate(qkv_all[0], cosine_table, sine_table, ROT).astype(jnp.bfloat16)
    key_rot = rotate(qkv_all[1], cosine_table, sine_table, ROT).astype(jnp.bfloat16)
    value_heads = qkv_all[2].astype(jnp.bfloat16)

    def attend(pieces):
        query_seq, key_seq, value_seq = pieces
        scores = (
            jnp.einsum("qhd,khd->hqk", query_seq, key_seq, preferred_element_type=jnp.float32)
            * score_scale
        )
        scores = jnp.where(causal, scores, -jnp.inf)
        row_top = jnp.max(scores, axis=-1, keepdims=True)
        log_total = row_top + jnp.log(jnp.sum(jnp.exp(scores - row_top), axis=-1, keepdims=True))
        prob_low = jnp.exp(scores - log_total).astype(jnp.bfloat16)
        context_seq = jnp.einsum(
            "hqk,khd->qhd", prob_low, value_seq, preferred_element_type=jnp.float32
        ).astype(jnp.bfloat16)
        return (context_seq, log_total[..., 0])

    context, log_totals = lax.map(attend, (query_rot, key_rot, value_heads))
    context_rows = context.reshape(group_rows, head_cols)

    def attn_term(row_start, row_count):
        return jnp.dot(context_rows, out_local, preferred_element_type=jnp.float32)

    residual = x_float + spread_rows(attn_term, local_rows)
    gain_two, bias_two, gate_up_local, down_local = mlp_params(
        norm2_gain, norm2_bias, gate_up_weight, down_weight
    )
    hat_two, inv_two = layer_norm(residual)
    normed_two = (hat_two * gain_two.astype(jnp.float32) + bias_two.astype(jnp.float32)).astype(
        jnp.bfloat16
    )
    rows_two = collect_rows(normed_two)
    gate_proj = jnp.dot(rows_two, gate_up_local[0], preferred_element_type=jnp.float32)
    up_proj = jnp.dot(rows_two, gate_up_local[1], preferred_element_type=jnp.float32)
    sigmoid_gate = jax.nn.sigmoid(gate_proj)
    silu_gate = gate_proj * sigmoid_gate
    activation = (silu_gate * up_proj).astype(jnp.bfloat16)

    def mlp_term(row_start, row_count):
        return jnp.dot(activation, down_local, preferred_element_type=jnp.float32)

    layer_output = (residual + spread_rows(mlp_term, local_rows)).astype(jnp.bfloat16)
    cot_rows = collect_rows(out_cotangent)
    gain_two, bias_two, gate_up_local, down_local = mlp_params(
        norm2_gain, norm2_bias, gate_up_weight, down_weight
    )
    grad_act = lax.dot_general(
        cot_rows, down_local, (((1,), (1,)), ((), ())), preferred_element_type=jnp.float32
    )
    grad_gate = (
        grad_act * up_proj * sigmoid_gate * (1.0 + gate_proj * (1.0 - sigmoid_gate))
    ).astype(jnp.bfloat16)
    grad_up = (grad_act * silu_gate).astype(jnp.bfloat16)
    grad_down = lax.dot_general(
        activation, cot_rows, (((0,), (0,)), ((), ())), preferred_element_type=jnp.float32
    )
    grad_wgate = lax.dot_general(
        rows_two, grad_gate, (((0,), (0,)), ((), ())), preferred_element_type=jnp.float32
    )
    grad_wup = lax.dot_general(
        rows_two, grad_up, (((0,), (0,)), ((), ())), preferred_element_type=jnp.float32
    )

    def mlp_back_term(row_start, row_count):
        gate_back = lax.dot_general(
            grad_gate,
            gate_up_local[0],
            (((1,), (1,)), ((), ())),
            preferred_element_type=jnp.float32,
        )
        up_back = lax.dot_general(
            grad_up, gate_up_local[1], (((1,), (1,)), ((), ())), preferred_element_type=jnp.float32
        )
        return gate_back + up_back

    grad_normed_two = spread_rows(mlp_back_term, local_rows)
    grad_gain_two = jnp.sum(grad_normed_two * hat_two, axis=0)
    grad_bias_two = jnp.sum(grad_normed_two, axis=0)
    grad_resid = out_cotangent.astype(jnp.float32) + norm_back(
        grad_normed_two * gain_two.astype(jnp.float32), hat_two, inv_two
    )
    mlp_shares = (
        lax.psum_scatter(
            grad_wgate.astype(jnp.bfloat16), "dp", scatter_dimension=0, tiled=True
        ).astype(jnp.float32),
        lax.psum_scatter(
            grad_wup.astype(jnp.bfloat16), "dp", scatter_dimension=0, tiled=True
        ).astype(jnp.float32),
        lax.psum_scatter(
            grad_down.astype(jnp.bfloat16), "dp", scatter_dimension=1, tiled=True
        ).astype(jnp.float32),
        lax.psum_scatter(
            grad_gain_two.astype(jnp.bfloat16), "dp", scatter_dimension=0, tiled=True
        ).astype(jnp.float32),
        lax.psum_scatter(
            grad_bias_two.astype(jnp.bfloat16), "dp", scatter_dimension=0, tiled=True
        ).astype(jnp.float32),
    )
    grad_resid_rows = collect_rows(grad_resid.astype(jnp.bfloat16))
    gain_one, bias_one, qkv_local, bias_local, out_local = attention_params(
        norm1_gain, norm1_bias, qkv_weight, qkv_bias, out_weight
    )
    grad_context = lax.dot_general(
        grad_resid_rows, out_local, (((1,), (1,)), ((), ())), preferred_element_type=jnp.float32
    ).astype(jnp.bfloat16)
    grad_wout = lax.dot_general(
        context_rows, grad_resid_rows, (((0,), (0,)), ((), ())), preferred_element_type=jnp.float32
    )
    grad_ctx_heads = grad_context.reshape(seq_count, SEQ_LEN, heads_here, HEAD_DIM)

    def attend_back(pieces):
        query_seq, key_seq, value_seq, context_seq, grad_ctx_seq, total_seq = pieces
        scores = (
            jnp.einsum("qhd,khd->hqk", query_seq, key_seq, preferred_element_type=jnp.float32)
            * score_scale
        )
        scores = jnp.where(causal, scores, -jnp.inf)
        prob_full = jnp.exp(scores - total_seq[..., None])
        prob_low = prob_full.astype(jnp.bfloat16)
        grad_probs = jnp.einsum(
            "qhd,khd->hqk", grad_ctx_seq, value_seq, preferred_element_type=jnp.float32
        )
        delta_sum = jnp.einsum(
            "qhd,qhd->hq", grad_ctx_seq, context_seq, preferred_element_type=jnp.float32
        )
        grad_scores = (prob_full * (grad_probs - delta_sum[..., None]) * score_scale).astype(
            jnp.bfloat16
        )
        grad_value_seq = jnp.einsum(
            "hqk,qhd->khd", prob_low, grad_ctx_seq, preferred_element_type=jnp.float32
        )
        grad_query_seq = jnp.einsum(
            "hqk,khd->qhd", grad_scores, key_seq, preferred_element_type=jnp.float32
        )
        grad_key_seq = jnp.einsum(
            "hqk,qhd->khd", grad_scores, query_seq, preferred_element_type=jnp.float32
        )
        return (grad_query_seq, grad_key_seq, grad_value_seq)

    grad_query, grad_keys, grad_values = lax.map(
        attend_back, (query_rot, key_rot, value_heads, context, grad_ctx_heads, log_totals)
    )
    grad_query = unrotate(grad_query, cosine_table, sine_table, ROT)
    grad_keys = unrotate(grad_keys, cosine_table, sine_table, ROT)
    grad_pre = (
        jnp.stack([grad_query, grad_keys, grad_values])
        .astype(jnp.bfloat16)
        .reshape(3, group_rows, head_cols)
    )
    grad_bqkv = jnp.sum(grad_pre, axis=1, dtype=jnp.float32)
    grad_wqkv = jnp.einsum("rd,crk->cdk", rows_one, grad_pre, preferred_element_type=jnp.float32)

    def qkv_back_term(row_start, row_count):
        return jnp.einsum("crk,cdk->rd", grad_pre, qkv_local, preferred_element_type=jnp.float32)

    grad_normed_one = spread_rows(qkv_back_term, local_rows)
    grad_gain_one = jnp.sum(grad_normed_one * hat_one, axis=0)
    grad_bias_one = jnp.sum(grad_normed_one, axis=0)
    grad_input = grad_resid + norm_back(
        grad_normed_one * gain_one.astype(jnp.float32), hat_one, inv_one
    )
    attn_shares = (
        lax.psum_scatter(
            grad_wqkv.astype(jnp.bfloat16), "dp", scatter_dimension=1, tiled=True
        ).astype(jnp.float32),
        lax.psum_scatter(
            grad_bqkv.astype(jnp.bfloat16), "dp", scatter_dimension=1, tiled=True
        ).astype(jnp.float32),
        lax.psum_scatter(
            grad_wout.astype(jnp.bfloat16), "dp", scatter_dimension=1, tiled=True
        ).astype(jnp.float32),
        lax.psum_scatter(
            grad_gain_one.astype(jnp.bfloat16), "dp", scatter_dimension=0, tiled=True
        ).astype(jnp.float32),
        lax.psum_scatter(
            grad_bias_one.astype(jnp.bfloat16), "dp", scatter_dimension=0, tiled=True
        ).astype(jnp.float32),
    )
    norm_totals = lax.psum((attn_shares[3], attn_shares[4], mlp_shares[3], mlp_shares[4]), "tensor")
    grad_gate_up = jnp.stack([mlp_shares[0], mlp_shares[1]])
    return (
        layer_output,
        grad_input,
        norm_totals[0],
        norm_totals[1],
        attn_shares[0],
        attn_shares[1],
        attn_shares[2],
        norm_totals[2],
        norm_totals[3],
        grad_gate_up,
        mlp_shares[2],
    )


def solution(mesh):
    placed = (
        P(("dp", "tensor"), None),
        P("dp"),
        P("dp"),
        P(None, "dp", "tensor"),
        P(None, ("tensor", "dp")),
        P("tensor", "dp"),
        P("dp"),
        P("dp"),
        P(None, "dp", "tensor"),
        P("tensor", "dp"),
        P(("dp", "tensor"), None),
    )
    return jax.shard_map(
        shards,
        mesh=mesh,
        in_specs=placed,
        out_specs=(
            P(("dp", "tensor"), None),
            P(("dp", "tensor"), None),
            P("dp"),
            P("dp"),
            P(None, "dp", "tensor"),
            P(None, ("tensor", "dp")),
            P("tensor", "dp"),
            P("dp"),
            P("dp"),
            P(None, "dp", "tensor"),
            P("tensor", "dp"),
        ),
        check_vma=False,
    )
```

profile of v0, /device:TPU:0, one launch (start us, length us, event | category | flops | bytes accessed | tf_op | source)
XLA Modules:
  0.0 1151.3 jit_solution(1779346989243993215)
XLA Ops:
  11.1 13.5 %all-gather = bf16[8,1,256]{2,1,0:T(2,128)(2,1)S(1)} all-gather(bf16[1,1,256]{2,1,0:T(2,128)(2,1)S(1)} %reshape.169), channel_id=1, replica_groups=mesh['dp'=8,'tensor'=4] {'dp'}, dimensions={0}, use_global_device_ids=true | all-gather | bytes 4608 | tf_op jit(solution)/shard_map/all_gather | solution.py:71
  47.4 40.1 %all-gather.14.cloned.1.call-done = bf16[1024,2048]{1,0:T(8,128)(2,1)} async-done(((bf16[256,2048]{1,0:T(8,128)(2,1)}), bf16[1024,2048]{1,0:T(8,128)(2,1)}) %all-gather.14.cloned.1.call-update) | async-done | bytes 4194320 | tf_op jit(solution)/shard_map/all_gather | solution.py:89
  87.6 66.3 %all-gather.16.cloned.1.call-done = bf16[3,2048,512]{2,1,0:T(8,128)(2,1)} async-done(((bf16[3,256,512]{2,1,0:T(8,128)(2,1)}), bf16[3,2048,512]{2,1,0:T(8,128)(2,1)}) %all-gather.16.cloned.1.call-update) | async-done | bytes 6291472 | tf_op jit(solution)/shard_map/all_gather | solution.py:73
  193.2 13.5 %while.28 = (s32[]{:T(128)}, bf16[2,512,8,64]{1,3,2,0:T(8,128)(2,1)}, f32[2,8,512]{2,1,0:T(8,128)S(1)}, bf16[2,512,8,64]{1,3,2,0:T(8,128)(2,1)}, bf16[2,512,8,64...) while((s32[]{:T(128)}, bf16[2,512,8,64]{1,3,2,0:T(8,128)(2,1)}, ...), condition=%wide.region_5.6_spmd.clone, body=%wide.region_2.5_spmd.clone.sunk | while | flops 560459776 | bytes 41027748 | solution.py:155
  236.1 31.8 %reduce-scatter.13.cloned.1.call-done = bf16[256,2048]{1,0:T(8,128)(2,1)} async-done(((bf16[1024,2048]{1,0:T(8,128)(2,1)}), bf16[256,2048]{1,0:T(8,128)(2,1)}) %reduce-scatter.13.cloned.1.call-update) | async-done | bytes 1048592 | tf_op jit(solution)/shard_map/reduce_scatter | solution.py:93
  274.5 103.0 %all-gather.22.cloned.1.call-done = bf16[2,2048,1408]{2,1,0:T(8,128)(2,1)} async-done(((bf16[2,256,1408]{2,1,0:T(8,128)(2,1)}), bf16[2,2048,1408]{2,1,0:T(8,128)(2,1)}) %all-gather.22.cloned.1.call-update) | async-done | bytes 11534352 | tf_op jit(solution)/shard_map/all_gather | solution.py:83
  377.5 53.1 %all-gather.20.cloned.1.call-done = bf16[1024,2048]{1,0:T(8,128)(2,1)} async-done(((bf16[256,2048]{1,0:T(8,128)(2,1)}), bf16[1024,2048]{1,0:T(8,128)(2,1)}) %all-gather.20.cloned.1.call-update) | async-done | bytes 4194320 | tf_op jit(solution)/shard_map/all_gather | solution.py:89
  430.6 12.5 %fusion.57 = f32[1024,1408]{1,0:T(8,128)} fusion(bf16[1024,2048]{1,0:T(8,128)(2,1)} %all-gather.20.cloned.1.call-done, bf16[2,2048,1408]{2,1,0:T(8,128)(2,1)} %all-gather.22.cloned.1.call-done), kind=kOutput, calls=%fused_computation.78 | convolution fusion | flops 5905580032 | bytes 15728640 | tf_op jit(solution)/shard_map/dot_general | solution.py:170
  451.6 33.5 %all-gather.26.cloned.1.call-done = bf16[1024,2048]{1,0:T(8,128)(2,1)} async-done(((bf16[256,2048]{1,0:T(8,128)(2,1)}), bf16[1024,2048]{1,0:T(8,128)(2,1)}) %all-gather.26.cloned.1.call-update) | async-done | bytes 4194320 | tf_op jit(solution)/shard_map/all_gather | solution.py:89
  485.1 62.4 %all-gather.24.cloned.1.call-done = bf16[1408,2048]{1,0:T(8,128)(2,1)} async-done(((bf16[1408,256]{1,0:T(8,128)(2,1)}), bf16[1408,2048]{1,0:T(8,128)(2,1)}) %all-gather.24.cloned.1.call-update) | async-done | bytes 5767184 | tf_op jit(solution)/shard_map/all_gather | solution.py:84
  547.5 16.7 %multiply_convert_fusion.1 = (bf16[1024,1408]{1,0:T(8,128)(2,1)}, bf16[1024,1408]{1,0:T(8,128)(2,1)}, bf16[1024,1408]{1,0:T(8,128)(2,1)}) fusion(f32[1024,1408]{1,0:T(8,128)} %fusion.57, f32[1024,1408]{1,0:T(8,128)} %fusion.59, bf16[1024,2048]{1,0:T(8,128)(2,1)} %all-gather.26.cloned.1.call-done, bf16[1408,2048]{1,0:T(8,128)(2,1)} %all-gather.24.cloned.1.call-done), kind=kOutput, calls=%fused_computation.72 | convolution fusion | flops 5927206912 | bytes 30146560 | tf_op jit(solution)/shard_map/dot_general | solution.py:184
  584.4 50.7 %reduce-scatter.17.cloned.1.call-done = bf16[256,2048]{1,0:T(8,128)(2,1)} async-done(((bf16[1024,2048]{1,0:T(8,128)(2,1)}), bf16[256,2048]{1,0:T(8,128)(2,1)}) %reduce-scatter.17.cloned.1.call-update) | async-done | bytes 1048592 | tf_op jit(solution)/shard_map/reduce_scatter | solution.py:93
  673.4 20.0 %all-gather.28.cloned.1.call-done = bf16[1024,2048]{1,0:T(8,128)(2,1)} async-done(((bf16[256,2048]{1,0:T(8,128)(2,1)}), bf16[1024,2048]{1,0:T(8,128)(2,1)}) %all-gather.28.cloned.1.call-update) | async-done | bytes 4194320 | tf_op jit(solution)/shard_map/all_gather | solution.py:89
  704.5 44.3 %while.29 = (s32[]{:T(128)}, f32[2,512,8,64]{1,3,2,0:T(8,128)}, f32[2,512,8,64]{1,3,2,0:T(8,128)}, bf16[2,512,8,64]{1,3,2,0:T(8,128)(2,1)}, bf16[2,512,8,64]{1,3...) while((s32[]{:T(128)}, f32[2,512,8,64]{1,3,2,0:T(8,128)}, ...), condition=%wide.region_14.15_spmd.clone, body=%wide.region_13.14_spmd.clone.sunk | while | flops 1366552576 | bytes 111810008 | solution.py:277
  785.9 11.2 bitcast_convert_fusion.1
  797.2 11.0 convolution_convert_fusion.3
  808.2 11.5 convert_bitcast_fusion
  826.0 65.6 %reduce-scatter.27.cloned.1.call-done = bf16[256,1408]{1,0:T(8,128)(2,1)} async-done(((bf16[2048,1408]{1,0:T(8,128)(2,1)}), bf16[256,1408]{1,0:T(8,128)(2,1)}) %reduce-scatter.27.cloned.1.call-update) | async-done | bytes 720912 | tf_op jit(solution)/shard_map/reduce_scatter | solution.py:223
  894.8 28.5 %reduce-scatter.31.cloned.1.call-done = bf16[64,3]{1,0:T(8,128)(2,1)} async-done(((bf16[512,3]{1,0:T(8,128)(2,1)}), bf16[64,3]{1,0:T(8,128)(2,1)}) %reduce-scatter.31.cloned.1.call-update) | async-done | bytes 400
  924.7 35.4 %reduce-scatter.23.cloned.1.call-done = bf16[512,256]{1,0:T(8,128)(2,1)} async-done(((bf16[512,2048]{1,0:T(8,128)(2,1)}), bf16[512,256]{1,0:T(8,128)(2,1)}) %reduce-scatter.23.cloned.1.call-update) | async-done | bytes 262160 | tf_op jit(solution)/shard_map/reduce_scatter | solution.py:306
  961.9 52.3 %reduce-scatter.19.cloned.1.call-done = bf16[256,2048]{1,0:T(8,128)(2,1)} async-done(((bf16[1024,2048]{1,0:T(8,128)(2,1)}), bf16[256,2048]{1,0:T(8,128)(2,1)}) %reduce-scatter.19.cloned.1.call-update) | async-done | bytes 1048592 | tf_op jit(solution)/shard_map/reduce_scatter | solution.py:93
  1017.8 28.4 %all-reduce.5 = (bf16[2048]{0:T(1024)(128)(2,1)S(1)}, bf16[2048]{0:T(1024)(128)(2,1)S(1)}, bf16[2048]{0:T(1024)(128)(2,1)S(1)}, bf16[2048]{0:T(1024)(128)(2,1)S(1)}) all-reduce(bf16[2048]{0:T(1024)(128)(2,1)S(1)} %get-tuple-element.259, bf16[2048]{0:T(1024)(128)(2,1)S(1)} %reduce_sum.144, ...), channel_id=6, replica_groups=mesh['dp'=8,'tensor'=4] {'dp'}, use_global_device_ids=true, to_apply=%region_19.20.clone | all-reduce | flops 8192 | bytes 32768
  1056.0 13.8 %reduce-scatter.15.cloned.1.call-done = bf16[256,2048]{1,0:T(8,128)(2,1)} async-done(((bf16[1024,2048]{1,0:T(8,128)(2,1)}), bf16[256,2048]{1,0:T(8,128)(2,1)}) %reduce-scatter.15.cloned.1.call-update) | async-done | bytes 1048592 | tf_op jit(solution)/shard_map/reduce_scatter | solution.py:93
  1074.6 67.2 %reduce-scatter.21.cloned.1.call-done = bf16[3,256,512]{1,2,0:T(8,128)(2,1)} async-done(((bf16[3,2048,512]{1,2,0:T(8,128)(2,1)}), bf16[3,256,512]{1,2,0:T(8,128)(2,1)}) %reduce-scatter.21.cloned.1.call-update) | async-done | bytes 786448 | tf_op jit(solution)/shard_map/reduce_scatter | solution.py:300
  (321 shorter events, 306.3 us)
Async XLA Ops:
  7.2 80.4 %all-gather.14.cloned.1.call-start = ((), (), s32[]{:S(2)}) async-start(), calls=%async_computation.10 | async-start | bytes 5242880 | tf_op jit(solution)/shard_map/all_gather | solution.py:89
  35.5 118.4 %all-gather.16.cloned.1.call-start = ((), (), s32[]{:S(2)}) async-start(), calls=%async_computation.11 | async-start | bytes 7077888 | tf_op jit(solution)/shard_map/all_gather | solution.py:73
  36.3 174.0 %all-gather.18.cloned.1.call-start = ((), (), s32[]{:S(2)}) async-start(), calls=%async_computation.12 | async-start | bytes 2359296 | tf_op jit(solution)/shard_map/all_gather | solution.py:75
  37.0 230.9 %reduce-scatter.13.cloned.1.call-start = ((), (), s32[]{:S(2)}) async-start(), calls=%async_computation.13 | async-start | bytes 5242880 | tf_op jit(solution)/shard_map/reduce_scatter | solution.py:93
  216.5 160.9 %all-gather.22.cloned.1.call-start = ((), (), s32[]{:S(2)}) async-start(), calls=%async_computation.15 | async-start | bytes 12976128 | tf_op jit(solution)/shard_map/all_gather | solution.py:83
  217.1 213.5 %all-gather.20.cloned.1.call-start = ((), (), s32[]{:S(2)}) async-start(), calls=%async_computation.14 | async-start | bytes 5242880 | tf_op jit(solution)/shard_map/all_gather | solution.py:89
  226.4 412.0 %copy-start.26 = (f32[8,1,256]{2,1,0:T(1,128)}, f32[8,1,256]{2,1,0:T(1,128)S(1)}, u32[]{:S(2)}) copy-start(f32[8,1,256]{2,1,0:T(1,128)S(1)} %convert_element_type.191) | copy-start | bytes 24580
  269.6 368.8 %copy-start.34 = (f32[256]{0:T(256)}, f32[256]{0:T(256)S(1)}, u32[]{:S(2)}) copy-start(f32[256]{0:T(256)S(1)} %broadcast_multiply_fusion.4) | copy-start | bytes 3076
  271.4 367.1 %copy-start.38 = (f32[256]{0:T(256)}, f32[256]{0:T(256)S(1)}, u32[]{:S(2)}) copy-start(f32[256]{0:T(256)S(1)} %add_rsqrt_fusion) | copy-start | bytes 3076
  272.9 212.1 %all-gather.26.cloned.1.call-start = ((), (), s32[]{:S(2)}) async-start(), calls=%async_computation.18 | async-start | bytes 5242880 | tf_op jit(solution)/shard_map/all_gather | solution.py:89
  273.7 273.8 %all-gather.24.cloned.1.call-start = ((), (), s32[]{:S(2)}) async-start(), calls=%async_computation.16 | async-start | bytes 6488064 | tf_op jit(solution)/shard_map/all_gather | solution.py:84
  274.4 360.6 %reduce-scatter.17.cloned.1.call-start = ((), (), s32[]{:S(2)}) async-start(), calls=%async_computation.19 | async-start | bytes 5242880 | tf_op jit(solution)/shard_map/reduce_scatter | solution.py:93
  584.1 109.3 %all-gather.28.cloned.1.call-start = ((), (), s32[]{:S(2)}) async-start(), calls=%async_computation.20 | async-start | bytes 5242880 | tf_op jit(solution)/shard_map/all_gather | solution.py:89
  640.7 181.1 %reduce-scatter.29.cloned.1.call-start = ((), (), s32[]{:S(2)}) async-start(), calls=%async_computation.26 | async-start | bytes 6488064 | tf_op jit(solution)/shard_map/reduce_scatter | solution.py:226
  651.3 174.7 %reduce-scatter.25.cloned.1.call-start = ((), (), s32[]{:S(2)}) async-start(), calls=%async_computation.24 | async-start | bytes 6488064 | tf_op jit(solution)/shard_map/reduce_scatter | solution.py:220
  662.3 229.2 %reduce-scatter.27.cloned.1.call-start = ((), (), s32[]{:S(2)}) async-start(), calls=%async_computation.25 | async-start | bytes 6488064 | tf_op jit(solution)/shard_map/reduce_scatter | solution.py:223
  673.4 249.9 %reduce-scatter.31.cloned.1.call-start = ((), (), s32[]{:S(2)}) async-start(), calls=%async_computation.27 | async-start | bytes 147456
  779.9 180.2 %reduce-scatter.23.cloned.1.call-start = ((), (), s32[]{:S(2)}) async-start(), calls=%async_computation.23 | async-start | bytes 2359296 | tf_op jit(solution)/shard_map/reduce_scatter | solution.py:306
  785.9 228.3 %reduce-scatter.19.cloned.1.call-start = ((), (), s32[]{:S(2)}) async-start(), calls=%async_computation.21 | async-start | bytes 5242880 | tf_op jit(solution)/shard_map/reduce_scatter | solution.py:93
  797.1 272.7 %reduce-scatter.15.cloned.1.call-start = ((), (), s32[]{:S(2)}) async-start(), calls=%async_computation.17 | async-start | bytes 5242880 | tf_op jit(solution)/shard_map/reduce_scatter | solution.py:93
  808.2 333.5 %reduce-scatter.21.cloned.1.call-start = ((), (), s32[]{:S(2)}) async-start(), calls=%async_computation.22 | async-start | bytes 7077888 | tf_op jit(solution)/shard_map/reduce_scatter | solution.py:300
  894.7 175.1 %copy-start.8 = (bf16[256,2048]{1,0:T(8,128)(2,1)S(1)}, bf16[256,2048]{1,0:T(8,128)(2,1)}, u32[]{:S(2)}) copy-start(bf16[256,2048]{1,0:T(8,128)(2,1)} %reduce-scatter.13.cloned.1.call-done) | copy-start | bytes 3145732
  894.7 175.1 %copy-start.27 = (f32[8,1,256]{2,1,0:T(1,128)S(1)}, f32[8,1,256]{2,1,0:T(1,128)}, u32[]{:S(2)}) copy-start(f32[8,1,256]{2,1,0:T(1,128)} %copy-done.26) | copy-start | bytes 24580
  894.7 175.1 %copy-start.35 = (f32[256]{0:T(256)S(1)}, f32[256]{0:T(256)}, u32[]{:S(2)}) copy-start(f32[256]{0:T(256)} %copy-done.34) | copy-start | bytes 3076
  (65 other events, 1731.5 us)
Sparse Core Ops, SparseCore 0:
  35.6 51.8 all-gather.13
  89.2 64.6 all-gather.15
  155.5 29.2 all-gather.17
  216.7 51.2 reduce-scatter.12
  269.4 108.0 all-gather.21
  379.8 50.8 all-gather.19
  432.5 52.5 all-gather.25
  486.7 60.7 all-gather.23
  584.2 50.7 reduce-scatter.16
  640.8 52.5 all-gather.27
  695.7 64.7 reduce-scatter.28
  762.7 63.2 reduce-scatter.24
  828.3 63.2 reduce-scatter.26
  894.2 29.0 reduce-scatter.30
  926.0 34.0 reduce-scatter.22
  962.9 51.1 reduce-scatter.18
  1017.0 52.7 reduce-scatter.14
  1072.0 69.7 reduce-scatter.20
where the time goes:
time: 1160 us; the launch traced here: 1150 us
  waiting for transfers between devices  729 us (63%)
  matrix products  182 us (16%)
  blocking collectives  89 us (8%)
  local copies, waits for them, and re-layouts  84.7 us (7%)
  other arithmetic  49.1 us (4%)
  between operations  15.9 us (1%)
    reduce_scatter x4, waiting for transfers between devices, spread_rows(): lax.psum_scatter(term_fn(jnp.int32(0), row_total * lax.axis_size('tensor'...  149 us
    all_gather x4, waiting for transfers between devices, collect_rows(): return lax.all_gather(row_block, 'tensor', axis=0, tiled=True)  147 us
    all_gather x1, waiting for transfers between devices, mlp_params(): lax.all_gather(gate_up_weight, 'dp', axis=1, tiled=True)  103 us
    reduce_scatter x1, waiting for transfers between devices, shards(): lax.psum_scatter(grad_wqkv.astype(jnp.bfloat16), 'dp', scatter_dimension=...  67.2 us
    all_gather x1, waiting for transfers between devices, attention_params(): lax.all_gather(qkv_weight, 'dp', axis=1, tiled=True)  66.3 us
    reduce_scatter x1, waiting for transfers between devices, shards(): lax.psum_scatter(grad_wup.astype(jnp.bfloat16), 'dp', scatter_dimension=0...  65.6 us
    all_gather x1, waiting for transfers between devices, mlp_params(): lax.all_gather(down_weight, 'dp', axis=1, tiled=True)  62.4 us
    reduce_scatter x1, waiting for transfers between devices, shards(): lax.psum_scatter(grad_wout.astype(jnp.bfloat16), 'dp', scatter_dimension=...  35.4 us
  transfers between devices with their start and end apart: 18, of which 16 were waited for; matrix products, arithmetic and copies ran while one was open for 22% of the time, Pallas kernels for 0%

commit v1 on v0

v1 whole, which is shorter than its diff:
```python
import jax
import jax.numpy as jnp
from jax import lax
from jax.experimental import pallas as pl
from jax.experimental.pallas import tpu as pltpu
from jax.sharding import PartitionSpec as P

HEAD_DIM = 64
ROT = 16
SEQ_LEN = 512
LANES = 128
EPS = 1e-05
F32 = jnp.float32
BF16 = jnp.bfloat16
NT = (((1,), (1,)), ((), ()))
TN = (((0,), (0,)), ((), ()))


def layer_norm(values):
    row_mean = jnp.mean(values, axis=-1, keepdims=True)
    centered = values - row_mean
    inv_sigma = lax.rsqrt(jnp.mean(centered * centered, axis=-1, keepdims=True) + EPS)
    return (centered * inv_sigma, inv_sigma)


def norm_back(grad_hat, normed, inv_sigma):
    return inv_sigma * (
        grad_hat
        - jnp.mean(grad_hat, axis=-1, keepdims=True)
        - normed * jnp.mean(grad_hat * normed, axis=-1, keepdims=True)
    )


def rotary_lanes():
    half = ROT // 2
    frequency = 10000.0 ** (-(2.0 * jnp.arange(half, dtype=F32)) / ROT)
    angles = jnp.arange(SEQ_LEN, dtype=F32)[:, None] * frequency[None, :]
    cosine, sine = jnp.cos(angles), jnp.sin(angles)
    rest = HEAD_DIM - ROT
    zero = jnp.zeros((SEQ_LEN, half), F32)
    tail = jnp.zeros((SEQ_LEN, rest), F32)
    copies = LANES // HEAD_DIM
    keep = jnp.concatenate([cosine, cosine, tail + 1.0] * copies, axis=1)
    low = jnp.concatenate([-sine, zero, tail] * copies, axis=1)
    high = jnp.concatenate([zero, sine, tail] * copies, axis=1)
    return keep, low, high


def bits_of(axis):
    size = lax.axis_size(axis)
    return [1 << b for b in range(size.bit_length() - 1)]


def swap(value, axis, bit):
    return lax.ppermute(value, axis, [(i, i ^ bit) for i in range(lax.axis_size(axis))])


def total_over(value, axis):
    for bit in bits_of(axis):
        value = value + swap(value, axis, bit)
    return value


def row_parts(rows, count):
    tiles = rows // 16
    edges = [16 * (tiles * k // count) for k in range(count)] + [rows]
    return list(zip(edges[:-1], edges[1:]))


def part_plan(rows):
    bits = bits_of("tensor")
    return [
        (lo, hi, bits[k:] + bits[:k]) for k, (lo, hi) in enumerate(row_parts(rows, len(bits)))
    ]


def collect_rows(block):
    rows = block.shape[0]
    pieces = {}
    for lo, hi, order in part_plan(rows):
        held = {0: block[lo:hi]}
        for bit in order:
            held.update({m ^ bit: swap(v, "tensor", bit) for m, v in held.items()})
        for m, v in held.items():
            pieces[(m, lo)] = v
    return jnp.concatenate([pieces[k] for k in sorted(pieces)], axis=0)


def spread_rows(terms, rows):
    done = []
    for lo, hi, order in part_plan(rows):
        held = {m: terms[m * rows + lo : m * rows + hi] for m in range(lax.axis_size("tensor"))}
        for bit in order[::-1]:
            last = bit == order[0]
            nxt = {}
            for m in [m for m in held if not m & bit]:
                total = held[m].astype(F32) + swap(held[m ^ bit], "tensor", bit).astype(F32)
                nxt[m] = total if last else total.astype(BF16)
            held = nxt
        done.append(held[0])
    return jnp.concatenate(done, axis=0)


def ordered(ref, lead, flip, rows):
    return jnp.concatenate(
        [
            ref[lead + (pl.ds(pl.multiple_of((n ^ flip) * rows, rows), rows), slice(None))]
            for n in range(SEQ_LEN // rows)
        ],
        axis=0,
    )


def put_ordered(ref, lead, flip, rows, value):
    for n in range(SEQ_LEN // rows):
        ref[lead + (pl.ds(pl.multiple_of((n ^ flip) * rows, rows), rows), slice(None))] = value[
            n * rows : (n + 1) * rows
        ]


CHUNK = 256
HEADS_STEP = LANES // HEAD_DIM


def lane_roll(value, shift):
    return pltpu.roll(value, shift % LANES, 1)


def masked(scores, start):
    rows = lax.broadcasted_iota(jnp.int32, scores.shape, 0) + start
    cols = lax.broadcasted_iota(jnp.int32, scores.shape, 1)
    return jnp.where(rows >= cols, scores, -jnp.inf)


def attend_kernel(flip_ref, pre_ref, keep_ref, low_ref, high_ref, qkv_ref, ctx_ref, lse_ref, *, rows):
    flip = flip_ref[0]
    half = ROT // 2
    scale = HEAD_DIM ** (-0.5)
    keep, low, high = keep_ref[...], low_ref[...], high_ref[...]
    for c in range(3):
        v = ordered(pre_ref, (c, 0), flip, rows)
        if c < 2:
            v = v * keep + lane_roll(v, -half) * low + lane_roll(v, half) * high
        qkv_ref[c, 0] = v.astype(BF16)
    ctx_parts, lse_parts = [], []
    for start in range(0, SEQ_LEN, CHUNK):
        end = start + CHUNK
        ctxs, lses = [], []
        for h in range(HEADS_STEP):
            cols = slice(h * HEAD_DIM, (h + 1) * HEAD_DIM)
            q = qkv_ref[0, 0, start:end, cols]
            k = qkv_ref[1, 0, :end, cols]
            v = qkv_ref[2, 0, :end, cols]
            s = lax.dot_general(q, k, NT, preferred_element_type=F32) * scale
            s = masked(s, start)
            top = jnp.max(s, axis=-1, keepdims=True)
            e = jnp.exp(s - top)
            total = jnp.sum(e, axis=-1, keepdims=True)
            p = (e * (1.0 / total)).astype(BF16)
            ctxs.append(jnp.dot(p, v, preferred_element_type=F32).astype(BF16))
            lses.append(jnp.broadcast_to(top + jnp.log(total), (CHUNK, HEAD_DIM)))
        ctx_parts.append(jnp.concatenate(ctxs, axis=1))
        lse_parts.append(jnp.concatenate(lses, axis=1))
    put_ordered(ctx_ref, (0,), flip, rows, jnp.concatenate(ctx_parts, axis=0))
    lse_ref[0] = jnp.concatenate(lse_parts, axis=0)


def attend_back_kernel(
    flip_ref, qkv_ref, ctx_ref, gctx_ref, lse_ref, keep_ref, low_ref, high_ref, gpre_ref, bias_ref, *, rows
):
    flip = flip_ref[0]
    half = ROT // 2
    scale = HEAD_DIM ** (-0.5)
    ctx = ordered(ctx_ref, (0,), flip, rows)
    gctx = ordered(gctx_ref, (0,), flip, rows)
    prod = gctx.astype(F32) * ctx.astype(F32)
    starts = list(range(0, SEQ_LEN, CHUNK))
    gq, gk, gv = [], [], []
    for h in range(HEADS_STEP):
        cols = slice(h * HEAD_DIM, (h + 1) * HEAD_DIM)
        dq_parts = []
        dk = [None] * len(starts)
        dv = [None] * len(starts)
        for i, start in enumerate(starts):
            end = start + CHUNK
            q = qkv_ref[0, 0, start:end, cols]
            k = qkv_ref[1, 0, :end, cols]
            v = qkv_ref[2, 0, :end, cols]
            g = gctx[start:end, cols]
            lse = lse_ref[0, start:end, h * HEAD_DIM : h * HEAD_DIM + 1]
            delta = jnp.sum(prod[start:end, cols], axis=-1, keepdims=True)
            s = lax.dot_general(q, k, NT, preferred_element_type=F32) * scale
            p = jnp.exp(masked(s, start) - lse)
            dp = lax.dot_general(g, v, NT, preferred_element_type=F32)
            ds = (p * (dp - delta) * scale).astype(BF16)
            p_low = p.astype(BF16)
            dq_parts.append(jnp.dot(ds, k, preferred_element_type=F32))
            dk_i = lax.dot_general(ds, q, TN, preferred_element_type=F32)
            dv_i = lax.dot_general(p_low, g, TN, preferred_element_type=F32)
            for j in range(i + 1):
                part = slice(j * CHUNK, (j + 1) * CHUNK)
                dk[j] = dk_i[part] if dk[j] is None else dk[j] + dk_i[part]
                dv[j] = dv_i[part] if dv[j] is None else dv[j] + dv_i[part]
        gq.append(jnp.concatenate(dq_parts, axis=0))
        gk.append(jnp.concatenate(dk, axis=0))
        gv.append(jnp.concatenate(dv, axis=0))
    keep, low, high = keep_ref[...], low_ref[...], high_ref[...]
    for c, parts in enumerate((gq, gk, gv)):
        v = jnp.concatenate(parts, axis=1)
        if c < 2:
            v = v * keep - lane_roll(v, -half) * low - lane_roll(v, half) * high
        v = v.astype(BF16)
        put_ordered(gpre_ref, (c, 0), flip, rows, v)
        bias_ref[0, c : c + 1] = jnp.sum(v.astype(F32), axis=0, keepdims=True)


def attend_specs(cols):
    whole = pl.BlockSpec((SEQ_LEN, LANES), lambda s, h, f: (0, 0))
    triple = pl.BlockSpec((3, 1, SEQ_LEN, LANES), lambda s, h, f: (0, s, 0, h))
    single = pl.BlockSpec((1, SEQ_LEN, LANES), lambda s, h, f: (s, 0, h))
    bias = pl.BlockSpec((1, 3, LANES), lambda s, h, f: (s, 0, h))
    return whole, triple, single, bias


def attend(flip, pre, tables, rows):
    import functools

    _, seqs, _, cols = pre.shape
    whole, triple, single, _ = attend_specs(cols)
    return pl.pallas_call(
        functools.partial(attend_kernel, rows=rows),
        out_shape=(
            jax.ShapeDtypeStruct((3, seqs, SEQ_LEN, cols), BF16),
            jax.ShapeDtypeStruct((seqs, SEQ_LEN, cols), BF16),
            jax.ShapeDtypeStruct((seqs, SEQ_LEN, cols), F32),
        ),
        grid_spec=pltpu.PrefetchScalarGridSpec(
            num_scalar_prefetch=1,
            grid=(seqs, cols // LANES),
            in_specs=[triple, whole, whole, whole],
            out_specs=[triple, single, single],
        ),
        name="attend",
    )(flip, pre, *tables)


def attend_back(flip, qkv, ctx, gctx, lse, tables, rows):
    import functools

    _, seqs, _, cols = qkv.shape
    whole, triple, single, bias = attend_specs(cols)
    return pl.pallas_call(
        functools.partial(attend_back_kernel, rows=rows),
        out_shape=(
            jax.ShapeDtypeStruct((3, seqs, SEQ_LEN, cols), BF16),
            jax.ShapeDtypeStruct((seqs, 3, cols), F32),
        ),
        grid_spec=pltpu.PrefetchScalarGridSpec(
            num_scalar_prefetch=1,
            grid=(seqs, cols // LANES),
            in_specs=[triple, single, single, single, whole, whole, whole],
            out_specs=[triple, bias],
        ),
        name="attend_back",
    )(flip, qkv, ctx, gctx, lse, *tables)


def shards(
    layer_input,
    norm1_gain,
    norm1_bias,
    qkv_weight,
    qkv_bias,
    out_weight,
    norm2_gain,
    norm2_bias,
    gate_up_weight,
    down_weight,
    out_cotangent,
):
    rows, width = layer_input.shape
    part = norm1_gain.shape[0]
    dp_count = lax.axis_size("dp")
    dp_here = lax.axis_index("dp")
    blocks = max(SEQ_LEN // rows, 1)
    flip = (lax.axis_index("tensor") & (blocks - 1)).astype(jnp.int32)[None]
    group_rows = rows * lax.axis_size("tensor")
    seqs = group_rows // SEQ_LEN
    head_cols = qkv_weight.shape[2]
    tables = rotary_lanes()

    packed = jnp.concatenate(
        [norm1_gain, norm1_bias, norm2_gain, norm2_bias, qkv_bias.reshape(-1)]
    )
    packed = lax.all_gather(packed, "dp", axis=0, tiled=False)
    gain_one, bias_one, gain_two, bias_two = (
        packed[:, k * part : (k + 1) * part].reshape(width).astype(F32) for k in range(4)
    )
    bias_local = (
        packed[:, 4 * part :].reshape(dp_count, 3, -1).transpose(1, 0, 2).reshape(3, head_cols)
    ).astype(F32)

    qkv_local = lax.all_gather(qkv_weight, "dp", axis=1, tiled=True)
    out_local = lax.all_gather(out_weight, "dp", axis=1, tiled=True)
    gate_up_local = lax.all_gather(gate_up_weight, "dp", axis=1, tiled=True)
    down_local = lax.all_gather(down_weight, "dp", axis=1, tiled=True)

    x_float = layer_input.astype(F32)
    hat_one, inv_one = layer_norm(x_float)
    rows_one = collect_rows((hat_one * gain_one + bias_one).astype(BF16))
    pre = (
        jnp.einsum("rd,cdk->crk", rows_one, qkv_local, preferred_element_type=F32)
        + bias_local[:, None, :]
    )
    qkv_heads, context, lse = attend(
        flip, pre.reshape(3, seqs, SEQ_LEN, head_cols), tables, min(rows, SEQ_LEN)
    )
    context_rows = context.reshape(group_rows, head_cols)
    attn_terms = jnp.dot(context_rows, out_local, preferred_element_type=F32).astype(BF16)
    residual = x_float + spread_rows(attn_terms, rows)

    hat_two, inv_two = layer_norm(residual)
    rows_two = collect_rows((hat_two * gain_two + bias_two).astype(BF16))
    cot_rows = collect_rows(out_cotangent)
    gate_proj = jnp.dot(rows_two, gate_up_local[0], preferred_element_type=F32)
    up_proj = jnp.dot(rows_two, gate_up_local[1], preferred_element_type=F32)
    sigmoid_gate = jax.nn.sigmoid(gate_proj)
    silu_gate = gate_proj * sigmoid_gate
    activation = (silu_gate * up_proj).astype(BF16)
    mlp_terms = jnp.dot(activation, down_local, preferred_element_type=F32).astype(BF16)
    layer_output = (residual + spread_rows(mlp_terms, rows)).astype(BF16)

    grad_act = lax.dot_general(cot_rows, down_local, NT, preferred_element_type=F32)
    grad_gate = (
        grad_act * up_proj * sigmoid_gate * (1.0 + gate_proj * (1.0 - sigmoid_gate))
    ).astype(BF16)
    grad_up = (grad_act * silu_gate).astype(BF16)
    back_terms = (
        lax.dot_general(grad_gate, gate_up_local[0], NT, preferred_element_type=F32)
        + lax.dot_general(grad_up, gate_up_local[1], NT, preferred_element_type=F32)
    ).astype(BF16)
    grad_down = lax.dot_general(activation, cot_rows, TN, preferred_element_type=F32)
    grad_wgate = lax.dot_general(rows_two, grad_gate, TN, preferred_element_type=F32)
    grad_wup = lax.dot_general(rows_two, grad_up, TN, preferred_element_type=F32)
    share_down = lax.psum_scatter(
        grad_down.astype(BF16), "dp", scatter_dimension=1, tiled=True
    ).astype(F32)
    share_gate = lax.psum_scatter(
        grad_wgate.astype(BF16), "dp", scatter_dimension=0, tiled=True
    ).astype(F32)
    share_up = lax.psum_scatter(
        grad_wup.astype(BF16), "dp", scatter_dimension=0, tiled=True
    ).astype(F32)
    grad_normed_two = spread_rows(back_terms, rows)
    grad_resid = out_cotangent.astype(F32) + norm_back(
        grad_normed_two * gain_two, hat_two, inv_two
    )

    resid_rows = collect_rows(grad_resid.astype(BF16))
    grad_context = lax.dot_general(
        resid_rows, out_local, NT, preferred_element_type=F32
    ).astype(BF16)
    grad_pre, bias_sums = attend_back(
        flip,
        qkv_heads,
        context,
        grad_context.reshape(seqs, SEQ_LEN, head_cols),
        lse,
        tables,
        min(rows, SEQ_LEN),
    )
    grad_pre = grad_pre.reshape(3, group_rows, head_cols)
    qkv_terms = jnp.einsum(
        "crk,cdk->rd", grad_pre, qkv_local, preferred_element_type=F32
    ).astype(BF16)
    grad_wout = lax.dot_general(context_rows, resid_rows, TN, preferred_element_type=F32)
    grad_wqkv = jnp.einsum("rd,crk->cdk", rows_one, grad_pre, preferred_element_type=F32)
    share_out = lax.psum_scatter(
        grad_wout.astype(BF16), "dp", scatter_dimension=1, tiled=True
    ).astype(F32)
    share_qkv = lax.psum_scatter(
        grad_wqkv.astype(BF16), "dp", scatter_dimension=1, tiled=True
    ).astype(F32)
    grad_normed_one = spread_rows(qkv_terms, rows)
    grad_input = grad_resid + norm_back(grad_normed_one * gain_one, hat_one, inv_one)

    bias_total = total_over(jnp.sum(bias_sums, axis=0), "dp")
    bias_part = qkv_bias.shape[1]
    share_bias = lax.dynamic_slice_in_dim(bias_total, dp_here * bias_part, bias_part, axis=1)
    norm_sums = jnp.stack(
        [
            jnp.sum(grad_normed_one * hat_one, axis=0),
            jnp.sum(grad_normed_one, axis=0),
            jnp.sum(grad_normed_two * hat_two, axis=0),
            jnp.sum(grad_normed_two, axis=0),
        ]
    )
    norm_total = total_over(total_over(norm_sums, "tensor"), "dp")
    share_norm = lax.dynamic_slice_in_dim(norm_total, dp_here * part, part, axis=1)
    return (
        layer_output,
        grad_input,
        share_norm[0],
        share_norm[1],
        share_qkv,
        share_bias,
        share_out,
        share_norm[2],
        share_norm[3],
        jnp.stack([share_gate, share_up]),
        share_down,
    )


def solution(mesh):
    placed = (
        P(("dp", "tensor"), None),
        P("dp"),
        P("dp"),
        P(None, "dp", "tensor"),
        P(None, ("tensor", "dp")),
        P("tensor", "dp"),
        P("dp"),
        P("dp"),
        P(None, "dp", "tensor"),
        P("tensor", "dp"),
        P(("dp", "tensor"), None),
    )
    return jax.shard_map(
        shards,
        mesh=mesh,
        in_specs=placed,
        out_specs=(
            P(("dp", "tensor"), None),
            P(("dp", "tensor"), None),
            P("dp"),
            P("dp"),
            P(None, "dp", "tensor"),
            P(None, ("tensor", "dp")),
            P("tensor", "dp"),
            P("dp"),
            P("dp"),
            P(None, "dp", "tensor"),
            P("tensor", "dp"),
        ),
        check_vma=False,
    )
```

time: 1160 us -> 763 us (0.66)
  waiting for transfers between devices: 729 us -> 394 us
  starting transfers between devices: 0.9 us -> 60.9 us
  blocking collectives: 89 us -> 32.6 us
  local copies, waits for them, and re-layouts: 84.7 us -> 39.1 us
  matrix products: 182 us -> 142 us
  Pallas kernels: 0 us -> 38.9 us
  other arithmetic: 49.1 us -> 29.3 us
    all_gather x8 -> x4, waiting for transfers between devices: 378 us -> 28 us  [the longest x1 28 us: shards(): down_local = lax.all_gather(down_weight, 'dp', axis=1, tiled=True)]
    ppermute x0 -> x56, waiting for transfers between devices: none -> 218 us  [swap(): lax.ppermute(value, axis, [(i, i ^ bit) for i in range(lax.axis_size(axis...]
    reduce_scatter x9 -> x5, waiting for transfers between devices: 319 us -> 146 us  [the longest x1 67.4 us: shards(): lax.psum_scatter(grad_wqkv.astype(BF16), 'dp', scatter_dimension=1, tiled...]
    ppermute x0 -> x56, starting transfers between devices: none -> 59.9 us  [swap(): lax.ppermute(value, axis, [(i, i ^ bit) for i in range(lax.axis_size(axis...]
    all_gather x5 -> x0, blocking collectives: 51.1 us -> none  [the longest x1 13.5 us: attention_params(): lax.all_gather(norm1_gain, 'dp', axis=0, tiled=True)]
    dot_general x29 -> x15, matrix products: 182 us -> 142 us  [the longest x1 16.2 us: shards(): lax.dot_general(cot_rows, down_local, NT, preferred_element_type=F32)]
    pallas_call x0 -> x2, Pallas kernels: none -> 38.9 us  [the longest x1 19.7 us: attend(): pl.pallas_call(functools.partial(attend_kernel, rows=rows), out_shape=(ja...]
    unnamed x19 -> x9, waiting for transfers between devices: 32 us -> 2.16 us
  transfers between devices with their start and end apart: 18 -> 65, of which waited for: 16 -> 42; matrix products, arithmetic and copies ran while one was open for 22% -> 22% of each run, Pallas kernels for 0% -> 5%
where the time goes in v1:
time: 763 us; the launch traced here: 753 us
  waiting for transfers between devices  394 us (52%)
  matrix products  142 us (19%)
  starting transfers between devices  60.9 us (8%)
  local copies, waits for them, and re-layouts  39.1 us (5%)
  Pallas kernels  38.9 us (5%)
  blocking collectives  32.6 us (4%)
  other arithmetic  29.3 us (4%)
  between operations  15.7 us (2%)
    ppermute x56, waiting for transfers between devices, swap(): lax.ppermute(value, axis, [(i, i ^ bit) for i in range(lax.axis_size(axis...  218 us
    reduce_scatter x1, waiting for transfers between devices, shards(): lax.psum_scatter(grad_wqkv.astype(BF16), 'dp', scatter_dimension=1, tiled...  67.4 us
    reduce_scatter x1, waiting for transfers between devices, shards(): lax.psum_scatter(grad_wup.astype(BF16), 'dp', scatter_dimension=0, tiled=...  65.6 us
    ppermute x56, starting transfers between devices, swap(): lax.ppermute(value, axis, [(i, i ^ bit) for i in range(lax.axis_size(axis...  59.9 us
    unnamed x1, blocking collectives  32.6 us
    unnamed x81, local copies, waits for them, and re-layouts  28.4 us
    all_gather x1, waiting for transfers between devices, shards(): down_local = lax.all_gather(down_weight, 'dp', axis=1, tiled=True)  28 us
    pallas_call x1, Pallas kernels, attend(): pl.pallas_call(functools.partial(attend_kernel, rows=rows), out_shape=(ja...  19.7 us
  transfers between devices with their start and end apart: 65, of which 42 were waited for; matrix products, arithmetic and copies ran while one was open for 22% of the time, Pallas kernels for 5%

profile of v1, /device:TPU:0, one launch (start us, length us, event | category | flops | bytes accessed | tf_op | source)
XLA Modules:
  0.0 752.6 jit_solution(16071570499552407710)
XLA Ops:
  15.8 32.6 %all-reduce = bf16[9728]{0:T(1024)(128)(2,1)S(1)} all-reduce(bf16[9728]{0:T(1024)(128)(2,1)S(1)} %dynamic-update-slice), channel_id=2, replica_groups=mesh['dp'=8,'tensor'=4] {'dp'}, use_global_device_ids=true, to_apply=%add | all-reduce | flops 9728 | bytes 38912
  69.4 11.2 %collective-permute-done.3 = bf16[128,2048]{1,0:T(8,128)(2,1)S(1)} collective-permute-done((bf16[128,2048]{1,0:T(8,128)(2,1)}, bf16[128,2048]{1,0:T(8,128)(2,1)S(1)}, u32[]{:S(2)}, u32[]{:S(2)}) %collective-permute-start.3) | collective-permute-done | bytes 524320 | tf_op jit(solution)/shard_map/ppermute | solution.py:55
  90.6 11.9 %broadcast_add_fusion = f32[1024,3,512]{2,0,1:T(8,128)} fusion(f32[3,512]{1,0:T(4,128)S(1)} %reshape.158, bf16[3,2048,512]{2,1,0:T(8,128)(2,1)} %all-gather.6.cloned.1.call-done, bf16[1024,2048]{1,0:T(8,128)(2,1)} %constant_dynamic-update-slice_fusion), kind=kOutput, calls=%fused_computation.22 | convolution fusion | flops 6444023808 | bytes 16783360 | tf_op jit(solution)/shard_map/rd,cdk->crk/dot_general | solution.py:312
  102.4 19.7 %attend.1 = (bf16[3,2,512,512]{3,2,1,0:T(8,128)(2,1)}, bf16[2,512,512]{2,1,0:T(8,128)(2,1)}, f32[2,512,512]{2,1,0:T(8,128)}) custom-call(s32[1]{0:T(128)} %bitcast.flip_ref, f32[3,2,512,512]{3,2,1,0:T(8,128)} %bitcast.76, f32[512,128]{1,0:T(8,128)} %concatenate.42.keep_ref, f32[512,128]{1,0:T(8,128)} %concatenate.43.low_ref, f32[512,128]{1,0:T(8,128)} %concatenate.44.high_ref), custom_call_target="tpu_custom_call" | custom-call | tf_op jit(solution)/shard_map/attend/pallas_call | solution.py:230
  130.3 12.1 %collective-permute-done.7 = bf16[128,2048]{1,0:T(8,128)(2,1)S(1)} collective-permute-done((bf16[128,2048]{1,0:T(8,128)(2,1)S(1)}, bf16[128,2048]{1,0:T(8,128)(2,1)S(1)}, u32[]{:S(2)}, u32[]{:S(2)}) %collective-permute-start.7) | collective-permute-done | bytes 524320 | tf_op jit(solution)/shard_map/ppermute | solution.py:55
  202.4 11.2 %collective-permute-done.12 = bf16[128,2048]{1,0:T(8,128)(2,1)S(1)} collective-permute-done((bf16[128,2048]{1,0:T(8,128)(2,1)S(1)}, bf16[128,2048]{1,0:T(8,128)(2,1)S(1)}, u32[]{:S(2)}, u32[]{:S(2)}) %collective-permute-start.12) | collective-permute-done | bytes 524320 | tf_op jit(solution)/shard_map/ppermute | solution.py:55
  227.6 12.0 %fusion.2 = f32[1024,1408]{1,0:T(8,128)} fusion(bf16[1024,2048]{1,0:T(8,128)(2,1)} %constant_dynamic-update-slice_fusion.7, bf16[2,2048,1408]{2,1,0:T(8,128)(2,1)} %all-gather.10.cloned.1.call-done), kind=kOutput, calls=%fused_computation.14 | convolution fusion | flops 5905580032 | bytes 15728640 | tf_op jit(solution)/shard_map/dot_general | solution.py:325
  239.7 10.0 %fusion.4 = f32[1024,1408]{1,0:T(8,128)} fusion(bf16[1024,2048]{1,0:T(8,128)(2,1)} %constant_dynamic-update-slice_fusion.7, bf16[2,2048,1408]{2,1,0:T(8,128)(2,1)S(1)} %copy-done.15), kind=kOutput, calls=%fused_computation.16 | convolution fusion | flops 5905580032 | bytes 15728640 | tf_op jit(solution)/shard_map/dot_general | solution.py:326
  249.7 28.0 %all-gather.12.cloned.1.call-done = bf16[1408,2048]{1,0:T(8,128)(2,1)} async-done(((bf16[1408,256]{1,0:T(8,128)(2,1)}), bf16[1408,2048]{1,0:T(8,128)(2,1)}) %all-gather.12.cloned.1.call-update) | async-done | bytes 5767184 | tf_op jit(solution)/shard_map/all_gather | solution.py:306
  277.7 16.2 %multiply_convert_fusion = (bf16[1024,1408]{1,0:T(8,128)(2,1)}, bf16[1024,1408]{1,0:T(8,128)(2,1)}, bf16[1024,1408]{1,0:T(8,128)(2,1)S(1)}) fusion(f32[1024,1408]{1,0:T(8,128)} %fusion.2, f32[1024,1408]{1,0:T(8,128)} %fusion.4, bf16[1024,2048]{1,0:T(8,128)(2,1)} %copy-done.7, bf16[1408,2048]{1,0:T(8,128)(2,1)} %all-gather.12.cloned.1.call-done), kind=kOutput, calls=%fused_computation.8 | convolution fusion | flops 5927206912 | bytes 30146560 | tf_op jit(solution)/shard_map/dot_general | solution.py:333
  311.3 9.8 %add_convert_fusion = bf16[1024,2048]{1,0:T(8,128)(2,1)S(1)} fusion(f32[1024,2048]{1,0:T(8,128)S(1)} %fusion.1, bf16[1024,1408]{1,0:T(8,128)(2,1)} %get-tuple-element.77, bf16[2,2048,1408]{2,1,0:T(8,128)(2,1)} %all-gather.10.cloned.1.call-done), kind=kOutput, calls=%fused_computation.1 | convolution fusion | flops 5909774336 | bytes 21233664 | tf_op jit(solution)/shard_map/dot_general | solution.py:340
  337.9 9.6 %collective-permute-done.18 = bf16[128,2048]{1,0:T(8,128)(2,1)S(1)} collective-permute-done((bf16[128,2048]{1,0:T(8,128)(2,1)S(1)}, bf16[128,2048]{1,0:T(8,128)(2,1)S(1)}, u32[]{:S(2)}, u32[]{:S(2)}) %collective-permute-start.18) | collective-permute-done | bytes 524320 | tf_op jit(solution)/shard_map/ppermute | solution.py:55
  360.2 11.8 %collective-permute-done.34 = bf16[128,2048]{1,0:T(8,128)(2,1)S(1)} collective-permute-done((bf16[128,2048]{1,0:T(8,128)(2,1)S(1)}, bf16[128,2048]{1,0:T(8,128)(2,1)S(1)}, u32[]{:S(2)}, u32[]{:S(2)}) %collective-permute-start.34) | collective-permute-done | bytes 524320 | tf_op jit(solution)/shard_map/ppermute | solution.py:55
  372.0 11.2 %collective-permute-done.32 = bf16[128,2048]{1,0:T(8,128)(2,1)S(1)} collective-permute-done((bf16[128,2048]{1,0:T(8,128)(2,1)S(1)}, bf16[128,2048]{1,0:T(8,128)(2,1)S(1)}, u32[]{:S(2)}, u32[]{:S(2)}) %collective-permute-start.32) | collective-permute-done | bytes 524320 | tf_op jit(solution)/shard_map/ppermute | solution.py:55
  403.8 10.7 %collective-permute-done.36 = bf16[128,2048]{1,0:T(8,128)(2,1)S(1)} collective-permute-done((bf16[128,2048]{1,0:T(8,128)(2,1)S(1)}, bf16[128,2048]{1,0:T(8,128)(2,1)S(1)}, u32[]{:S(2)}, u32[]{:S(2)}) %collective-permute-start.36) | collective-permute-done | bytes 524320 | tf_op jit(solution)/shard_map/ppermute | solution.py:55
  440.0 10.9 %convolution_convert_fusion = bf16[1408,2048]{1,0:T(8,128)(2,1)} fusion(bf16[1024,1408]{1,0:T(8,128)(2,1)S(1)} %copy-done.20, bf16[1024,2048]{1,0:T(8,128)(2,1)} %copy-done.7), kind=kOutput, calls=%fused_computation.2 | convolution fusion | flops 5908463616 | bytes 12845056 | tf_op jit(solution)/shard_map/dot_general | solution.py:342
  452.8 10.9 %convolution_convert_fusion.2 = bf16[2048,1408]{1,0:T(8,128)(2,1)} fusion(bf16[1024,2048]{1,0:T(8,128)(2,1)} %constant_dynamic-update-slice_fusion.7, bf16[1024,1408]{1,0:T(8,128)(2,1)S(1)} %copy-done.22), kind=kOutput, calls=%fused_computation.4 | convolution fusion | flops 5908463616 | bytes 12845056 | tf_op jit(solution)/shard_map/dot_general | solution.py:343
  465.5 10.9 %convolution_convert_fusion.1 = bf16[2048,1408]{1,0:T(8,128)(2,1)} fusion(bf16[1024,2048]{1,0:T(8,128)(2,1)} %constant_dynamic-update-slice_fusion.7, bf16[1024,1408]{1,0:T(8,128)(2,1)S(1)} %copy-done.23), kind=kOutput, calls=%fused_computation.3 | convolution fusion | flops 5908463616 | bytes 12845056 | tf_op jit(solution)/shard_map/dot_general | solution.py:344
  483.5 19.2 %attend_back.1 = (bf16[3,2,512,512]{3,2,1,0:T(8,128)(2,1)}, f32[2,3,512]{2,1,0:T(4,128)}) custom-call(s32[1]{0:T(128)} %bitcast.flip_ref, bf16[3,2,512,512]{3,2,1,0:T(8,128)(2,1)} %get-tuple-element.17.qkv_ref, bf16[2,512,512]{2,1,0:T(8,128)(2,1)} %get-tuple-element.16.ctx_ref, bf16[2,512,512]{2,1,0:T(8,128)(2,1)} %bitcast.79, ...), custom_call_target="tpu_custom_call" | custom-call | tf_op jit(solution)/shard_map/attend_back/pallas_call | solution.py:252
  502.7 11.4 %convert_bitcast_fusion = bf16[3,2048,512]{1,2,0:T(8,128)(2,1)} fusion(bf16[3,1024,512]{2,1,0:T(8,128)(2,1)} %bitcast.107, bf16[1024,2048]{1,0:T(8,128)(2,1)} %constant_dynamic-update-slice_fusion), kind=kOutput, calls=%fused_computation.5 | convolution fusion | flops 6445596672 | bytes 13631488 | tf_op jit(solution)/shard_map/rd,crk->cdk/dot_general | solution.py:377
  528.1 12.1 %collective-permute-done.43 = bf16[128,2048]{1,0:T(8,128)(2,1)S(1)} collective-permute-done((bf16[128,2048]{1,0:T(8,128)(2,1)S(1)}, bf16[128,2048]{1,0:T(8,128)(2,1)S(1)}, u32[]{:S(2)}, u32[]{:S(2)}) %collective-permute-start.43) | collective-permute-done | bytes 524320 | tf_op jit(solution)/shard_map/ppermute | solution.py:55
  593.9 13.1 %reduce-scatter.10.cloned.1.call-done = bf16[256,1408]{1,0:T(8,128)(2,1)} async-done(((bf16[2048,1408]{1,0:T(8,128)(2,1)}), bf16[256,1408]{1,0:T(8,128)(2,1)}) %reduce-scatter.10.cloned.1.call-update) | async-done | bytes 720912 | tf_op jit(solution)/shard_map/reduce_scatter | solution.py:348
  607.0 65.6 %reduce-scatter.12.cloned.1.call-done = bf16[256,1408]{1,0:T(8,128)(2,1)} async-done(((bf16[2048,1408]{1,0:T(8,128)(2,1)}), bf16[256,1408]{1,0:T(8,128)(2,1)}) %reduce-scatter.12.cloned.1.call-update) | async-done | bytes 720912 | tf_op jit(solution)/shard_map/reduce_scatter | solution.py:351
  675.6 67.4 %reduce-scatter.6.cloned.1.call-done = bf16[3,256,512]{1,2,0:T(8,128)(2,1)} async-done(((bf16[3,2048,512]{1,2,0:T(8,128)(2,1)}), bf16[3,256,512]{1,2,0:T(8,128)(2,1)}) %reduce-scatter.6.cloned.1.call-update) | async-done | bytes 786448 | tf_op jit(solution)/shard_map/reduce_scatter | solution.py:381
  (288 shorter events, 297.4 us)
Async XLA Ops:
  7.2 83.4 %all-gather.6.cloned.1.call-start = ((), (), s32[]{:S(2)}) async-start(), calls=%async_computation.5 | async-start | bytes 7077888 | tf_op jit(solution)/shard_map/all_gather | solution.py:303
  7.9 114.2 %all-gather.8.cloned.1.call-start = ((), (), s32[]{:S(2)}) async-start(), calls=%async_computation.6 | async-start | bytes 2359296 | tf_op jit(solution)/shard_map/all_gather | solution.py:304
  8.7 219.0 %all-gather.10.cloned.1.call-start = ((), (), s32[]{:S(2)}) async-start(), calls=%async_computation.7 | async-start | bytes 12976128 | tf_op jit(solution)/shard_map/all_gather | solution.py:305
  9.4 268.3 %all-gather.12.cloned.1.call-start = ((), (), s32[]{:S(2)}) async-start(), calls=%async_computation.8 | async-start | bytes 6488064 | tf_op jit(solution)/shard_map/all_gather | solution.py:306
  54.3 29.7 %collective-permute-start.2 = (bf16[128,2048]{1,0:T(8,128)(2,1)}, bf16[128,2048]{1,0:T(8,128)(2,1)}, u32[]{:S(2)}, u32[]{:S(2)}) collective-permute-start(bf16[128,2048]{1,0:T(8,128)(2,1)} %get-tuple-element.110), channel_id=1, source_target_pairs={{0,2},{1,3},{2,0},{3,1},{4,6},{5,7},{6,4},{7,5},{8,10},{9,11},{10,... | collective-permute-start | bytes 1572872 | tf_op jit(solution)/shard_map/ppermute | solution.py:55
  55.9 26.2 %collective-permute-start.1 = (bf16[128,2048]{1,0:T(8,128)(2,1)}, bf16[128,2048]{1,0:T(8,128)(2,1)}, u32[]{:S(2)}, u32[]{:S(2)}) collective-permute-start(bf16[128,2048]{1,0:T(8,128)(2,1)} %get-tuple-element.109), channel_id=1, source_target_pairs={{0,1},{1,0},{2,3},{3,2},{4,5},{5,4},{6,7},{7,6},{8,9},{9,8},{10,11... | collective-permute-start | bytes 1572872 | tf_op jit(solution)/shard_map/ppermute | solution.py:55
  144.3 24.4 %collective-permute-start.24 = (bf16[128,2048]{1,0:T(8,128)(2,1)}, bf16[128,2048]{1,0:T(8,128)(2,1)}, u32[]{:S(2)}, u32[]{:S(2)}) collective-permute-start(bf16[128,2048]{1,0:T(8,128)(2,1)} %get-tuple-element.106), channel_id=1, source_target_pairs={{0,1},{1,0},{2,3},{3,2},{4,5},{5,4},{6,7},{7,6},{8,9},{9,8},{10,11... | collective-permute-start | bytes 1572872 | tf_op jit(solution)/shard_map/ppermute | solution.py:55
  145.7 36.3 %collective-permute-start.26 = (bf16[128,2048]{1,0:T(8,128)(2,1)}, bf16[128,2048]{1,0:T(8,128)(2,1)S(1)}, u32[]{:S(2)}, u32[]{:S(2)}) collective-permute-start(bf16[128,2048]{1,0:T(8,128)(2,1)} %get-tuple-element.106), channel_id=1, source_target_pairs={{0,2},{1,3},{2,0},{3,1},{4,6},{5,7},{6,4},{7,5},{8,10},{9,11},{10,... | collective-permute-start | bytes 1572872 | tf_op jit(solution)/shard_map/ppermute | solution.py:55
  147.3 442.5 %reduce-scatter.8.cloned.1.call-start = ((), (), s32[]{:S(2)}) async-start(), calls=%async_computation.10 | async-start | bytes 2359296 | tf_op jit(solution)/shard_map/reduce_scatter | solution.py:378
  147.8 32.0 %collective-permute-start.25 = (bf16[128,2048]{1,0:T(8,128)(2,1)}, bf16[128,2048]{1,0:T(8,128)(2,1)S(1)}, u32[]{:S(2)}, u32[]{:S(2)}) collective-permute-start(bf16[128,2048]{1,0:T(8,128)(2,1)} %get-tuple-element.105), channel_id=1, source_target_pairs={{0,1},{1,0},{2,3},{3,2},{4,5},{5,4},{6,7},{7,6},{8,9},{9,8},{10,11... | collective-permute-start | bytes 1572872 | tf_op jit(solution)/shard_map/ppermute | solution.py:55
  153.7 27.7 %collective-permute-start.27 = (bf16[128,2048]{1,0:T(8,128)(2,1)}, bf16[128,2048]{1,0:T(8,128)(2,1)S(1)}, u32[]{:S(2)}, u32[]{:S(2)}) collective-permute-start(bf16[128,2048]{1,0:T(8,128)(2,1)} %get-tuple-element.105), channel_id=1, source_target_pairs={{0,2},{1,3},{2,0},{3,1},{4,6},{5,7},{6,4},{7,5},{8,10},{9,11},{10,... | collective-permute-start | bytes 1572872 | tf_op jit(solution)/shard_map/ppermute | solution.py:55
  157.5 33.6 %collective-permute-start.9 = (bf16[128,2048]{1,0:T(8,128)(2,1)}, bf16[128,2048]{1,0:T(8,128)(2,1)S(1)}, u32[]{:S(2)}, u32[]{:S(2)}) collective-permute-start(bf16[128,2048]{1,0:T(8,128)(2,1)} %get-tuple-element.100), channel_id=1, source_target_pairs={{0,1},{1,0},{2,3},{3,2},{4,5},{5,4},{6,7},{7,6},{8,9},{9,8},{10,11... | collective-permute-start | bytes 1572872 | tf_op jit(solution)/shard_map/ppermute | solution.py:55
  322.9 24.5 %collective-permute-start.18 = (bf16[128,2048]{1,0:T(8,128)(2,1)S(1)}, bf16[128,2048]{1,0:T(8,128)(2,1)S(1)}, u32[]{:S(2)}, u32[]{:S(2)}) collective-permute-start(bf16[128,2048]{1,0:T(8,128)(2,1)S(1)} %get-tuple-element.92), channel_id=1, source_target_pairs={{0,2},{1,3},{2,0},{3,1},{4,6},{5,7},{6,4},{7,5},{8,10},{9,11},{10,... | collective-permute-start | bytes 1572872 | tf_op jit(solution)/shard_map/ppermute | solution.py:55
  323.5 25.5 %collective-permute-start.22 = (bf16[128,2048]{1,0:T(8,128)(2,1)S(1)}, bf16[128,2048]{1,0:T(8,128)(2,1)S(1)}, u32[]{:S(2)}, u32[]{:S(2)}) collective-permute-start(bf16[128,2048]{1,0:T(8,128)(2,1)S(1)} %get-tuple-element.93), channel_id=1, source_target_pairs={{0,1},{1,0},{2,3},{3,2},{4,5},{5,4},{6,7},{7,6},{8,9},{9,8},{10,11... | collective-permute-start | bytes 1572872 | tf_op jit(solution)/shard_map/ppermute | solution.py:55
  325.1 24.4 %collective-permute-start.20 = (bf16[128,2048]{1,0:T(8,128)(2,1)S(1)}, bf16[128,2048]{1,0:T(8,128)(2,1)S(1)}, u32[]{:S(2)}, u32[]{:S(2)}) collective-permute-start(bf16[128,2048]{1,0:T(8,128)(2,1)S(1)} %add_convert_fusion.12), channel_id=1, source_target_pairs={{0,1},{1,0},{2,3},{3,2},{4,5},{5,4},{6,7},{7,6},{8,9},{9,8},{10,11... | collective-permute-start | bytes 1572872 | tf_op jit(solution)/shard_map/ppermute | solution.py:55
  325.7 59.6 %collective-permute-start.21 = (bf16[128,2048]{1,0:T(8,128)(2,1)S(1)}, bf16[128,2048]{1,0:T(8,128)(2,1)S(1)}, u32[]{:S(2)}, u32[]{:S(2)}) collective-permute-start(bf16[128,2048]{1,0:T(8,128)(2,1)S(1)} %get-tuple-element.94), channel_id=1, source_target_pairs={{0,1},{1,0},{2,3},{3,2},{4,5},{5,4},{6,7},{7,6},{8,9},{9,8},{10,11... | collective-permute-start | bytes 1572872 | tf_op jit(solution)/shard_map/ppermute | solution.py:55
  347.5 24.5 %collective-permute-start.34 = (bf16[128,2048]{1,0:T(8,128)(2,1)S(1)}, bf16[128,2048]{1,0:T(8,128)(2,1)S(1)}, u32[]{:S(2)}, u32[]{:S(2)}) collective-permute-start(bf16[128,2048]{1,0:T(8,128)(2,1)S(1)} %get-tuple-element.87), channel_id=1, source_target_pairs={{0,1},{1,0},{2,3},{3,2},{4,5},{5,4},{6,7},{7,6},{8,9},{9,8},{10,11... | collective-permute-start | bytes 1572872 | tf_op jit(solution)/shard_map/ppermute | solution.py:55
  348.9 34.3 %collective-permute-start.32 = (bf16[128,2048]{1,0:T(8,128)(2,1)S(1)}, bf16[128,2048]{1,0:T(8,128)(2,1)S(1)}, u32[]{:S(2)}, u32[]{:S(2)}) collective-permute-start(bf16[128,2048]{1,0:T(8,128)(2,1)S(1)} %add_convert_fusion.8), channel_id=1, source_target_pairs={{0,1},{1,0},{2,3},{3,2},{4,5},{5,4},{6,7},{7,6},{8,9},{9,8},{10,11... | collective-permute-start | bytes 1572872 | tf_op jit(solution)/shard_map/ppermute | solution.py:55
  350.0 35.3 %collective-permute-start.23 = (bf16[128,2048]{1,0:T(8,128)(2,1)S(1)}, bf16[128,2048]{1,0:T(8,128)(2,1)S(1)}, u32[]{:S(2)}, u32[]{:S(2)}) collective-permute-start(bf16[128,2048]{1,0:T(8,128)(2,1)S(1)} %get-tuple-element.91), channel_id=1, source_target_pairs={{0,2},{1,3},{2,0},{3,1},{4,6},{5,7},{6,4},{7,5},{8,10},{9,11},{10,... | collective-permute-start | bytes 1572872 | tf_op jit(solution)/shard_map/ppermute | solution.py:55
  358.7 34.5 %collective-permute-start.33 = (bf16[128,2048]{1,0:T(8,128)(2,1)S(1)}, bf16[128,2048]{1,0:T(8,128)(2,1)S(1)}, u32[]{:S(2)}, u32[]{:S(2)}) collective-permute-start(bf16[128,2048]{1,0:T(8,128)(2,1)S(1)} %get-tuple-element.88), channel_id=1, source_target_pairs={{0,1},{1,0},{2,3},{3,2},{4,5},{5,4},{6,7},{7,6},{8,9},{9,8},{10,11... | collective-permute-start | bytes 1572872 | tf_op jit(solution)/shard_map/ppermute | solution.py:55
  440.0 151.6 %reduce-scatter.14.cloned.1.call-start = ((), (), s32[]{:S(2)}) async-start(), calls=%async_computation.13 | async-start | bytes 6488064 | tf_op jit(solution)/shard_map/reduce_scatter | solution.py:345
  451.0 156.0 %reduce-scatter.10.cloned.1.call-start = ((), (), s32[]{:S(2)}) async-start(), calls=%async_computation.11 | async-start | bytes 6488064 | tf_op jit(solution)/shard_map/reduce_scatter | solution.py:348
  463.7 208.8 %reduce-scatter.12.cloned.1.call-start = ((), (), s32[]{:S(2)}) async-start(), calls=%async_computation.12 | async-start | bytes 6488064 | tf_op jit(solution)/shard_map/reduce_scatter | solution.py:351
  476.4 266.6 %reduce-scatter.6.cloned.1.call-start = ((), (), s32[]{:S(2)}) async-start(), calls=%async_computation.9 | async-start | bytes 7077888 | tf_op jit(solution)/shard_map/reduce_scatter | solution.py:381
  (65 other events, 1006.4 us)
Sparse Core Ops, SparseCore 0:
  9.6 67.8 all-gather.5
  79.1 29.2 all-gather.7
  110.0 107.0 all-gather.9
  218.6 59.0 all-gather.11
  440.1 33.9 reduce-scatter.7
  476.2 63.3 reduce-scatter.13
  541.9 64.9 reduce-scatter.9
  609.3 63.2 reduce-scatter.11
  674.8 68.1 reduce-scatter.5

commit v2 on v1

v2 whole, which is shorter than its diff:
```python
import functools

import jax
import jax.numpy as jnp
from jax import lax
from jax.experimental import pallas as pl
from jax.experimental.pallas import tpu as pltpu
from jax.sharding import PartitionSpec as P

HEAD_DIM = 64
ROT = 16
SEQ_LEN = 512
LANES = 128
EPS = 1e-05
F32 = jnp.float32
BF16 = jnp.bfloat16
NT = (((1,), (1,)), ((), ()))
TN = (((0,), (0,)), ((), ()))


def layer_norm(values):
    row_mean = jnp.mean(values, axis=-1, keepdims=True)
    centered = values - row_mean
    inv_sigma = lax.rsqrt(jnp.mean(centered * centered, axis=-1, keepdims=True) + EPS)
    return (centered * inv_sigma, inv_sigma)


def norm_back(grad_hat, normed, inv_sigma):
    return inv_sigma * (
        grad_hat
        - jnp.mean(grad_hat, axis=-1, keepdims=True)
        - normed * jnp.mean(grad_hat * normed, axis=-1, keepdims=True)
    )


def rotary_lanes():
    half = ROT // 2
    frequency = 10000.0 ** (-(2.0 * jnp.arange(half, dtype=F32)) / ROT)
    angles = jnp.arange(SEQ_LEN, dtype=F32)[:, None] * frequency[None, :]
    cosine, sine = jnp.cos(angles), jnp.sin(angles)
    rest = HEAD_DIM - ROT
    zero = jnp.zeros((SEQ_LEN, half), F32)
    tail = jnp.zeros((SEQ_LEN, rest), F32)
    copies = LANES // HEAD_DIM
    keep = jnp.concatenate([cosine, cosine, tail + 1.0] * copies, axis=1)
    low = jnp.concatenate([-sine, zero, tail] * copies, axis=1)
    high = jnp.concatenate([zero, sine, tail] * copies, axis=1)
    return keep, low, high


def bits_of(axis):
    size = lax.axis_size(axis)
    return [1 << b for b in range(size.bit_length() - 1)]


def swap(value, axis, bit):
    return lax.ppermute(value, axis, [(i, i ^ bit) for i in range(lax.axis_size(axis))])


def total_over(value, axis):
    for bit in bits_of(axis):
        value = value + swap(value, axis, bit)
    return value


def row_parts(rows, count):
    tiles = rows // 16
    edges = [16 * (tiles * k // count) for k in range(count)] + [rows]
    return list(zip(edges[:-1], edges[1:]))


def part_plan(rows):
    bits = bits_of("tensor")
    return [
        (lo, hi, bits[k:] + bits[:k]) for k, (lo, hi) in enumerate(row_parts(rows, len(bits)))
    ]


def collect_rows(block):
    parts = []
    for lo, hi, order in part_plan(block.shape[0]):
        held = block[lo:hi]
        for bit in order:
            held = jnp.concatenate([held, swap(held, "tensor", bit)], axis=0)
        parts.append(held)
    return jnp.concatenate(parts, axis=0)


def spread_part(terms, order):
    held = terms
    for bit in order[::-1]:
        half = held.shape[0] // 2
        got = swap(held[half:], "tensor", bit)
        total = held[:half].astype(F32) + got.astype(F32)
        held = total if bit == order[0] else total.astype(BF16)
    return held


def spread_rows(term_fn, group, rows):
    count = lax.axis_size("tensor")
    return jnp.concatenate(
        [
            spread_part(term_fn(slice(lo * count, hi * count)), order)
            for lo, hi, order in part_plan(rows)
        ],
        axis=0,
    )


def frame_pieces(rows):
    count = lax.axis_size("tensor")
    per_seq = SEQ_LEN // rows
    return [
        (member, lo, hi, order)
        for member in range(count)
        for lo, hi, order in part_plan(rows)
    ], per_seq * len(part_plan(rows))


def frame_offsets(rows):
    count = lax.axis_size("tensor")
    here = lax.axis_index("tensor").astype(jnp.int32)
    places = []
    for member, lo, hi, order in frame_pieces(rows)[0]:
        other = here ^ member
        place = jnp.int32(0)
        for j, bit in enumerate(order):
            place = place + jnp.where((other & bit) != 0, 1 << j, 0)
        places.append(lo * count + place * (hi - lo))
    return jnp.stack(places).astype(jnp.int32)


def ring_step(value):
    count = lax.axis_size("dp")
    return lax.ppermute(value, "dp", [(i, (i + 2) % count) for i in range(count)])


def ring_gather(shard, axis):
    count = lax.axis_size("dp")
    here = lax.axis_index("dp")
    size = shard.shape[axis]
    full = jnp.zeros(shard.shape[:axis] + (size * count,) + shard.shape[axis + 1 :], shard.dtype)
    seen = []
    held = shard
    for k in range(count // 2):
        if k:
            held = ring_step(held)
        seen.append(held)
        owner = (here - 2 * k) % count
        full = lax.dynamic_update_slice_in_dim(full, held, owner * size, axis)
        full = lax.dynamic_update_slice_in_dim(full, swap(held, "dp", 1), (owner ^ 1) * size, axis)
    return full, seen


def ring_reduce(grad, axis):
    count = lax.axis_size("dp")
    here = lax.axis_index("dp")
    size = grad.shape[axis] // count
    lead, tail = grad.shape[:axis], grad.shape[axis + 1 :]
    pairs = grad.reshape(lead + (count // 2, 2, size) + tail)
    core = here % 2
    mine = lax.dynamic_index_in_dim(pairs, core, axis + 1, keepdims=False)
    other = lax.dynamic_index_in_dim(pairs, 1 - core, axis + 1, keepdims=False)
    other = swap(other, "dp", 1)

    def block(k):
        owner = (here // 2 - k) % (count // 2)
        return lax.dynamic_index_in_dim(mine, owner, axis, keepdims=False).astype(
            F32
        ) + lax.dynamic_index_in_dim(other, owner, axis, keepdims=False).astype(F32)

    total = block(1)
    for k in list(range(2, count // 2)) + [0]:
        total = block(k) + ring_step(total.astype(BF16)).astype(F32)
    return total


def after(value, *others):
    return lax.optimization_barrier((value,) + others)[0]


def ordered(ref, lead, offs_ref, runs):
    return jnp.concatenate(
        [
            ref[lead + (pl.ds(pl.multiple_of(offs_ref[i], 16), size), slice(None))]
            for i, size in runs
        ],
        axis=0,
    )


def put_ordered(ref, lead, offs_ref, runs, value):
    at = 0
    for i, size in runs:
        ref[lead + (pl.ds(pl.multiple_of(offs_ref[i], 16), size), slice(None))] = value[
            at : at + size
        ]
        at += size


CHUNK = 256
HEADS_STEP = LANES // HEAD_DIM


def lane_roll(value, shift):
    return pltpu.roll(value, shift % LANES, 1)


def masked(scores, start):
    rows = lax.broadcasted_iota(jnp.int32, scores.shape, 0) + start
    cols = lax.broadcasted_iota(jnp.int32, scores.shape, 1)
    return jnp.where(rows >= cols, scores, -jnp.inf)


def attend_kernel(offs_ref, pre_ref, keep_ref, low_ref, high_ref, qkv_ref, ctx_ref, lse_ref, *, runs):
    for seq, seq_runs in enumerate(runs):
        attend_seq(
            offs_ref, pre_ref, keep_ref, low_ref, high_ref, qkv_ref, ctx_ref, lse_ref, seq, seq_runs
        )


def attend_seq(
    offs_ref, pre_ref, keep_ref, low_ref, high_ref, qkv_ref, ctx_ref, lse_ref, seq, runs
):
    half = ROT // 2
    scale = HEAD_DIM ** (-0.5)
    keep, low, high = keep_ref[...], low_ref[...], high_ref[...]
    for c in range(3):
        v = ordered(pre_ref, (c,), offs_ref, runs)
        if c < 2:
            v = v * keep + lane_roll(v, -half) * low + lane_roll(v, half) * high
        qkv_ref[c, seq] = v.astype(BF16)
    ctx_parts, lse_parts = [], []
    for start in range(0, SEQ_LEN, CHUNK):
        end = start + CHUNK
        ctxs, lses = [], []
        for h in range(HEADS_STEP):
            cols = slice(h * HEAD_DIM, (h + 1) * HEAD_DIM)
            q = qkv_ref[0, seq, start:end, cols]
            k = qkv_ref[1, seq, :end, cols]
            v = qkv_ref[2, seq, :end, cols]
            s = lax.dot_general(q, k, NT, preferred_element_type=F32) * scale
            s = masked(s, start)
            top = jnp.max(s, axis=-1, keepdims=True)
            e = jnp.exp(s - top)
            total = jnp.sum(e, axis=-1, keepdims=True)
            p = (e * (1.0 / total)).astype(BF16)
            ctxs.append(jnp.dot(p, v, preferred_element_type=F32).astype(BF16))
            lses.append(jnp.broadcast_to(top + jnp.log(total), (CHUNK, HEAD_DIM)))
        ctx_parts.append(jnp.concatenate(ctxs, axis=1))
        lse_parts.append(jnp.concatenate(lses, axis=1))
    put_ordered(ctx_ref, (), offs_ref, runs, jnp.concatenate(ctx_parts, axis=0))
    lse_ref[seq] = jnp.concatenate(lse_parts, axis=0)


def attend_back_kernel(offs_ref, *refs, runs):
    for seq, seq_runs in enumerate(runs):
        attend_back_seq(offs_ref, *refs, seq, seq_runs)


def attend_back_seq(
    offs_ref,
    qkv_ref,
    ctx_ref,
    gctx_ref,
    lse_ref,
    keep_ref,
    low_ref,
    high_ref,
    gpre_ref,
    bias_ref,
    seq,
    runs,
):
    half = ROT // 2
    scale = HEAD_DIM ** (-0.5)
    ctx = ordered(ctx_ref, (), offs_ref, runs)
    gctx = ordered(gctx_ref, (), offs_ref, runs)
    prod = gctx.astype(F32) * ctx.astype(F32)
    starts = list(range(0, SEQ_LEN, CHUNK))
    gq, gk, gv = [], [], []
    for h in range(HEADS_STEP):
        cols = slice(h * HEAD_DIM, (h + 1) * HEAD_DIM)
        dq_parts = []
        dk = [None] * len(starts)
        dv = [None] * len(starts)
        for i, start in enumerate(starts):
            end = start + CHUNK
            q = qkv_ref[0, seq, start:end, cols]
            k = qkv_ref[1, seq, :end, cols]
            v = qkv_ref[2, seq, :end, cols]
            g = gctx[start:end, cols]
            lse = lse_ref[seq, start:end, h * HEAD_DIM : h * HEAD_DIM + 1]
            delta = jnp.sum(prod[start:end, cols], axis=-1, keepdims=True)
            s = lax.dot_general(q, k, NT, preferred_element_type=F32) * scale
            p = jnp.exp(masked(s, start) - lse)
            dp = lax.dot_general(g, v, NT, preferred_element_type=F32)
            ds = (p * (dp - delta) * scale).astype(BF16)
            p_low = p.astype(BF16)
            dq_parts.append(jnp.dot(ds, k, preferred_element_type=F32))
            dk_i = lax.dot_general(ds, q, TN, preferred_element_type=F32)
            dv_i = lax.dot_general(p_low, g, TN, preferred_element_type=F32)
            for j in range(i + 1):
                part = slice(j * CHUNK, (j + 1) * CHUNK)
                dk[j] = dk_i[part] if dk[j] is None else dk[j] + dk_i[part]
                dv[j] = dv_i[part] if dv[j] is None else dv[j] + dv_i[part]
        gq.append(jnp.concatenate(dq_parts, axis=0))
        gk.append(jnp.concatenate(dk, axis=0))
        gv.append(jnp.concatenate(dv, axis=0))
    keep, low, high = keep_ref[...], low_ref[...], high_ref[...]
    for c, parts in enumerate((gq, gk, gv)):
        v = jnp.concatenate(parts, axis=1)
        if c < 2:
            v = v * keep - lane_roll(v, -half) * low - lane_roll(v, half) * high
        v = v.astype(BF16)
        put_ordered(gpre_ref, (c,), offs_ref, runs, v)
        bias_ref[seq, c : c + 1] = jnp.sum(v.astype(F32), axis=0, keepdims=True)


def attend_specs(seqs, group_rows):
    table = pl.BlockSpec((SEQ_LEN, LANES), lambda h, f: (0, 0))
    framed3 = pl.BlockSpec((3, group_rows, LANES), lambda h, f: (0, 0, h))
    framed = pl.BlockSpec((group_rows, LANES), lambda h, f: (0, h))
    natural3 = pl.BlockSpec((3, seqs, SEQ_LEN, LANES), lambda h, f: (0, 0, 0, h))
    natural = pl.BlockSpec((seqs, SEQ_LEN, LANES), lambda h, f: (0, 0, h))
    bias = pl.BlockSpec((seqs, 3, LANES), lambda h, f: (0, 0, h))
    return table, framed3, framed, natural3, natural, bias


def sequence_runs(rows):
    pieces, per_seq = frame_pieces(rows)
    runs = [(i, hi - lo) for i, (_, lo, hi, _) in enumerate(pieces)]
    return tuple(tuple(runs[i : i + per_seq]) for i in range(0, len(runs), per_seq))


def attend(offs, pre, tables, runs):
    _, group_rows, cols = pre.shape
    seqs = group_rows // SEQ_LEN
    table, framed3, framed, natural3, natural, _ = attend_specs(seqs, group_rows)
    return pl.pallas_call(
        functools.partial(attend_kernel, runs=runs),
        out_shape=(
            jax.ShapeDtypeStruct((3, seqs, SEQ_LEN, cols), BF16),
            jax.ShapeDtypeStruct((group_rows, cols), BF16),
            jax.ShapeDtypeStruct((seqs, SEQ_LEN, cols), F32),
        ),
        grid_spec=pltpu.PrefetchScalarGridSpec(
            num_scalar_prefetch=1,
            grid=(cols // LANES,),
            in_specs=[framed3, table, table, table],
            out_specs=[natural3, framed, natural],
        ),
        name="attend",
    )(offs, pre, *tables)


def attend_back(offs, qkv, ctx, gctx, lse, tables, runs):
    _, seqs, _, cols = qkv.shape
    group_rows = seqs * SEQ_LEN
    table, framed3, framed, natural3, natural, bias = attend_specs(seqs, group_rows)
    return pl.pallas_call(
        functools.partial(attend_back_kernel, runs=runs),
        out_shape=(
            jax.ShapeDtypeStruct((3, group_rows, cols), BF16),
            jax.ShapeDtypeStruct((seqs, 3, cols), F32),
        ),
        grid_spec=pltpu.PrefetchScalarGridSpec(
            num_scalar_prefetch=1,
            grid=(cols // LANES,),
            in_specs=[natural3, framed, framed, natural, table, table, table],
            out_specs=[framed3, bias],
        ),
        name="attend_back",
    )(offs, qkv, ctx, gctx, lse, *tables)


def shards(
    layer_input,
    norm1_gain,
    norm1_bias,
    qkv_weight,
    qkv_bias,
    out_weight,
    norm2_gain,
    norm2_bias,
    gate_up_weight,
    down_weight,
    out_cotangent,
):
    rows, width = layer_input.shape
    part = norm1_gain.shape[0]
    dp_count = lax.axis_size("dp")
    dp_here = lax.axis_index("dp")
    group_rows = rows * lax.axis_size("tensor")
    head_cols = qkv_weight.shape[2]
    offs = frame_offsets(rows)
    runs = sequence_runs(rows)
    tables = rotary_lanes()

    packed = jnp.concatenate(
        [norm1_gain, norm1_bias, norm2_gain, norm2_bias, qkv_bias.reshape(-1)]
    )[None]
    for bit in bits_of("dp"):
        packed = jnp.concatenate([packed, swap(packed, "dp", bit)], axis=0)
    packed = jnp.take(packed, jnp.arange(dp_count) ^ dp_here, axis=0)
    gain_one, bias_one, gain_two, bias_two = (
        packed[:, k * part : (k + 1) * part].reshape(width).astype(F32) for k in range(4)
    )
    bias_local = (
        packed[:, 4 * part :].reshape(dp_count, 3, -1).transpose(1, 0, 2).reshape(3, head_cols)
    ).astype(F32)

    qkv_local, qkv_seen = ring_gather(qkv_weight, 1)
    out_local = lax.all_gather(after(out_weight, qkv_seen[-2]), "dp", axis=1, tiled=True)
    gate_up_local = lax.all_gather(after(gate_up_weight, qkv_seen[-1]), "dp", axis=1, tiled=True)
    down_turned, _ = ring_gather(after(down_weight.T, qkv_seen[-1]), 0)

    x_float = layer_input.astype(F32)
    hat_one, inv_one = layer_norm(x_float)
    rows_one = collect_rows((hat_one * gain_one + bias_one).astype(BF16))
    cot_rows = collect_rows(after(out_cotangent, rows_one))
    pre = (
        jnp.einsum("rd,cdk->crk", rows_one, qkv_local, preferred_element_type=F32)
        + bias_local[:, None, :]
    )
    qkv_heads, context, lse = attend(offs, pre, tables, runs)
    residual = x_float + spread_rows(
        lambda at: jnp.dot(context[at], out_local, preferred_element_type=F32).astype(BF16),
        context,
        rows,
    )

    hat_two, inv_two = layer_norm(residual)
    rows_two = collect_rows((hat_two * gain_two + bias_two).astype(BF16))
    gate_proj = jnp.dot(rows_two, gate_up_local[0], preferred_element_type=F32)
    up_proj = jnp.dot(rows_two, gate_up_local[1], preferred_element_type=F32)
    sigmoid_gate = jax.nn.sigmoid(gate_proj)
    silu_gate = gate_proj * sigmoid_gate
    activation = (silu_gate * up_proj).astype(BF16)

    grad_down = lax.dot_general(cot_rows, activation, TN, preferred_element_type=F32)
    share_down = ring_reduce(grad_down.astype(BF16), 0).T
    grad_act = jnp.dot(cot_rows, down_turned, preferred_element_type=F32)
    grad_gate = (
        grad_act * up_proj * sigmoid_gate * (1.0 + gate_proj * (1.0 - sigmoid_gate))
    ).astype(BF16)
    grad_up = (grad_act * silu_gate).astype(BF16)
    grad_normed_two = spread_rows(
        lambda at: (
            lax.dot_general(grad_gate[at], gate_up_local[0], NT, preferred_element_type=F32)
            + lax.dot_general(grad_up[at], gate_up_local[1], NT, preferred_element_type=F32)
        ).astype(BF16),
        grad_gate,
        rows,
    )
    grad_wgate = lax.dot_general(
        rows_two, grad_gate, TN, preferred_element_type=F32
    ).astype(BF16)
    grad_wup = lax.dot_general(rows_two, grad_up, TN, preferred_element_type=F32).astype(BF16)
    share_gate = lax.psum_scatter(grad_wgate, "dp", scatter_dimension=0, tiled=True).astype(F32)
    share_up = lax.psum_scatter(grad_wup, "dp", scatter_dimension=0, tiled=True).astype(F32)
    grad_normed_two = after(grad_normed_two, grad_wgate, grad_wup)
    grad_resid = out_cotangent.astype(F32) + norm_back(
        grad_normed_two * gain_two, hat_two, inv_two
    )

    resid_rows = collect_rows(grad_resid.astype(BF16))
    late_act = after(activation, resid_rows)
    layer_output = (
        residual
        + spread_rows(
            lambda at: lax.dot_general(
                late_act[at], down_turned, NT, preferred_element_type=F32
            ).astype(BF16),
            activation,
            rows,
        )
    ).astype(BF16)
    grad_context = lax.dot_general(
        resid_rows, out_local, NT, preferred_element_type=F32
    ).astype(BF16)
    grad_pre, bias_sums = attend_back(offs, qkv_heads, context, grad_context, lse, tables, runs)
    grad_wqkv = jnp.einsum(
        "rd,crk->cdk", rows_one, grad_pre, preferred_element_type=F32
    ).astype(BF16)
    share_qkv = ring_reduce(grad_wqkv, 1)
    late_pre = after(grad_pre, grad_wqkv)
    grad_normed_one = spread_rows(
        lambda at: jnp.einsum(
            "crk,cdk->rd", late_pre[:, at], qkv_local, preferred_element_type=F32
        ).astype(BF16),
        grad_pre,
        rows,
    )
    grad_wout = lax.dot_general(context, resid_rows, TN, preferred_element_type=F32)
    share_out = lax.psum_scatter(
        grad_wout.astype(BF16), "dp", scatter_dimension=1, tiled=True
    ).astype(F32)
    grad_input = grad_resid + norm_back(grad_normed_one * gain_one, hat_one, inv_one)

    bias_total = total_over(jnp.sum(bias_sums, axis=0), "dp")
    bias_part = qkv_bias.shape[1]
    share_bias = lax.dynamic_slice_in_dim(bias_total, dp_here * bias_part, bias_part, axis=1)
    norm_sums = jnp.stack(
        [
            jnp.sum(grad_normed_one * hat_one, axis=0),
            jnp.sum(grad_normed_one, axis=0),
            jnp.sum(grad_normed_two * hat_two, axis=0),
            jnp.sum(grad_normed_two, axis=0),
        ]
    )
    norm_total = total_over(total_over(norm_sums, "tensor"), "dp")
    share_norm = lax.dynamic_slice_in_dim(norm_total, dp_here * part, part, axis=1)
    return (
        layer_output,
        grad_input,
        share_norm[0],
        share_norm[1],
        share_qkv,
        share_bias,
        share_out,
        share_norm[2],
        share_norm[3],
        jnp.stack([share_gate, share_up]),
        share_down,
    )


def solution(mesh):
    placed = (
        P(("dp", "tensor"), None),
        P("dp"),
        P("dp"),
        P(None, "dp", "tensor"),
        P(None, ("tensor", "dp")),
        P("tensor", "dp"),
        P("dp"),
        P("dp"),
        P(None, "dp", "tensor"),
        P("tensor", "dp"),
        P(("dp", "tensor"), None),
    )
    return jax.shard_map(
        shards,
        mesh=mesh,
        in_specs=placed,
        out_specs=(
            P(("dp", "tensor"), None),
            P(("dp", "tensor"), None),
            P("dp"),
            P("dp"),
            P(None, "dp", "tensor"),
            P(None, ("tensor", "dp")),
            P("tensor", "dp"),
            P("dp"),
            P("dp"),
            P(None, "dp", "tensor"),
            P("tensor", "dp"),
        ),
        check_vma=False,
    )
```

time: 763 us -> 836 us (1.096)
  local copies, waits for them, and re-layouts: 39.1 us -> 148 us
  waiting for transfers between devices: 394 us -> 346 us
  blocking collectives: 32.6 us -> 0 us
  other arithmetic: 29.3 us -> 47.3 us
  starting transfers between devices: 60.9 us -> 73.9 us
  matrix products: 142 us -> 155 us
    reduce_scatter x4 -> x2, waiting for transfers between devices: 146 us -> 0.01 us  [the longest x1 0.01 us: shards(): lax.psum_scatter(grad_wup, 'dp', scatter_dimension=0, tiled=True)]
    ppermute x0 -> x12, waiting for transfers between devices: none -> 120 us  [ring_step(): lax.ppermute(value, 'dp', [(i, (i + 2) % count) for i in range(count)])]
    dynamic_slice x0 -> x6, local copies, waits for them, and re-layouts: none -> 41.3 us  [the longest x4 30.4 us: ring_reduce(): other = lax.dynamic_index_in_dim(pairs, 1 - core, axis + 1, keepdims=False)]
    unnamed x1 -> x0, blocking collectives: 32.6 us -> none
    all_gather x4 -> x2, waiting for transfers between devices: 28 us -> 0.01 us  [the longest x1 0.01 us: shards(): lax.all_gather(after(out_weight, qkv_seen[-2]), 'dp', axis=1, tiled=True)]
    ppermute x0 -> x12, starting transfers between devices: none -> 23.9 us  [ring_step(): lax.ppermute(value, 'dp', [(i, (i + 2) % count) for i in range(count)])]
    dynamic_update_slice x0 -> x16, local copies, waits for them, and re-layouts: none -> 20.3 us  [the longest x8 10.4 us: ring_gather(): lax.dynamic_update_slice_in_dim(full, swap(held, 'dp', 1), (owner ^ 1) *...]
    unnamed x81 -> x148, local copies, waits for them, and re-layouts: 28.4 us -> 48.2 us
  transfers between devices with their start and end apart: 65 -> 70, of which waited for: 42 -> 28; matrix products, arithmetic and copies ran while one was open for 22% -> 34% of each run, Pallas kernels for 5% -> 5%
where the time goes in v2:
time: 836 us; the launch traced here: 827 us
  waiting for transfers between devices  346 us (41%)
  matrix products  155 us (19%)
  local copies, waits for them, and re-layouts  148 us (18%)
  starting transfers between devices  73.9 us (9%)
  other arithmetic  47.3 us (6%)
  Pallas kernels  41 us (5%)
  between operations  15.3 us (2%)
    ppermute x53, waiting for transfers between devices, swap(): lax.ppermute(value, axis, [(i, i ^ bit) for i in range(lax.axis_size(axis...  226 us
    ppermute x12, waiting for transfers between devices, ring_step(): lax.ppermute(value, 'dp', [(i, (i + 2) % count) for i in range(count)])  120 us
    ppermute x53, starting transfers between devices, swap(): lax.ppermute(value, axis, [(i, i ^ bit) for i in range(lax.axis_size(axis...  49.8 us
    unnamed x148, local copies, waits for them, and re-layouts  48.2 us
    dynamic_slice x4, local copies, waits for them, and re-layouts, ring_reduce(): other = lax.dynamic_index_in_dim(pairs, 1 - core, axis + 1, keepdims=False)  30.4 us
    ppermute x12, starting transfers between devices, ring_step(): lax.ppermute(value, 'dp', [(i, (i + 2) % count) for i in range(count)])  23.9 us
    pallas_call x1, Pallas kernels, attend(): pl.pallas_call(functools.partial(attend_kernel, runs=runs), out_shape=(ja...  20.5 us
    pallas_call x1, Pallas kernels, attend_back(): pl.pallas_call(functools.partial(attend_back_kernel, runs=runs), out_shap...  20.4 us
  transfers between devices with their start and end apart: 70, of which 28 were waited for; matrix products, arithmetic and copies ran while one was open for 34% of the time, Pallas kernels for 5%

profile of v2, /device:TPU:0, one launch (start us, length us, event | category | flops | bytes accessed | tf_op | source)
XLA Modules:
  0.0 827.2 jit_solution(7371861624360535165)
XLA Ops:
  10.3 19.8 %collective-permute-done.1 = bf16[3,256,512]{2,1,0:T(8,128)(2,1)S(1)} collective-permute-done((bf16[3,256,512]{2,1,0:T(8,128)(2,1)}, bf16[3,256,512]{2,1,0:T(8,128)(2,1)S(1)}, u32[]{:S(2)}, u32[]{:S(2)}) %collective-permute-start.1) | collective-permute-done | bytes 786464 | tf_op jit(solution)/shard_map/ppermute | solution.py:135
  31.0 20.5 %collective-permute-done.3 = bf16[3,256,512]{2,1,0:T(8,128)(2,1)S(1)} collective-permute-done((bf16[3,256,512]{2,1,0:T(8,128)(2,1)S(1)}, bf16[3,256,512]{2,1,0:T(8,128)(2,1)S(1)}, u32[]{:S(2)}, u32[]{:S(2)}) %collective-permute-start.3) | collective-permute-done | bytes 786464 | tf_op jit(solution)/shard_map/ppermute | solution.py:135
  57.4 26.2 %collective-permute-done.5 = bf16[3,256,512]{2,1,0:T(8,128)(2,1)S(1)} collective-permute-done((bf16[3,256,512]{2,1,0:T(8,128)(2,1)S(1)}, bf16[3,256,512]{2,1,0:T(8,128)(2,1)S(1)}, u32[]{:S(2)}, u32[]{:S(2)}) %collective-permute-start.5) | collective-permute-done | bytes 786464 | tf_op jit(solution)/shard_map/ppermute | solution.py:135
  120.0 13.5 %collective-permute-done.11 = bf16[256,2048]{1,0:T(8,128)(2,1)} collective-permute-done((bf16[256,2048]{1,0:T(8,128)(2,1)}, bf16[256,2048]{1,0:T(8,128)(2,1)}, u32[]{:S(2)}, u32[]{:S(2)}) %collective-permute-start.11) | collective-permute-done | bytes 1048608 | tf_op jit(solution)/shard_map/ppermute | solution.py:57
  166.4 28.8 %collective-permute-done.27 = bf16[256,1408]{0,1:T(8,128)(2,1)} collective-permute-done((bf16[256,1408]{0,1:T(8,128)(2,1)S(1)}, bf16[256,1408]{0,1:T(8,128)(2,1)}, u32[]{:S(2)}, u32[]{:S(2)}) %collective-permute-start.27) | collective-permute-done | bytes 720928 | tf_op jit(solution)/shard_map/ppermute | solution.py:135
  195.2 12.0 %collective-permute-start.29 = (bf16[256,1408]{0,1:T(8,128)(2,1)}, bf16[256,1408]{0,1:T(8,128)(2,1)}, u32[]{:S(2)}, u32[]{:S(2)}) collective-permute-start(bf16[256,1408]{0,1:T(8,128)(2,1)} %collective-permute-done.27), channel_id=1, source_target_pairs={{0,8},{4,12},{8,16},{12,20},{16,24},{20,28},{24,0},{28,4},{1,9},{5... | collective-permute-start | bytes 2162696 | tf_op jit(solution)/shard_map/ppermute | solution.py:135
  221.8 20.5 %attend.1 = (bf16[3,2,512,512]{3,2,1,0:T(8,128)(2,1)}, bf16[1024,512]{1,0:T(8,128)(2,1)}, f32[2,512,512]{2,1,0:T(8,128)}) custom-call(s32[8]{0:T(128)} %stack.62.offs_ref, f32[3,1024,512]{2,1,0:T(8,128)} %add_bitcast_fusion.pre_ref, f32[512,128]{1,0:T(8,128)} %concatenate.82.keep_ref.refs_4_, f32[512,128]{1,0:T(8,128)} %concatenate.83.low_ref.refs_5_, ...), custom_call_target="tpu_custom_call" | custom-call | tf_op jit(solution)/shard_map/attend/pallas_call | solution.py:340
  250.6 20.3 %collective-permute-done.16 = bf16[256,2048]{1,0:T(8,128)(2,1)S(1)} collective-permute-done((bf16[256,2048]{1,0:T(8,128)(2,1)S(1)}, bf16[256,2048]{1,0:T(8,128)(2,1)S(1)}, u32[]{:S(2)}, u32[]{:S(2)}) %collective-permute-start.16) | collective-permute-done | bytes 1048608 | tf_op jit(solution)/shard_map/ppermute | solution.py:57
  313.2 20.2 %collective-permute-done.19 = bf16[256,2048]{1,0:T(8,128)(2,1)S(1)} collective-permute-done((bf16[256,2048]{1,0:T(8,128)(2,1)S(1)}, bf16[256,2048]{1,0:T(8,128)(2,1)S(1)}, u32[]{:S(2)}, u32[]{:S(2)}) %collective-permute-start.19) | collective-permute-done | bytes 1048608 | tf_op jit(solution)/shard_map/ppermute | solution.py:57
  337.2 12.2 %fusion.3 = f32[1024,1408]{1,0:T(8,128)} fusion(bf16[1024,2048]{1,0:T(8,128)(2,1)} %constant_dynamic-update-slice_fusion.6, bf16[2,2048,1408]{2,1,0:T(8,128)(2,1)} %all-gather.5.cloned.1.call-done), kind=kOutput, calls=%fused_computation.15 | convolution fusion | flops 5905580032 | bytes 15728640 | tf_op jit(solution)/shard_map/dot_general | solution.py:435
  359.6 14.7 %multiply_convert_fusion.1 = (bf16[1024,1408]{1,0:T(8,128)(2,1)S(1)}, bf16[1024,1408]{1,0:T(8,128)(2,1)}, bf16[1024,1408]{1,0:T(8,128)(2,1)}) fusion(f32[1024,1408]{1,0:T(8,128)} %fusion.3, f32[1024,1408]{1,0:T(8,128)} %fusion.6, bf16[1024,2048]{1,0:T(8,128)(2,1)S(1)} %copy-done.41, bf16[2048,1408]{0,1:T(8,128)(2,1)} %constant_dynamic-update-slice_fusion.24), kind=kOutput, calls=%fused_computation.9 | convolution fusion | flops 5927206912 | bytes 30146560 | tf_op jit(solution)/shard_map/dot_general | solution.py:443
  400.9 10.8 %convolution_convert_fusion.2 = bf16[2048,1408]{1,0:T(8,128)(2,1)} fusion(bf16[1024,2048]{1,0:T(8,128)(2,1)} %constant_dynamic-update-slice_fusion.6, bf16[1024,1408]{1,0:T(8,128)(2,1)S(1)} %get-tuple-element.46), kind=kOutput, calls=%fused_computation.3 | convolution fusion | flops 5908463616 | bytes 12845056 | tf_op jit(solution)/shard_map/dot_general | solution.py:456
  430.2 11.3 %convolution_convert_fusion.1 = bf16[2048,1408]{1,0:T(8,128)(2,1)} fusion(bf16[1024,2048]{1,0:T(8,128)(2,1)} %constant_dynamic-update-slice_fusion.6, bf16[1024,1408]{1,0:T(8,128)(2,1)S(1)} %copy-done.51), kind=kOutput, calls=%fused_computation.2 | convolution fusion | flops 5908463616 | bytes 12845056 | tf_op jit(solution)/shard_map/dot_general | solution.py:459
  460.8 30.5 %collective-permute-done.39 = bf16[128,2048]{1,0:T(8,128)(2,1)S(1)} collective-permute-done((bf16[128,2048]{1,0:T(8,128)(2,1)S(1)}, bf16[128,2048]{1,0:T(8,128)(2,1)S(1)}, u32[]{:S(2)}, u32[]{:S(2)}) %collective-permute-start.39) | collective-permute-done | bytes 524320 | tf_op jit(solution)/shard_map/ppermute | solution.py:57
  493.0 18.8 %collective-permute-done.40 = bf16[256,2048]{1,0:T(8,128)(2,1)S(1)} collective-permute-done((bf16[256,2048]{1,0:T(8,128)(2,1)S(1)}, bf16[256,2048]{1,0:T(8,128)(2,1)S(1)}, u32[]{:S(2)}, u32[]{:S(2)}) %collective-permute-start.40) | collective-permute-done | bytes 1048608 | tf_op jit(solution)/shard_map/ppermute | solution.py:57
  557.8 20.4 %attend_back.1 = (bf16[3,1024,512]{2,1,0:T(8,128)(2,1)}, f32[2,3,512]{2,1,0:T(4,128)}) custom-call(s32[8]{0:T(128)} %stack.62.offs_ref, bf16[3,2,512,512]{3,2,1,0:T(8,128)(2,1)} %get-tuple-element.30.refs_0_, bf16[1024,512]{1,0:T(8,128)(2,1)} %get-tuple-element.23.refs_1_, bf16[1024,512]{1,0:T(8,128)(2,1)} %convolution_convert_fusion.8.refs_2_, ...), custom_call_target="tpu_custom_call" | custom-call | tf_op jit(solution)/shard_map/attend_back/pallas_call | solution.py:361
  578.3 11.5 %convert_bitcast_fusion = bf16[3,2048,512]{1,2,0:T(8,128)(2,1)} fusion(bf16[3,1024,512]{2,1,0:T(8,128)(2,1)} %get-tuple-element.33, bf16[1024,2048]{1,0:T(8,128)(2,1)} %constant_dynamic-update-slice_fusion), kind=kOutput, calls=%fused_computation.4 | convolution fusion | flops 6445596672 | bytes 13631488 | tf_op jit(solution)/shard_map/rd,crk->cdk/dot_general | solution.py:483
  604.9 11.2 %reshape.203 = bf16[3,4,2,256,512]{3,2,1,4,0:T(2,128)(2,1)} reshape(bf16[3,2048,512]{1,2,0:T(8,128)(2,1)} %convert_bitcast_fusion) | data formatting | bytes 12582912 | tf_op jit(solution)/shard_map/reshape | solution.py:160
  660.4 15.2 %copy.54 = bf16[3,4,1,256,512]{4,3,0,1,2:T(8,128)(2,1)} copy(bf16[3,4,1,256,512]{3,2,1,4,0:T(2,128)(2,1)} %constant_dynamic-slice_fusion.11) | data formatting | bytes 6291456 | tf_op jit(solution)/shard_map/jit(dynamic_index_in_dim)/dynamic_slice | solution.py:163
  702.2 13.6 %collective-permute-done.45 = bf16[256,2048]{1,0:T(8,128)(2,1)S(1)} collective-permute-done((bf16[256,2048]{1,0:T(8,128)(2,1)}, bf16[256,2048]{1,0:T(8,128)(2,1)S(1)}, u32[]{:S(2)}, u32[]{:S(2)}) %collective-permute-start.45) | collective-permute-done | bytes 1048608 | tf_op jit(solution)/shard_map/ppermute | solution.py:57
  720.1 16.2 %collective-permute-done.48 = bf16[128,2048]{1,0:T(8,128)(2,1)S(1)} collective-permute-done((bf16[128,2048]{1,0:T(8,128)(2,1)S(1)}, bf16[128,2048]{1,0:T(8,128)(2,1)S(1)}, u32[]{:S(2)}, u32[]{:S(2)}) %collective-permute-start.48) | collective-permute-done | bytes 524320 | tf_op jit(solution)/shard_map/ppermute | solution.py:57
  746.9 24.3 %collective-permute-done.55 = bf16[3,256,512]{2,1,0:T(8,128)(2,1)S(1)} collective-permute-done((bf16[3,256,512]{2,1,0:T(8,128)(2,1)S(1)}, bf16[3,256,512]{2,1,0:T(8,128)(2,1)S(1)}, u32[]{:S(2)}, u32[]{:S(2)}) %collective-permute-start.55) | collective-permute-done | bytes 786464 | tf_op jit(solution)/shard_map/ppermute | solution.py:135
  773.2 13.8 %collective-permute-done.52 = f32[4,2048]{1,0:T(4,128)S(1)} collective-permute-done((f32[4,2048]{1,0:T(4,128)S(1)}, f32[4,2048]{1,0:T(4,128)S(1)}, u32[]{:S(2)}, u32[]{:S(2)}) %collective-permute-start.52) | collective-permute-done | bytes 32800 | tf_op jit(solution)/shard_map/ppermute | solution.py:57
  792.2 17.6 %collective-permute-done.53 = f32[4,2048]{1,0:T(4,128)S(1)} collective-permute-done((f32[4,2048]{1,0:T(4,128)S(1)}, f32[4,2048]{1,0:T(4,128)S(1)}, u32[]{:S(2)}, u32[]{:S(2)}) %collective-permute-start.53) | collective-permute-done | bytes 32800 | tf_op jit(solution)/shard_map/ppermute | solution.py:57
  (433 shorter events, 388.0 us)
Async XLA Ops:
  7.2 235.1 %all-gather.3.cloned.1.call-start = ((), (), s32[]{:S(2)}) async-start(), calls=%async_computation.3 | async-start | bytes 2359296 | tf_op jit(solution)/shard_map/all_gather | solution.py:414
  51.5 285.7 %all-gather.5.cloned.1.call-start = ((), (), s32[]{:S(2)}) async-start(), calls=%async_computation.4 | async-start | bytes 12976128 | tf_op jit(solution)/shard_map/all_gather | solution.py:415
  51.6 32.0 %collective-permute-start.5 = (bf16[3,256,512]{2,1,0:T(8,128)(2,1)S(1)}, bf16[3,256,512]{2,1,0:T(8,128)(2,1)S(1)}, u32[]{:S(2)}, u32[]{:S(2)}) collective-permute-start(bf16[3,256,512]{2,1,0:T(8,128)(2,1)S(1)} %collective-permute-done.3), channel_id=1, source_target_pairs={{0,8},{4,12},{8,16},{12,20},{16,24},{20,28},{24,0},{28,4},{1,9},{5... | collective-permute-start | bytes 2359304 | tf_op jit(solution)/shard_map/ppermute | solution.py:135
  83.6 729.3 %reduce-scatter.4.cloned.1.call-start = ((), (), s32[]{:S(2)}) async-start(), calls=%async_computation.5 | async-start | bytes 2359296 | tf_op jit(solution)/shard_map/reduce_scatter | solution.py:496
  96.3 45.4 %collective-permute-start = (bf16[3,256,512]{2,1,0:T(8,128)(2,1)}, bf16[3,256,512]{2,1,0:T(8,128)(2,1)}, u32[]{:S(2)}, u32[]{:S(2)}) collective-permute-start(bf16[3,256,512]{2,1,0:T(8,128)(2,1)} %param.14), channel_id=1, source_target_pairs={{0,4},{4,0},{8,12},{12,8},{16,20},{20,16},{24,28},{28,24},{1,5},{5... | collective-permute-start | bytes 2359304 | tf_op jit(solution)/shard_map/ppermute | solution.py:57
  155.0 93.3 %collective-permute-start.23 = (bf16[256,2048]{1,0:T(8,128)(2,1)}, bf16[256,2048]{1,0:T(8,128)(2,1)}, u32[]{:S(2)}, u32[]{:S(2)}) collective-permute-start(bf16[256,2048]{1,0:T(8,128)(2,1)} %pad_maximum_fusion.6), channel_id=1, source_target_pairs={{0,2},{1,3},{2,0},{3,1},{4,6},{5,7},{6,4},{7,5},{8,10},{9,11},{10,... | collective-permute-start | bytes 3145736 | tf_op jit(solution)/shard_map/ppermute | solution.py:57
  158.4 132.1 %collective-permute-start.25 = (bf16[256,2048]{1,0:T(8,128)(2,1)}, bf16[256,2048]{1,0:T(8,128)(2,1)}, u32[]{:S(2)}, u32[]{:S(2)}) collective-permute-start(bf16[256,2048]{1,0:T(8,128)(2,1)} %pad_maximum_fusion.7), channel_id=1, source_target_pairs={{0,1},{1,0},{2,3},{3,2},{4,5},{5,4},{6,7},{7,6},{8,9},{9,8},{10,11... | collective-permute-start | bytes 3145736 | tf_op jit(solution)/shard_map/ppermute | solution.py:57
  158.9 36.3 %collective-permute-start.26 = (bf16[256,1408]{0,1:T(8,128)(2,1)S(1)}, bf16[256,1408]{0,1:T(8,128)(2,1)S(1)}, u32[]{:S(2)}, u32[]{:S(2)}) collective-permute-start(bf16[256,1408]{0,1:T(8,128)(2,1)S(1)} %bitcast.146), channel_id=1, source_target_pairs={{0,4},{4,0},{8,12},{12,8},{16,20},{20,16},{24,28},{28,24},{1,5},{5... | collective-permute-start | bytes 2162696 | tf_op jit(solution)/shard_map/ppermute | solution.py:57
  158.9 36.3 %collective-permute-start.27 = (bf16[256,1408]{0,1:T(8,128)(2,1)S(1)}, bf16[256,1408]{0,1:T(8,128)(2,1)}, u32[]{:S(2)}, u32[]{:S(2)}) collective-permute-start(bf16[256,1408]{0,1:T(8,128)(2,1)S(1)} %bitcast.147), channel_id=1, source_target_pairs={{0,8},{4,12},{8,16},{12,20},{16,24},{20,28},{24,0},{28,4},{1,9},{5... | collective-permute-start | bytes 2162696 | tf_op jit(solution)/shard_map/ppermute | solution.py:135
  159.8 50.5 %collective-permute-start.6 = (bf16[3,256,512]{2,1,0:T(8,128)(2,1)S(1)}, bf16[3,256,512]{2,1,0:T(8,128)(2,1)S(1)}, u32[]{:S(2)}, u32[]{:S(2)}) collective-permute-start(bf16[3,256,512]{2,1,0:T(8,128)(2,1)S(1)} %copy-done.30), channel_id=1, source_target_pairs={{0,4},{4,0},{8,12},{12,8},{16,20},{20,16},{24,28},{28,24},{1,5},{5... | collective-permute-start | bytes 2359304 | tf_op jit(solution)/shard_map/ppermute | solution.py:57
  195.2 96.7 %collective-permute-start.28 = (bf16[256,1408]{0,1:T(8,128)(2,1)}, bf16[256,1408]{0,1:T(8,128)(2,1)}, u32[]{:S(2)}, u32[]{:S(2)}) collective-permute-start(bf16[256,1408]{0,1:T(8,128)(2,1)} %collective-permute-done.27), channel_id=1, source_target_pairs={{0,4},{4,0},{8,12},{12,8},{16,20},{20,16},{24,28},{28,24},{1,5},{5... | collective-permute-start | bytes 2162696 | tf_op jit(solution)/shard_map/ppermute | solution.py:57
  195.2 79.9 %collective-permute-start.29 = (bf16[256,1408]{0,1:T(8,128)(2,1)}, bf16[256,1408]{0,1:T(8,128)(2,1)}, u32[]{:S(2)}, u32[]{:S(2)}) collective-permute-start(bf16[256,1408]{0,1:T(8,128)(2,1)} %collective-permute-done.27), channel_id=1, source_target_pairs={{0,8},{4,12},{8,16},{12,20},{16,24},{20,28},{24,0},{28,4},{1,9},{5... | collective-permute-start | bytes 2162696 | tf_op jit(solution)/shard_map/ppermute | solution.py:135
  458.7 34.2 %collective-permute-start.38 = (bf16[256,2048]{1,0:T(8,128)(2,1)S(1)}, bf16[256,2048]{1,0:T(8,128)(2,1)S(1)}, u32[]{:S(2)}, u32[]{:S(2)}) collective-permute-start(bf16[256,2048]{1,0:T(8,128)(2,1)S(1)} %pad_maximum_fusion.8), channel_id=1, source_target_pairs={{0,2},{1,3},{2,0},{3,1},{4,6},{5,7},{6,4},{7,5},{8,10},{9,11},{10,... | collective-permute-start | bytes 3145736 | tf_op jit(solution)/shard_map/ppermute | solution.py:57
  517.7 299.6 %reduce-scatter.8.cloned.1.call-start = ((), (), s32[]{:S(2)}) async-start(), calls=%async_computation.7 | async-start | bytes 6488064 | tf_op jit(solution)/shard_map/reduce_scatter | solution.py:461
  518.3 299.0 %reduce-scatter.6.cloned.1.call-start = ((), (), s32[]{:S(2)}) async-start(), calls=%async_computation.6 | async-start | bytes 6488064 | tf_op jit(solution)/shard_map/reduce_scatter | solution.py:460
  549.2 141.8 %collective-permute-start.62 = (bf16[256,1408]{0,1:T(8,128)(2,1)}, bf16[256,1408]{0,1:T(8,128)(2,1)}, u32[]{:S(2)}, u32[]{:S(2)}) collective-permute-start(bf16[256,1408]{0,1:T(8,128)(2,1)} %fusion.39), channel_id=1, source_target_pairs={{0,8},{4,12},{8,16},{12,20},{16,24},{20,28},{24,0},{28,4},{1,9},{5... | collective-permute-start | bytes 2162696 | tf_op jit(solution)/shard_map/ppermute | solution.py:135
  641.4 51.7 %collective-permute-start.43 = (bf16[256,2048]{1,0:T(8,128)(2,1)}, bf16[256,2048]{1,0:T(8,128)(2,1)}, u32[]{:S(2)}, u32[]{:S(2)}) collective-permute-start(bf16[256,2048]{1,0:T(8,128)(2,1)} %slice.288), channel_id=1, source_target_pairs={{0,1},{1,0},{2,3},{3,2},{4,5},{5,4},{6,7},{7,6},{8,9},{9,8},{10,11... | collective-permute-start | bytes 3145736 | tf_op jit(solution)/shard_map/ppermute | solution.py:57
  642.8 46.8 %collective-permute-start.60 = (f32[3,512]{1,0:T(4,128)S(1)}, f32[3,512]{1,0:T(4,128)S(1)}, u32[]{:S(2)}, u32[]{:S(2)}) collective-permute-start(f32[3,512]{1,0:T(4,128)S(1)} %add.480), channel_id=1, source_target_pairs={{0,16},{4,20},{8,24},{12,28},{16,0},{20,4},{24,8},{28,12},{1,17},{... | collective-permute-start | bytes 18440 | tf_op jit(solution)/shard_map/ppermute | solution.py:57
  653.1 42.7 %collective-permute-start.41 = (bf16[256,2048]{1,0:T(8,128)(2,1)}, bf16[256,2048]{1,0:T(8,128)(2,1)}, u32[]{:S(2)}, u32[]{:S(2)}) collective-permute-start(bf16[256,2048]{1,0:T(8,128)(2,1)} %slice.284), channel_id=1, source_target_pairs={{0,2},{1,3},{2,0},{3,1},{4,6},{5,7},{6,4},{7,5},{8,10},{9,11},{10,... | collective-permute-start | bytes 3145736 | tf_op jit(solution)/shard_map/ppermute | solution.py:57
  655.6 43.1 %collective-permute-start.47 = (bf16[256,2048]{1,0:T(8,128)(2,1)}, bf16[256,2048]{1,0:T(8,128)(2,1)}, u32[]{:S(2)}, u32[]{:S(2)}) collective-permute-start(bf16[256,2048]{1,0:T(8,128)(2,1)} %slice.296), channel_id=1, source_target_pairs={{0,1},{1,0},{2,3},{3,2},{4,5},{5,4},{6,7},{7,6},{8,9},{9,8},{10,11... | collective-permute-start | bytes 3145736 | tf_op jit(solution)/shard_map/ppermute | solution.py:57
  691.0 52.8 %collective-permute-start.54 = (bf16[3,4,256,512]{3,2,0,1:T(8,128)(2,1)}, bf16[3,4,256,512]{3,2,0,1:T(8,128)(2,1)S(1)}, u32[]{:S(2)}, u32[]{:S(2)}) collective-permute-start(bf16[3,4,256,512]{3,2,0,1:T(8,128)(2,1)} %bitcast.144), channel_id=1, source_target_pairs={{0,4},{4,0},{8,12},{12,8},{16,20},{20,16},{24,28},{28,24},{1,5},{5... | collective-permute-start | bytes 9437192 | tf_op jit(solution)/shard_map/ppermute | solution.py:57
  695.8 49.4 %collective-permute-start.44 = (bf16[128,2048]{1,0:T(8,128)(2,1)S(1)}, bf16[128,2048]{1,0:T(8,128)(2,1)S(1)}, u32[]{:S(2)}, u32[]{:S(2)}) collective-permute-start(bf16[128,2048]{1,0:T(8,128)(2,1)S(1)} %slice.290), channel_id=1, source_target_pairs={{0,2},{1,3},{2,0},{3,1},{4,6},{5,7},{6,4},{7,5},{8,10},{9,11},{10,... | collective-permute-start | bytes 1572872 | tf_op jit(solution)/shard_map/ppermute | solution.py:57
  698.7 72.9 %collective-permute-start.42 = (bf16[128,2048]{1,0:T(8,128)(2,1)S(1)}, bf16[128,2048]{1,0:T(8,128)(2,1)S(1)}, u32[]{:S(2)}, u32[]{:S(2)}) collective-permute-start(bf16[128,2048]{1,0:T(8,128)(2,1)S(1)} %slice.286), channel_id=1, source_target_pairs={{0,1},{1,0},{2,3},{3,2},{4,5},{5,4},{6,7},{7,6},{8,9},{9,8},{10,11... | collective-permute-start | bytes 1572872 | tf_op jit(solution)/shard_map/ppermute | solution.py:57
  736.2 74.1 %collective-permute-start.64 = (bf16[256,1408]{0,1:T(8,128)(2,1)S(1)}, bf16[256,1408]{0,1:T(8,128)(2,1)S(1)}, u32[]{:S(2)}, u32[]{:S(2)}) collective-permute-start(bf16[256,1408]{0,1:T(8,128)(2,1)S(1)} %fusion.43), channel_id=1, source_target_pairs={{0,8},{4,12},{8,16},{12,20},{16,24},{20,28},{24,0},{28,4},{1,9},{5... | collective-permute-start | bytes 2162696 | tf_op jit(solution)/shard_map/ppermute | solution.py:135
  (104 other events, 1669.8 us)
Sparse Core Ops, SparseCore 0:
  51.6 38.4 all-gather.2
  91.8 121.1 all-gather.4
  517.8 36.1 reduce-scatter.3
  556.2 68.7 reduce-scatter.7
  627.1 64.7 reduce-scatter.5

commit v3 on v2

--- a/solution.py
+++ b/solution.py
@@ -6,6 +6,7 @@
 from jax.experimental import pallas as pl
 from jax.experimental.pallas import tpu as pltpu
 from jax.sharding import PartitionSpec as P
+
 
 HEAD_DIM = 64
 ROT = 16
@@ -96,14 +97,14 @@
     return held
 
 
-def spread_rows(term_fn, group, rows):
+def part_slices(rows):
     count = lax.axis_size("tensor")
+    return [slice(lo * count, hi * count) for lo, hi, _ in part_plan(rows)]
+
+
+def spread_rows(terms, rows):
     return jnp.concatenate(
-        [
-            spread_part(term_fn(slice(lo * count, hi * count)), order)
-            for lo, hi, order in part_plan(rows)
-        ],
-        axis=0,
+        [spread_part(t, order) for t, (_, _, order) in zip(terms, part_plan(rows))], axis=0
     )
 
 
@@ -128,51 +129,6 @@
             place = place + jnp.where((other & bit) != 0, 1 << j, 0)
         places.append(lo * count + place * (hi - lo))
     return jnp.stack(places).astype(jnp.int32)
-
-
-def ring_step(value):
-    count = lax.axis_size("dp")
-    return lax.ppermute(value, "dp", [(i, (i + 2) % count) for i in range(count)])
-
-
-def ring_gather(shard, axis):
-    count = lax.axis_size("dp")
-    here = lax.axis_index("dp")
-    size = shard.shape[axis]
-    full = jnp.zeros(shard.shape[:axis] + (size * count,) + shard.shape[axis + 1 :], shard.dtype)
-    seen = []
-    held = shard
-    for k in range(count // 2):
-        if k:
-            held = ring_step(held)
-        seen.append(held)
-        owner = (here - 2 * k) % count
-        full = lax.dynamic_update_slice_in_dim(full, held, owner * size, axis)
-        full = lax.dynamic_update_slice_in_dim(full, swap(held, "dp", 1), (owner ^ 1) * size, axis)
-    return full, seen
-
-
-def ring_reduce(grad, axis):
-    count = lax.axis_size("dp")
-    here = lax.axis_index("dp")
-    size = grad.shape[axis] // count
-    lead, tail = grad.shape[:axis], grad.shape[axis + 1 :]
-    pairs = grad.reshape(lead + (count // 2, 2, size) + tail)
-    core = here % 2
-    mine = lax.dynamic_index_in_dim(pairs, core, axis + 1, keepdims=False)
-    other = lax.dynamic_index_in_dim(pairs, 1 - core, axis + 1, keepdims=False)
-    other = swap(other, "dp", 1)
-
-    def block(k):
-        owner = (here // 2 - k) % (count // 2)
-        return lax.dynamic_index_in_dim(mine, owner, axis, keepdims=False).astype(
-            F32
-        ) + lax.dynamic_index_in_dim(other, owner, axis, keepdims=False).astype(F32)
-
-    total = block(1)
-    for k in list(range(2, count // 2)) + [0]:
-        total = block(k) + ring_step(total.astype(BF16)).astype(F32)
-    return total
 
 
 def after(value, *others):
@@ -391,18 +347,22 @@
     part = norm1_gain.shape[0]
     dp_count = lax.axis_size("dp")
     dp_here = lax.axis_index("dp")
-    group_rows = rows * lax.axis_size("tensor")
     head_cols = qkv_weight.shape[2]
     offs = frame_offsets(rows)
     runs = sequence_runs(rows)
     tables = rotary_lanes()
 
+    attn_shard = jnp.concatenate([qkv_weight, out_weight.T[None]], axis=0)
+    attn_local = lax.all_gather(attn_shard, "dp", axis=1, tiled=True)
+    qkv_local, out_turned = attn_local[:3], attn_local[3]
+    gate_up_local = lax.all_gather(gate_up_weight, "dp", axis=1, tiled=True)
+    down_local = lax.all_gather(down_weight, "dp", axis=1, tiled=True)
+
+    x_rows = collect_rows(layer_input)
     packed = jnp.concatenate(
         [norm1_gain, norm1_bias, norm2_gain, norm2_bias, qkv_bias.reshape(-1)]
-    )[None]
-    for bit in bits_of("dp"):
-        packed = jnp.concatenate([packed, swap(packed, "dp", bit)], axis=0)
-    packed = jnp.take(packed, jnp.arange(dp_count) ^ dp_here, axis=0)
+    )
+    packed = lax.all_gather(packed, "dp", axis=0, tiled=False)
     gain_one, bias_one, gain_two, bias_two = (
         packed[:, k * part : (k + 1) * part].reshape(width).astype(F32) for k in range(4)
     )
@@ -410,25 +370,21 @@
         packed[:, 4 * part :].reshape(dp_count, 3, -1).transpose(1, 0, 2).reshape(3, head_cols)
     ).astype(F32)
 
-    qkv_local, qkv_seen = ring_gather(qkv_weight, 1)
-    out_local = lax.all_gather(after(out_weight, qkv_seen[-2]), "dp", axis=1, tiled=True)
-    gate_up_local = lax.all_gather(after(gate_up_weight, qkv_seen[-1]), "dp", axis=1, tiled=True)
-    down_turned, _ = ring_gather(after(down_weight.T, qkv_seen[-1]), 0)
-
     x_float = layer_input.astype(F32)
     hat_one, inv_one = layer_norm(x_float)
-    rows_one = collect_rows((hat_one * gain_one + bias_one).astype(BF16))
-    cot_rows = collect_rows(after(out_cotangent, rows_one))
+    rows_one = (layer_norm(x_rows.astype(F32))[0] * gain_one + bias_one).astype(BF16)
     pre = (
         jnp.einsum("rd,cdk->crk", rows_one, qkv_local, preferred_element_type=F32)
         + bias_local[:, None, :]
     )
     qkv_heads, context, lse = attend(offs, pre, tables, runs)
-    residual = x_float + spread_rows(
-        lambda at: jnp.dot(context[at], out_local, preferred_element_type=F32).astype(BF16),
-        context,
-        rows,
-    )
+    parts = part_slices(rows)
+    attn_terms = [
+        lax.dot_general(context[at], out_turned, NT, preferred_element_type=F32).astype(BF16)
+        for at in parts
+    ]
+    residual = x_float + spread_rows(attn_terms, rows)
+    cot_rows = collect_rows(after(out_cotangent, rows_one))
 
     hat_two, inv_two = layer_norm(residual)
     rows_two = collect_rows((hat_two * gain_two + bias_two).astype(BF16))
@@ -438,69 +394,68 @@
     silu_gate = gate_proj * sigmoid_gate
     activation = (silu_gate * up_proj).astype(BF16)
 
-    grad_down = lax.dot_general(cot_rows, activation, TN, preferred_element_type=F32)
-    share_down = ring_reduce(grad_down.astype(BF16), 0).T
-    grad_act = jnp.dot(cot_rows, down_turned, preferred_element_type=F32)
+    grad_down = lax.dot_general(
+        activation, cot_rows, TN, preferred_element_type=F32
+    ).astype(BF16)
+    share_down = lax.psum_scatter(grad_down, "dp", scatter_dimension=1, tiled=True)
+    share_down = share_down.astype(F32)
+    grad_act = lax.dot_general(
+        after(cot_rows, grad_down), down_local, NT, preferred_element_type=F32
+    )
     grad_gate = (
         grad_act * up_proj * sigmoid_gate * (1.0 + gate_proj * (1.0 - sigmoid_gate))
     ).astype(BF16)
     grad_up = (grad_act * silu_gate).astype(BF16)
-    grad_normed_two = spread_rows(
-        lambda at: (
+    back_terms = [
+        (
             lax.dot_general(grad_gate[at], gate_up_local[0], NT, preferred_element_type=F32)
             + lax.dot_general(grad_up[at], gate_up_local[1], NT, preferred_element_type=F32)
-        ).astype(BF16),
-        grad_gate,
-        rows,
-    )
-    grad_wgate = lax.dot_general(
-        rows_two, grad_gate, TN, preferred_element_type=F32
+        ).astype(BF16)
+        for at in parts
+    ]
+    grad_normed_two = spread_rows(back_terms, rows)
+    grad_gate_up = jnp.stack([grad_gate, grad_up])
+    grad_wgate_up = jnp.einsum(
+        "rd,crk->cdk",
+        after(rows_two, *back_terms),
+        grad_gate_up,
+        preferred_element_type=F32,
     ).astype(BF16)
-    grad_wup = lax.dot_general(rows_two, grad_up, TN, preferred_element_type=F32).astype(BF16)
-    share_gate = lax.psum_scatter(grad_wgate, "dp", scatter_dimension=0, tiled=True).astype(F32)
-    share_up = lax.psum_scatter(grad_wup, "dp", scatter_dimension=0, tiled=True).astype(F32)
-    grad_normed_two = after(grad_normed_two, grad_wgate, grad_wup)
+    share_gate_up = lax.psum_scatter(grad_wgate_up, "dp", scatter_dimension=1, tiled=True)
+    share_gate_up = share_gate_up.astype(F32)
+    grad_normed_two, _, mlp_act = lax.optimization_barrier(
+        (grad_normed_two, grad_wgate_up, activation)
+    )
     grad_resid = out_cotangent.astype(F32) + norm_back(
         grad_normed_two * gain_two, hat_two, inv_two
     )
 
-    resid_rows = collect_rows(grad_resid.astype(BF16))
-    late_act = after(activation, resid_rows)
-    layer_output = (
-        residual
-        + spread_rows(
-            lambda at: lax.dot_general(
-                late_act[at], down_turned, NT, preferred_element_type=F32
-            ).astype(BF16),
-            activation,
-            rows,
-        )
-    ).astype(BF16)
-    grad_context = lax.dot_general(
-        resid_rows, out_local, NT, preferred_element_type=F32
-    ).astype(BF16)
+    mlp_terms = jnp.dot(mlp_act, down_local, preferred_element_type=F32).astype(BF16)
+    resid_rows, mlp_terms = lax.optimization_barrier(
+        (collect_rows(grad_resid.astype(BF16)), mlp_terms)
+    )
+    grad_context = jnp.dot(resid_rows, out_turned, preferred_element_type=F32).astype(BF16)
     grad_pre, bias_sums = attend_back(offs, qkv_heads, context, grad_context, lse, tables, runs)
     grad_wqkv = jnp.einsum(
         "rd,crk->cdk", rows_one, grad_pre, preferred_element_type=F32
     ).astype(BF16)
-    share_qkv = ring_reduce(grad_wqkv, 1)
-    late_pre = after(grad_pre, grad_wqkv)
-    grad_normed_one = spread_rows(
-        lambda at: jnp.einsum(
+    grad_wout = lax.dot_general(
+        resid_rows, context, TN, preferred_element_type=F32
+    ).astype(BF16)
+    grad_wattn = jnp.concatenate([grad_wqkv, grad_wout[None]], axis=0)
+    share_attn = lax.psum_scatter(grad_wattn, "dp", scatter_dimension=1, tiled=True)
+    share_attn = share_attn.astype(F32)
+    late_pre = after(grad_pre, grad_wattn)
+    qkv_terms = [
+        jnp.einsum(
             "crk,cdk->rd", late_pre[:, at], qkv_local, preferred_element_type=F32
-        ).astype(BF16),
-        grad_pre,
-        rows,
-    )
-    grad_wout = lax.dot_general(context, resid_rows, TN, preferred_element_type=F32)
-    share_out = lax.psum_scatter(
-        grad_wout.astype(BF16), "dp", scatter_dimension=1, tiled=True
-    ).astype(F32)
+        ).astype(BF16)
+        for at in parts
+    ]
+    grad_normed_one = spread_rows(qkv_terms, rows)
     grad_input = grad_resid + norm_back(grad_normed_one * gain_one, hat_one, inv_one)
-
-    bias_total = total_over(jnp.sum(bias_sums, axis=0), "dp")
-    bias_part = qkv_bias.shape[1]
-    share_bias = lax.dynamic_slice_in_dim(bias_total, dp_here * bias_part, bias_part, axis=1)
+    layer_output = (residual + spread_rows([mlp_terms[at] for at in parts], rows)).astype(BF16)
+
     norm_sums = jnp.stack(
         [
             jnp.sum(grad_normed_one * hat_one, axis=0),
@@ -509,19 +464,25 @@
             jnp.sum(grad_normed_two, axis=0),
         ]
     )
-    norm_total = total_over(total_over(norm_sums, "tensor"), "dp")
+    norm_total = total_over(norm_sums, "tensor").reshape(-1)
+    bias_total = jnp.sum(bias_sums, axis=0).reshape(-1)
+    totals = total_over(jnp.concatenate([norm_total, bias_total]), "dp")
+    norm_total = totals[: 4 * width].reshape(4, width)
+    bias_total = totals[4 * width :].reshape(3, head_cols)
     share_norm = lax.dynamic_slice_in_dim(norm_total, dp_here * part, part, axis=1)
+    bias_part = qkv_bias.shape[1]
+    share_bias = lax.dynamic_slice_in_dim(bias_total, dp_here * bias_part, bias_part, axis=1)
     return (
         layer_output,
         grad_input,
         share_norm[0],
         share_norm[1],
-        share_qkv,
+        share_attn[:3],
         share_bias,
-        share_out,
+        share_attn[3].T,
         share_norm[2],
         share_norm[3],
-        jnp.stack([share_gate, share_up]),
+        share_gate_up,
         share_down,
     )
 
@@ -540,6 +501,7 @@
         P("tensor", "dp"),
         P(("dp", "tensor"), None),
     )
+
     return jax.shard_map(
         shards,
         mesh=mesh,

time: 836 us -> 731 us (0.87)
  local copies, waits for them, and re-layouts: 148 us -> 44 us
  blocking collectives: 0 us -> 38.8 us
  starting transfers between devices: 73.9 us -> 50.1 us
    ppermute x12 -> x0, waiting for transfers between devices: 120 us -> none  [ring_step(): lax.ppermute(value, 'dp', [(i, (i + 2) % count) for i in range(count)])]
    reduce_scatter x3, waiting for transfers between devices: 0.01 us -> 100 us  [the longest x1 100 us: shards(): lax.psum_scatter(grad_wgate_up, 'dp', scatter_dimension=1, tiled=True)]
    dynamic_slice x6 -> x1, local copies, waits for them, and re-layouts: 41.3 us -> 0.66 us  [shards(): lax.dynamic_slice_in_dim(bias_total, dp_here * bias_part, bias_part, axis=1)]
    unnamed x0 -> x1, blocking collectives: none -> 38.8 us
    unnamed x148 -> x125, local copies, waits for them, and re-layouts: 48.2 us -> 22.3 us
    ppermute x12 -> x0, starting transfers between devices: 23.9 us -> none  [ring_step(): lax.ppermute(value, 'dp', [(i, (i + 2) % count) for i in range(count)])]
    dynamic_update_slice x16 -> x0, local copies, waits for them, and re-layouts: 20.3 us -> none  [the longest x8 10.4 us: ring_gather(): lax.dynamic_update_slice_in_dim(full, swap(held, 'dp', 1), (owner ^ 1) *...]
    ppermute x53 -> x37, waiting for transfers between devices: 226 us -> 240 us  [swap(): lax.ppermute(value, axis, [(i, i ^ bit) for i in range(lax.axis_size(axis...]
  transfers between devices with their start and end apart: 70 -> 43, of which waited for: 28 -> 27; matrix products, arithmetic and copies ran while one was open for 34% -> 27% of each run, Pallas kernels for 5% -> 6%
where the time goes in v3:
time: 731 us; the launch traced here: 727 us
  waiting for transfers between devices  341 us (47%)
  matrix products  151 us (21%)
  starting transfers between devices  50.1 us (7%)
  other arithmetic  45.3 us (6%)
  local copies, waits for them, and re-layouts  44 us (6%)
  Pallas kernels  41.2 us (6%)
  blocking collectives  38.8 us (5%)
  between operations  16.2 us (2%)
    ppermute x37, waiting for transfers between devices, swap(): lax.ppermute(value, axis, [(i, i ^ bit) for i in range(lax.axis_size(axis...  240 us
    reduce_scatter x1, waiting for transfers between devices, shards(): lax.psum_scatter(grad_wgate_up, 'dp', scatter_dimension=1, tiled=True)  100 us
    ppermute x37, starting transfers between devices, swap(): lax.ppermute(value, axis, [(i, i ^ bit) for i in range(lax.axis_size(axis...  49.4 us
    unnamed x1, blocking collectives  38.8 us
    unnamed x125, local copies, waits for them, and re-layouts  22.3 us
    pallas_call x1, Pallas kernels, attend(): pl.pallas_call(functools.partial(attend_kernel, runs=runs), out_shape=(ja...  20.7 us
    pallas_call x1, Pallas kernels, attend_back(): pl.pallas_call(functools.partial(attend_back_kernel, runs=runs), out_shap...  20.4 us
    dot_general x1, matrix products, shards(): jnp.einsum('rd,crk->cdk', after(rows_two, *back_terms), grad_gate_up, pre...  17.5 us
  transfers between devices with their start and end apart: 43, of which 27 were waited for; matrix products, arithmetic and copies ran while one was open for 27% of the time, Pallas kernels for 6%

profile of v3, /device:TPU:0, one launch (start us, length us, event | category | flops | bytes accessed | tf_op | source)
XLA Modules:
  0.0 727.4 jit_solution(18186736529320185869)
XLA Ops:
  15.5 11.9 %collective-permute-done = bf16[128,2048]{1,0:T(8,128)(2,1)S(1)} collective-permute-done((bf16[128,2048]{1,0:T(8,128)(2,1)S(1)}, bf16[128,2048]{1,0:T(8,128)(2,1)S(1)}, u32[]{:S(2)}, u32[]{:S(2)}) %collective-permute-start) | collective-permute-done | bytes 524320 | tf_op jit(solution)/shard_map/ppermute | solution.py:58
  30.2 21.8 %collective-permute-done.1 = bf16[256,2048]{1,0:T(8,128)(2,1)S(1)} collective-permute-done((bf16[256,2048]{1,0:T(8,128)(2,1)S(1)}, bf16[256,2048]{1,0:T(8,128)(2,1)S(1)}, u32[]{:S(2)}, u32[]{:S(2)}) %collective-permute-start.1) | collective-permute-done | bytes 1048608 | tf_op jit(solution)/shard_map/ppermute | solution.py:58
  58.1 38.8 %all-reduce = bf16[9728]{0:T(1024)(128)(2,1)S(1)} all-reduce(bf16[9728]{0:T(1024)(128)(2,1)S(1)} %dynamic-update-slice), channel_id=2, replica_groups=mesh['dp'=8,'tensor'=4] {'dp'}, use_global_device_ids=true, to_apply=%add | all-reduce | flops 9728 | bytes 38912
  104.3 13.1 %collective-permute-done.3 = bf16[256,2048]{1,0:T(8,128)(2,1)} collective-permute-done((bf16[256,2048]{1,0:T(8,128)(2,1)}, bf16[256,2048]{1,0:T(8,128)(2,1)}, u32[]{:S(2)}, u32[]{:S(2)}) %collective-permute-start.3) | collective-permute-done | bytes 1048608 | tf_op jit(solution)/shard_map/ppermute | solution.py:58
  130.8 11.7 %add_bitcast_fusion.pre_ref = f32[3,1024,512]{2,1,0:T(8,128)} fusion(f32[3,512]{1,0:T(4,128)S(1)} %reshape.163, bf16[4,2048,512]{1,2,0:T(8,128)(2,1)} %all-gather.5.cloned.1.call-done, bf16[1024,2048]{1,0:T(8,128)(2,1)} %fusion.5), kind=kOutput, calls=%fused_computation.12 | convolution fusion | flops 6444023808 | bytes 18880512 | tf_op jit(solution)/shard_map/rd,cdk->crk/dot_general | solution.py:377
  142.5 20.7 %attend.1 = (bf16[3,2,512,512]{3,2,1,0:T(8,128)(2,1)}, bf16[1024,512]{1,0:T(8,128)(2,1)}, f32[2,512,512]{2,1,0:T(8,128)}) custom-call(s32[8]{0:T(128)} %stack.57.offs_ref, f32[3,1024,512]{2,1,0:T(8,128)} %add_bitcast_fusion.pre_ref, f32[512,128]{1,0:T(8,128)} %concatenate.78.keep_ref.refs_4_, f32[512,128]{1,0:T(8,128)} %concatenate.79.low_ref.refs_5_, ...), custom_call_target="tpu_custom_call" | custom-call | tf_op jit(solution)/shard_map/attend/pallas_call | solution.py:296
  173.9 18.7 %collective-permute-done.4 = bf16[256,2048]{1,0:T(8,128)(2,1)S(1)} collective-permute-done((bf16[256,2048]{1,0:T(8,128)(2,1)S(1)}, bf16[256,2048]{1,0:T(8,128)(2,1)S(1)}, u32[]{:S(2)}, u32[]{:S(2)}) %collective-permute-start.4) | collective-permute-done | bytes 1048608 | tf_op jit(solution)/shard_map/ppermute | solution.py:58
  198.2 9.0 %collective-permute-done.8 = bf16[128,2048]{1,0:T(8,128)(2,1)S(1)} collective-permute-done((bf16[128,2048]{1,0:T(8,128)(2,1)S(1)}, bf16[128,2048]{1,0:T(8,128)(2,1)S(1)}, u32[]{:S(2)}, u32[]{:S(2)}) %collective-permute-start.8) | collective-permute-done | bytes 524320 | tf_op jit(solution)/shard_map/ppermute | solution.py:58
  223.0 12.4 %collective-permute-done.9 = bf16[256,2048]{1,0:T(8,128)(2,1)S(1)} collective-permute-done((bf16[256,2048]{1,0:T(8,128)(2,1)S(1)}, bf16[256,2048]{1,0:T(8,128)(2,1)S(1)}, u32[]{:S(2)}, u32[]{:S(2)}) %collective-permute-start.9) | collective-permute-done | bytes 1048608 | tf_op jit(solution)/shard_map/ppermute | solution.py:58
  237.8 18.4 %collective-permute-done.11 = bf16[256,2048]{1,0:T(8,128)(2,1)S(1)} collective-permute-done((bf16[256,2048]{1,0:T(8,128)(2,1)S(1)}, bf16[256,2048]{1,0:T(8,128)(2,1)S(1)}, u32[]{:S(2)}, u32[]{:S(2)}) %collective-permute-start.11) | collective-permute-done | bytes 1048608 | tf_op jit(solution)/shard_map/ppermute | solution.py:58
  258.2 13.3 %collective-permute-done.13 = bf16[256,2048]{1,0:T(8,128)(2,1)S(1)} collective-permute-done((bf16[256,2048]{1,0:T(8,128)(2,1)S(1)}, bf16[256,2048]{1,0:T(8,128)(2,1)S(1)}, u32[]{:S(2)}, u32[]{:S(2)}) %collective-permute-start.13) | collective-permute-done | bytes 1048608 | tf_op jit(solution)/shard_map/ppermute | solution.py:58
  281.1 12.2 %fusion.16 = f32[1024,1408]{1,0:T(8,128)} fusion(bf16[1024,2048]{1,0:T(8,128)(2,1)} %constant_dynamic-update-slice_fusion.12, bf16[2,2048,1408]{2,1,0:T(8,128)(2,1)} %all-gather.7.cloned.1.call-done), kind=kOutput, calls=%fused_computation.29 | convolution fusion | flops 5905580032 | bytes 15728640 | tf_op jit(solution)/shard_map/dot_general | solution.py:391
  293.3 11.9 %multiply_convert_fusion.2 = (bf16[1024,1408]{1,0:T(8,128)(2,1)S(1)}, f32[1024,1408]{1,0:T(8,128)}) fusion(f32[1024,1408]{1,0:T(8,128)} %fusion.16, bf16[1024,2048]{1,0:T(8,128)(2,1)} %constant_dynamic-update-slice_fusion.12, bf16[2,2048,1408]{2,1,0:T(8,128)(2,1)S(1)} %copy-done.31), kind=kOutput, calls=%fused_computation.20 | convolution fusion | flops 5914230784 | bytes 24379392 | tf_op jit(solution)/shard_map/dot_general | solution.py:392
  315.1 14.1 %multiply_convert_fusion = (bf16[1024,1408]{1,0:T(8,128)(2,1)S(1)}, bf16[1024,1408]{1,0:T(8,128)(2,1)S(1)}) fusion(f32[1024,1408]{1,0:T(8,128)} %fusion.16, f32[1024,1408]{1,0:T(8,128)} %get-tuple-element.117, bf16[1024,2048]{1,0:T(8,128)(2,1)} %copy-done.20, bf16[1408,2048]{1,0:T(8,128)(2,1)} %all-gather.9.cloned.1.call-done), kind=kOutput, calls=%fused_computation.18 | convolution fusion | flops 5924323328 | bytes 27262976 | tf_op jit(solution)/shard_map/dot_general | solution.py:402
  329.3 9.8 %fusion.15 = f32[512,2048]{1,0:T(8,128)} fusion(bf16[2,2048,1408]{2,1,0:T(8,128)(2,1)} %all-gather.7.cloned.1.call-done, bf16[1024,1408]{1,0:T(8,128)(2,1)S(1)} %get-tuple-element.82), kind=kOutput, calls=%fused_computation.28 | convolution fusion | flops 2952790016 | bytes 11403264 | tf_op jit(solution)/shard_map/dot_general | solution.py:411
  372.4 14.1 %collective-permute-done.18 = bf16[256,2048]{1,0:T(8,128)(2,1)} collective-permute-done((bf16[256,2048]{1,0:T(8,128)(2,1)}, bf16[256,2048]{1,0:T(8,128)(2,1)}, u32[]{:S(2)}, u32[]{:S(2)}) %collective-permute-start.18) | collective-permute-done | bytes 1048608 | tf_op jit(solution)/shard_map/ppermute | solution.py:58
  391.0 17.5 %convert_bitcast_fusion = bf16[2,2048,1408]{1,2,0:T(8,128)(2,1)} fusion(bf16[1,1024,1408]{2,1,0:T(8,128)(2,1)S(1)} %bitcast.131, bf16[1,1024,1408]{2,1,0:T(8,128)(2,1)S(1)} %bitcast.132, bf16[1024,2048]{1,0:T(8,128)(2,1)} %constant_dynamic-update-slice_fusion.12), kind=kOutput, calls=%fused_computation | convolution fusion | flops 11819810816 | bytes 21495808 | tf_op jit(solution)/shard_map/rd,crk->cdk/dot_general | solution.py:418
  434.0 12.4 %collective-permute-done.21 = bf16[256,2048]{1,0:T(8,128)(2,1)S(1)} collective-permute-done((bf16[256,2048]{1,0:T(8,128)(2,1)S(1)}, bf16[256,2048]{1,0:T(8,128)(2,1)S(1)}, u32[]{:S(2)}, u32[]{:S(2)}) %collective-permute-start.21) | collective-permute-done | bytes 1048608 | tf_op jit(solution)/shard_map/ppermute | solution.py:58
  457.4 20.4 %attend_back.1 = (bf16[3,1024,512]{2,1,0:T(8,128)(2,1)}, f32[2,3,512]{2,1,0:T(4,128)}) custom-call(s32[8]{0:T(128)} %stack.57.offs_ref, bf16[3,2,512,512]{3,2,1,0:T(8,128)(2,1)} %get-tuple-element.31.refs_0_, bf16[1024,512]{1,0:T(8,128)(2,1)} %get-tuple-element.24.refs_1_, bf16[1024,512]{1,0:T(8,128)(2,1)} %fusion.46.refs_2_, ...), custom_call_target="tpu_custom_call" | custom-call | tf_op jit(solution)/shard_map/attend_back/pallas_call | solution.py:317
  482.6 9.0 %convert_bitcast_fusion.1 = bf16[3,2048,512]{1,2,0:T(8,128)(2,1)} fusion(bf16[3,1024,512]{2,1,0:T(8,128)(2,1)S(1)} %copy-done.32, bf16[1024,2048]{1,0:T(8,128)(2,1)S(1)} %copy-done.6), kind=kOutput, calls=%fused_computation.11 | convolution fusion | flops 6445596672 | bytes 13631488 | tf_op jit(solution)/shard_map/rd,crk->cdk/dot_general | solution.py:439
  522.7 11.3 %collective-permute-done.28 = bf16[256,2048]{1,0:T(8,128)(2,1)} collective-permute-done((bf16[256,2048]{1,0:T(8,128)(2,1)}, bf16[256,2048]{1,0:T(8,128)(2,1)}, u32[]{:S(2)}, u32[]{:S(2)}) %collective-permute-start.28) | collective-permute-done | bytes 1048608 | tf_op jit(solution)/shard_map/ppermute | solution.py:58
  554.1 11.6 %collective-permute-done.26 = bf16[256,2048]{1,0:T(8,128)(2,1)S(1)} collective-permute-done((bf16[256,2048]{1,0:T(8,128)(2,1)S(1)}, bf16[256,2048]{1,0:T(8,128)(2,1)S(1)}, u32[]{:S(2)}, u32[]{:S(2)}) %collective-permute-start.26) | collective-permute-done | bytes 1048608 | tf_op jit(solution)/shard_map/ppermute | solution.py:58
  590.5 15.8 %collective-permute-start.36 = (f32[9728]{0:T(1024)S(1)}, f32[9728]{0:T(1024)S(1)}, u32[]{:S(2)}, u32[]{:S(2)}) collective-permute-start(f32[9728]{0:T(1024)S(1)} %add.242), channel_id=1, source_target_pairs={{0,16},{4,20},{8,24},{12,28},{16,0},{20,4},{24,8},{28,12},{1,17},{... | collective-permute-start | bytes 116744 | tf_op jit(solution)/shard_map/ppermute | solution.py:58
  617.4 100.0 %reduce-scatter.6.cloned.1.call-done = bf16[2,256,1408]{1,2,0:T(8,128)(2,1)} async-done(((bf16[2,2048,1408]{1,2,0:T(8,128)(2,1)}), bf16[2,256,1408]{1,2,0:T(8,128)(2,1)}) %reduce-scatter.6.cloned.1.call-update) | async-done | bytes 1441808 | tf_op jit(solution)/shard_map/reduce_scatter | solution.py:424
  (325 shorter events, 261.1 us)
Async XLA Ops:
  7.2 123.6 %all-gather.5.cloned.1.call-start = ((), (), s32[]{:S(2)}) async-start(), calls=%async_computation.3 | async-start | bytes 9437184 | tf_op jit(solution)/shard_map/all_gather | solution.py:356
  10.8 270.4 %all-gather.7.cloned.1.call-start = ((), (), s32[]{:S(2)}) async-start(), calls=%async_computation.4 | async-start | bytes 12976128 | tf_op jit(solution)/shard_map/all_gather | solution.py:358
  11.6 303.5 %all-gather.9.cloned.1.call-start = ((), (), s32[]{:S(2)}) async-start(), calls=%async_computation.5 | async-start | bytes 6488064 | tf_op jit(solution)/shard_map/all_gather | solution.py:359
  27.5 24.5 %collective-permute-start.1 = (bf16[256,2048]{1,0:T(8,128)(2,1)S(1)}, bf16[256,2048]{1,0:T(8,128)(2,1)S(1)}, u32[]{:S(2)}, u32[]{:S(2)}) collective-permute-start(bf16[256,2048]{1,0:T(8,128)(2,1)S(1)} %pad_maximum_fusion.4), channel_id=1, source_target_pairs={{0,2},{1,3},{2,0},{3,1},{4,6},{5,7},{6,4},{7,5},{8,10},{9,11},{10,... | collective-permute-start | bytes 3145736 | tf_op jit(solution)/shard_map/ppermute | solution.py:58
  54.0 43.1 %collective-permute-start.2 = (bf16[128,2048]{1,0:T(8,128)(2,1)S(1)}, bf16[128,2048]{1,0:T(8,128)(2,1)S(1)}, u32[]{:S(2)}, u32[]{:S(2)}) collective-permute-start(bf16[128,2048]{1,0:T(8,128)(2,1)S(1)} %get-tuple-element.101), channel_id=1, source_target_pairs={{0,2},{1,3},{2,0},{3,1},{4,6},{5,7},{6,4},{7,5},{8,10},{9,11},{10,... | collective-permute-start | bytes 1572872 | tf_op jit(solution)/shard_map/ppermute | solution.py:58
  55.5 555.6 %reduce-scatter.8.cloned.1.call-start = ((), (), s32[]{:S(2)}) async-start(), calls=%async_computation.8 | async-start | bytes 6488064 | tf_op jit(solution)/shard_map/reduce_scatter | solution.py:400
  166.5 26.1 %collective-permute-start.4 = (bf16[256,2048]{1,0:T(8,128)(2,1)S(1)}, bf16[256,2048]{1,0:T(8,128)(2,1)S(1)}, u32[]{:S(2)}, u32[]{:S(2)}) collective-permute-start(bf16[256,2048]{1,0:T(8,128)(2,1)S(1)} %slice.286), channel_id=1, source_target_pairs={{0,2},{1,3},{2,0},{3,1},{4,6},{5,7},{6,4},{7,5},{8,10},{9,11},{10,... | collective-permute-start | bytes 3145736 | tf_op jit(solution)/shard_map/ppermute | solution.py:58
  169.8 26.1 %collective-permute-start.6 = (bf16[256,2048]{1,0:T(8,128)(2,1)S(1)}, bf16[256,2048]{1,0:T(8,128)(2,1)S(1)}, u32[]{:S(2)}, u32[]{:S(2)}) collective-permute-start(bf16[256,2048]{1,0:T(8,128)(2,1)S(1)} %slice.290), channel_id=1, source_target_pairs={{0,1},{1,0},{2,3},{3,2},{4,5},{5,4},{6,7},{7,6},{8,9},{9,8},{10,11... | collective-permute-start | bytes 3145736 | tf_op jit(solution)/shard_map/ppermute | solution.py:58
  170.7 36.5 %collective-permute-start.8 = (bf16[128,2048]{1,0:T(8,128)(2,1)S(1)}, bf16[128,2048]{1,0:T(8,128)(2,1)S(1)}, u32[]{:S(2)}, u32[]{:S(2)}) collective-permute-start(bf16[128,2048]{1,0:T(8,128)(2,1)S(1)} %get-tuple-element.97), channel_id=1, source_target_pairs={{0,1},{1,0},{2,3},{3,2},{4,5},{5,4},{6,7},{7,6},{8,9},{9,8},{10,11... | collective-permute-start | bytes 1572872 | tf_op jit(solution)/shard_map/ppermute | solution.py:58
  172.2 48.8 %collective-permute-start.10 = (bf16[128,2048]{1,0:T(8,128)(2,1)S(1)}, bf16[128,2048]{1,0:T(8,128)(2,1)S(1)}, u32[]{:S(2)}, u32[]{:S(2)}) collective-permute-start(bf16[128,2048]{1,0:T(8,128)(2,1)S(1)} %get-tuple-element.95), channel_id=1, source_target_pairs={{0,2},{1,3},{2,0},{3,1},{4,6},{5,7},{6,4},{7,5},{8,10},{9,11},{10,... | collective-permute-start | bytes 1572872 | tf_op jit(solution)/shard_map/ppermute | solution.py:58
  193.0 24.4 %collective-permute-start.5 = (bf16[128,2048]{1,0:T(8,128)(2,1)S(1)}, bf16[128,2048]{1,0:T(8,128)(2,1)S(1)}, u32[]{:S(2)}, u32[]{:S(2)}) collective-permute-start(bf16[128,2048]{1,0:T(8,128)(2,1)S(1)} %slice.288), channel_id=1, source_target_pairs={{0,1},{1,0},{2,3},{3,2},{4,5},{5,4},{6,7},{7,6},{8,9},{9,8},{10,11... | collective-permute-start | bytes 1572872 | tf_op jit(solution)/shard_map/ppermute | solution.py:58
  207.3 28.1 %collective-permute-start.9 = (bf16[256,2048]{1,0:T(8,128)(2,1)S(1)}, bf16[256,2048]{1,0:T(8,128)(2,1)S(1)}, u32[]{:S(2)}, u32[]{:S(2)}) collective-permute-start(bf16[256,2048]{1,0:T(8,128)(2,1)S(1)} %pad_maximum_fusion.6), channel_id=1, source_target_pairs={{0,2},{1,3},{2,0},{3,1},{4,6},{5,7},{6,4},{7,5},{8,10},{9,11},{10,... | collective-permute-start | bytes 3145736 | tf_op jit(solution)/shard_map/ppermute | solution.py:58
  221.1 35.1 %collective-permute-start.11 = (bf16[256,2048]{1,0:T(8,128)(2,1)S(1)}, bf16[256,2048]{1,0:T(8,128)(2,1)S(1)}, u32[]{:S(2)}, u32[]{:S(2)}) collective-permute-start(bf16[256,2048]{1,0:T(8,128)(2,1)S(1)} %pad_maximum_fusion.7), channel_id=1, source_target_pairs={{0,1},{1,0},{2,3},{3,2},{4,5},{5,4},{6,7},{7,6},{8,9},{9,8},{10,11... | collective-permute-start | bytes 3145736 | tf_op jit(solution)/shard_map/ppermute | solution.py:58
  237.4 34.1 %collective-permute-start.13 = (bf16[256,2048]{1,0:T(8,128)(2,1)S(1)}, bf16[256,2048]{1,0:T(8,128)(2,1)S(1)}, u32[]{:S(2)}, u32[]{:S(2)}) collective-permute-start(bf16[256,2048]{1,0:T(8,128)(2,1)S(1)} %pad_maximum_fusion.8), channel_id=1, source_target_pairs={{0,2},{1,3},{2,0},{3,1},{4,6},{5,7},{6,4},{7,5},{8,10},{9,11},{10,... | collective-permute-start | bytes 3145736 | tf_op jit(solution)/shard_map/ppermute | solution.py:58
  360.2 26.3 %collective-permute-start.18 = (bf16[256,2048]{1,0:T(8,128)(2,1)}, bf16[256,2048]{1,0:T(8,128)(2,1)}, u32[]{:S(2)}, u32[]{:S(2)}) collective-permute-start(bf16[256,2048]{1,0:T(8,128)(2,1)} %slice.308), channel_id=1, source_target_pairs={{0,1},{1,0},{2,3},{3,2},{4,5},{5,4},{6,7},{7,6},{8,9},{9,8},{10,11... | collective-permute-start | bytes 3145736 | tf_op jit(solution)/shard_map/ppermute | solution.py:58
  360.5 252.9 %reduce-scatter.4.cloned.1.call-start = ((), (), s32[]{:S(2)}) async-start(), calls=%async_computation.6 | async-start | bytes 9437184 | tf_op jit(solution)/shard_map/reduce_scatter | solution.py:446
  371.9 36.5 %collective-permute-start.17 = (bf16[128,2048]{1,0:T(8,128)(2,1)}, bf16[128,2048]{1,0:T(8,128)(2,1)}, u32[]{:S(2)}, u32[]{:S(2)}) collective-permute-start(bf16[128,2048]{1,0:T(8,128)(2,1)} %slice.304), channel_id=1, source_target_pairs={{0,1},{1,0},{2,3},{3,2},{4,5},{5,4},{6,7},{7,6},{8,9},{9,8},{10,11... | collective-permute-start | bytes 1572872 | tf_op jit(solution)/shard_map/ppermute | solution.py:58
  498.4 219.0 %reduce-scatter.6.cloned.1.call-start = ((), (), s32[]{:S(2)}) async-start(), calls=%async_computation.7 | async-start | bytes 12976128 | tf_op jit(solution)/shard_map/reduce_scatter | solution.py:424
  507.6 26.3 %collective-permute-start.28 = (bf16[256,2048]{1,0:T(8,128)(2,1)}, bf16[256,2048]{1,0:T(8,128)(2,1)}, u32[]{:S(2)}, u32[]{:S(2)}) collective-permute-start(bf16[256,2048]{1,0:T(8,128)(2,1)} %slice.319), channel_id=1, source_target_pairs={{0,2},{1,3},{2,0},{3,1},{4,6},{5,7},{6,4},{7,5},{8,10},{9,11},{10,... | collective-permute-start | bytes 3145736 | tf_op jit(solution)/shard_map/ppermute | solution.py:58
  517.0 26.2 %collective-permute-start.30 = (bf16[256,2048]{1,0:T(8,128)(2,1)}, bf16[256,2048]{1,0:T(8,128)(2,1)S(1)}, u32[]{:S(2)}, u32[]{:S(2)}) collective-permute-start(bf16[256,2048]{1,0:T(8,128)(2,1)} %slice.323), channel_id=1, source_target_pairs={{0,1},{1,0},{2,3},{3,2},{4,5},{5,4},{6,7},{7,6},{8,9},{9,8},{10,11... | collective-permute-start | bytes 3145736 | tf_op jit(solution)/shard_map/ppermute | solution.py:58
  519.2 34.9 %collective-permute-start.24 = (bf16[256,2048]{1,0:T(8,128)(2,1)S(1)}, bf16[256,2048]{1,0:T(8,128)(2,1)S(1)}, u32[]{:S(2)}, u32[]{:S(2)}) collective-permute-start(bf16[256,2048]{1,0:T(8,128)(2,1)S(1)} %get-tuple-element.85), channel_id=1, source_target_pairs={{0,2},{1,3},{2,0},{3,1},{4,6},{5,7},{6,4},{7,5},{8,10},{9,11},{10,... | collective-permute-start | bytes 3145736 | tf_op jit(solution)/shard_map/ppermute | solution.py:58
  520.9 44.8 %collective-permute-start.26 = (bf16[256,2048]{1,0:T(8,128)(2,1)S(1)}, bf16[256,2048]{1,0:T(8,128)(2,1)S(1)}, u32[]{:S(2)}, u32[]{:S(2)}) collective-permute-start(bf16[256,2048]{1,0:T(8,128)(2,1)S(1)} %get-tuple-element.86), channel_id=1, source_target_pairs={{0,1},{1,0},{2,3},{3,2},{4,5},{5,4},{6,7},{7,6},{8,9},{9,8},{10,11... | collective-permute-start | bytes 3145736 | tf_op jit(solution)/shard_map/ppermute | solution.py:58
  535.6 37.7 %collective-permute-start.29 = (bf16[128,2048]{1,0:T(8,128)(2,1)S(1)}, bf16[128,2048]{1,0:T(8,128)(2,1)S(1)}, u32[]{:S(2)}, u32[]{:S(2)}) collective-permute-start(bf16[128,2048]{1,0:T(8,128)(2,1)S(1)} %slice.321), channel_id=1, source_target_pairs={{0,1},{1,0},{2,3},{3,2},{4,5},{5,4},{6,7},{7,6},{8,9},{9,8},{10,11... | collective-permute-start | bytes 1572872 | tf_op jit(solution)/shard_map/ppermute | solution.py:58
  543.7 29.8 %collective-permute-start.31 = (bf16[128,2048]{1,0:T(8,128)(2,1)S(1)}, bf16[128,2048]{1,0:T(8,128)(2,1)S(1)}, u32[]{:S(2)}, u32[]{:S(2)}) collective-permute-start(bf16[128,2048]{1,0:T(8,128)(2,1)S(1)} %slice.325), channel_id=1, source_target_pairs={{0,2},{1,3},{2,0},{3,1},{4,6},{5,7},{6,4},{7,5},{8,10},{9,11},{10,... | collective-permute-start | bytes 1572872 | tf_op jit(solution)/shard_map/ppermute | solution.py:58
  (66 other events, 1102.6 us)
Sparse Core Ops, SparseCore 0:
  10.9 85.7 all-gather.4
  98.3 106.2 all-gather.6
  206.2 59.0 all-gather.8
  360.7 66.2 reduce-scatter.7
  498.5 98.1 reduce-scatter.3
  598.8 118.5 reduce-scatter.5

commit v4 on v3

--- a/solution.py
+++ b/solution.py
@@ -77,24 +77,17 @@
     ]
 
 
+def together(values):
+    return list(lax.optimization_barrier(tuple(values)))
+
+
 def collect_rows(block):
-    parts = []
-    for lo, hi, order in part_plan(block.shape[0]):
-        held = block[lo:hi]
-        for bit in order:
-            held = jnp.concatenate([held, swap(held, "tensor", bit)], axis=0)
-        parts.append(held)
-    return jnp.concatenate(parts, axis=0)
-
-
-def spread_part(terms, order):
-    held = terms
-    for bit in order[::-1]:
-        half = held.shape[0] // 2
-        got = swap(held[half:], "tensor", bit)
-        total = held[:half].astype(F32) + got.astype(F32)
-        held = total if bit == order[0] else total.astype(BF16)
-    return held
+    plan = part_plan(block.shape[0])
+    held = [block[lo:hi] for lo, hi, _ in plan]
+    for j in range(len(plan)):
+        got = [swap(h, "tensor", order[j]) for h, (_, _, order) in zip(held, plan)]
+        held = together(jnp.concatenate([h, g], axis=0) for h, g in zip(held, got))
+    return jnp.concatenate(held, axis=0)
 
 
 def part_slices(rows):
@@ -103,9 +96,17 @@
 
 
 def spread_rows(terms, rows):
-    return jnp.concatenate(
-        [spread_part(t, order) for t, (_, _, order) in zip(terms, part_plan(rows))], axis=0
-    )
+    plan = part_plan(rows)
+    held = list(terms)
+    for j in reversed(range(len(plan))):
+        totals = []
+        for h, (_, _, order) in zip(held, plan):
+            half = h.shape[0] // 2
+            got = swap(h[half:], "tensor", order[j])
+            total = h[:half].astype(F32) + got.astype(F32)
+            totals.append(total.astype(BF16) if j else total)
+        held = together(totals)
+    return jnp.concatenate(held, axis=0)
 
 
 def frame_pieces(rows):
@@ -359,10 +360,11 @@
     down_local = lax.all_gather(down_weight, "dp", axis=1, tiled=True)
 
     x_rows = collect_rows(layer_input)
+    cot_rows = collect_rows(after(out_cotangent, x_rows))
     packed = jnp.concatenate(
         [norm1_gain, norm1_bias, norm2_gain, norm2_bias, qkv_bias.reshape(-1)]
     )
-    packed = lax.all_gather(packed, "dp", axis=0, tiled=False)
+    packed = lax.all_gather(after(packed, x_rows), "dp", axis=0, tiled=False)
     gain_one, bias_one, gain_two, bias_two = (
         packed[:, k * part : (k + 1) * part].reshape(width).astype(F32) for k in range(4)
     )
@@ -377,14 +379,13 @@
         jnp.einsum("rd,cdk->crk", rows_one, qkv_local, preferred_element_type=F32)
         + bias_local[:, None, :]
     )
-    qkv_heads, context, lse = attend(offs, pre, tables, runs)
+    qkv_heads, context, lse = attend(offs, after(pre, cot_rows), tables, runs)
     parts = part_slices(rows)
     attn_terms = [
         lax.dot_general(context[at], out_turned, NT, preferred_element_type=F32).astype(BF16)
         for at in parts
     ]
     residual = x_float + spread_rows(attn_terms, rows)
-    cot_rows = collect_rows(after(out_cotangent, rows_one))
 
     hat_two, inv_two = layer_norm(residual)
     rows_two = collect_rows((hat_two * gain_two + bias_two).astype(BF16))
@@ -445,7 +446,8 @@
     grad_wattn = jnp.concatenate([grad_wqkv, grad_wout[None]], axis=0)
     share_attn = lax.psum_scatter(grad_wattn, "dp", scatter_dimension=1, tiled=True)
     share_attn = share_attn.astype(F32)
-    late_pre = after(grad_pre, grad_wattn)
+    layer_output = (residual + spread_rows([mlp_terms[at] for at in parts], rows)).astype(BF16)
+    late_pre, layer_output = lax.optimization_barrier((grad_pre, layer_output, grad_wattn))[:2]
     qkv_terms = [
         jnp.einsum(
             "crk,cdk->rd", late_pre[:, at], qkv_local, preferred_element_type=F32
@@ -454,7 +456,6 @@
     ]
     grad_normed_one = spread_rows(qkv_terms, rows)
     grad_input = grad_resid + norm_back(grad_normed_one * gain_one, hat_one, inv_one)
-    layer_output = (residual + spread_rows([mlp_terms[at] for at in parts], rows)).astype(BF16)
 
     norm_sums = jnp.stack(
         [

time: 731 us -> 694 us (0.949)
  starting transfers between devices: 50.1 us -> 32.9 us
  waiting for transfers between devices: 341 us -> 325 us
  local copies, waits for them, and re-layouts: 44 us -> 36.1 us
    ppermute x37, starting transfers between devices: 49.4 us -> 32.6 us  [swap(): lax.ppermute(value, axis, [(i, i ^ bit) for i in range(lax.axis_size(axis...]
    ppermute x37, waiting for transfers between devices: 240 us -> 226 us  [swap(): lax.ppermute(value, axis, [(i, i ^ bit) for i in range(lax.axis_size(axis...]
    unnamed x125 -> x119, local copies, waits for them, and re-layouts: 22.3 us -> 17.7 us
  transfers between devices with their start and end apart: 43 -> 43, of which waited for: 27 -> 29; matrix products, arithmetic and copies ran while one was open for 27% -> 28% of each run, Pallas kernels for 6% -> 6%
where the time goes in v4:
time: 694 us; the launch traced here: 689 us
  waiting for transfers between devices  325 us (47%)
  matrix products  149 us (21%)
  other arithmetic  48.8 us (7%)
  Pallas kernels  41.6 us (6%)
  blocking collectives  38.2 us (6%)
  local copies, waits for them, and re-layouts  36.1 us (5%)
  starting transfers between devices  32.9 us (5%)
  between operations  16.3 us (2%)
    ppermute x37, waiting for transfers between devices, swap(): lax.ppermute(value, axis, [(i, i ^ bit) for i in range(lax.axis_size(axis...  226 us
    reduce_scatter x1, waiting for transfers between devices, shards(): lax.psum_scatter(grad_wgate_up, 'dp', scatter_dimension=1, tiled=True)  98 us
    unnamed x1, blocking collectives  38.2 us
    ppermute x37, starting transfers between devices, swap(): lax.ppermute(value, axis, [(i, i ^ bit) for i in range(lax.axis_size(axis...  32.6 us
    pallas_call x1, Pallas kernels, attend(): pl.pallas_call(functools.partial(attend_kernel, runs=runs), out_shape=(ja...  21.1 us
    pallas_call x1, Pallas kernels, attend_back(): pl.pallas_call(functools.partial(attend_back_kernel, runs=runs), out_shap...  20.4 us
    dot_general x1, matrix products, shards(): jnp.einsum('rd,crk->cdk', after(rows_two, *back_terms), grad_gate_up, pre...  17.8 us
    unnamed x119, local copies, waits for them, and re-layouts  17.7 us
  transfers between devices with their start and end apart: 43, of which 29 were waited for; matrix products, arithmetic and copies ran while one was open for 28% of the time, Pallas kernels for 6%

profile of v4, /device:TPU:0, one launch (start us, length us, event | category | flops | bytes accessed | tf_op | source)
XLA Modules:
  0.0 688.6 jit_solution(6231780587881155978)
XLA Ops:
  16.3 10.4 %collective-permute-done.1 = bf16[128,2048]{1,0:T(8,128)(2,1)S(1)} collective-permute-done((bf16[128,2048]{1,0:T(8,128)(2,1)S(1)}, bf16[128,2048]{1,0:T(8,128)(2,1)S(1)}, u32[]{:S(2)}, u32[]{:S(2)}) %collective-permute-start.1) | collective-permute-done | bytes 524320 | tf_op jit(solution)/shard_map/ppermute | solution.py:58
  33.0 19.3 %collective-permute-done.3 = bf16[256,2048]{1,0:T(8,128)(2,1)} collective-permute-done((bf16[256,2048]{1,0:T(8,128)(2,1)S(1)}, bf16[256,2048]{1,0:T(8,128)(2,1)}, u32[]{:S(2)}, u32[]{:S(2)}) %collective-permute-start.3) | collective-permute-done | bytes 1048608 | tf_op jit(solution)/shard_map/ppermute | solution.py:58
  66.0 38.2 %all-reduce = bf16[9728]{0:T(1024)(128)(2,1)S(1)} all-reduce(bf16[9728]{0:T(1024)(128)(2,1)S(1)} %dynamic-update-slice), channel_id=2, replica_groups=mesh['dp'=8,'tensor'=4] {'dp'}, use_global_device_ids=true, to_apply=%add | all-reduce | flops 9728 | bytes 38912
  113.1 17.7 %collective-permute-done.7 = bf16[256,2048]{1,0:T(8,128)(2,1)S(1)} collective-permute-done((bf16[256,2048]{1,0:T(8,128)(2,1)S(1)}, bf16[256,2048]{1,0:T(8,128)(2,1)S(1)}, u32[]{:S(2)}, u32[]{:S(2)}) %collective-permute-start.7) | collective-permute-done | bytes 1048608 | tf_op jit(solution)/shard_map/ppermute | solution.py:58
  138.0 12.3 %add_bitcast_fusion.pre_ref = f32[3,1024,512]{2,1,0:T(8,128)} fusion(f32[3,512]{1,0:T(4,128)S(1)} %reshape.163, bf16[4,2048,512]{1,2,0:T(8,128)(2,1)} %all-gather.5.cloned.1.call-done, bf16[1024,2048]{1,0:T(8,128)(2,1)} %constant_dynamic-update-slice_fusion, f32[2048]{0:T(1024)S(1)} %bitcast.120, f32[2048]{0:T(1024)S(1)} %bitcast.114, ...), kind=kOutput, calls=%fused_computation.12 | convolution fusion | flops 6456606720 | bytes 18905088 | tf_op jit(solution)/shard_map/rd,cdk->crk/dot_general | solution.py:379
  150.3 21.1 %attend.1 = (bf16[3,2,512,512]{3,2,1,0:T(8,128)(2,1)}, bf16[1024,512]{1,0:T(8,128)(2,1)}, f32[2,512,512]{2,1,0:T(8,128)}) custom-call(s32[8]{0:T(128)} %stack.57.offs_ref, f32[3,1024,512]{2,1,0:T(8,128)} %add_bitcast_fusion.pre_ref, f32[512,128]{1,0:T(8,128)} %concatenate.105.keep_ref.refs_4_, f32[512,128]{1,0:T(8,128)} %concatenate.106.low_ref.refs_5_, ...), custom_call_target="tpu_custom_call" | custom-call | tf_op jit(solution)/shard_map/attend/pallas_call | solution.py:297
  179.8 19.2 %collective-permute-done.9 = bf16[256,2048]{1,0:T(8,128)(2,1)S(1)} collective-permute-done((bf16[256,2048]{1,0:T(8,128)(2,1)S(1)}, bf16[256,2048]{1,0:T(8,128)(2,1)S(1)}, u32[]{:S(2)}, u32[]{:S(2)}) %collective-permute-start.9) | collective-permute-done | bytes 1048608 | tf_op jit(solution)/shard_map/ppermute | solution.py:58
  205.2 10.4 %collective-permute-done.11 = bf16[128,2048]{1,0:T(8,128)(2,1)S(1)} collective-permute-done((bf16[128,2048]{1,0:T(8,128)(2,1)S(1)}, bf16[128,2048]{1,0:T(8,128)(2,1)S(1)}, u32[]{:S(2)}, u32[]{:S(2)}) %collective-permute-start.11) | collective-permute-done | bytes 524320 | tf_op jit(solution)/shard_map/ppermute | solution.py:58
  220.7 9.1 %collective-permute-done.13 = bf16[128,2048]{1,0:T(8,128)(2,1)} collective-permute-done((bf16[128,2048]{1,0:T(8,128)(2,1)S(1)}, bf16[128,2048]{1,0:T(8,128)(2,1)}, u32[]{:S(2)}, u32[]{:S(2)}) %collective-permute-start.13) | collective-permute-done | bytes 524320 | tf_op jit(solution)/shard_map/ppermute | solution.py:58
  233.2 19.8 %collective-permute-done.15 = bf16[256,2048]{1,0:T(8,128)(2,1)S(1)} collective-permute-done((bf16[256,2048]{1,0:T(8,128)(2,1)S(1)}, bf16[256,2048]{1,0:T(8,128)(2,1)S(1)}, u32[]{:S(2)}, u32[]{:S(2)}) %collective-permute-start.15) | collective-permute-done | bytes 1048608 | tf_op jit(solution)/shard_map/ppermute | solution.py:58
  256.7 10.8 %fusion.16 = f32[1024,1408]{1,0:T(8,128)S(1)} fusion(bf16[1024,2048]{1,0:T(8,128)(2,1)} %constant_dynamic-update-slice_fusion.4, bf16[2,2048,1408]{2,1,0:T(8,128)(2,1)} %all-gather.7.cloned.1.call-done), kind=kOutput, calls=%fused_computation.29 | convolution fusion | flops 5905580032 | bytes 15728640 | tf_op jit(solution)/shard_map/dot_general | solution.py:392
  267.5 11.6 %multiply_convert_fusion.2 = (bf16[1024,1408]{1,0:T(8,128)(2,1)S(1)}, f32[1024,1408]{1,0:T(8,128)}) fusion(f32[1024,1408]{1,0:T(8,128)S(1)} %fusion.16, bf16[1024,2048]{1,0:T(8,128)(2,1)} %constant_dynamic-update-slice_fusion.4, bf16[2,2048,1408]{2,1,0:T(8,128)(2,1)S(1)} %copy-done.31), kind=kOutput, calls=%fused_computation.20 | convolution fusion | flops 5914230784 | bytes 24379392 | tf_op jit(solution)/shard_map/dot_general | solution.py:393
  280.7 10.6 %convolution_convert_fusion = bf16[1408,2048]{1,0:T(8,128)(2,1)} fusion(bf16[1024,1408]{1,0:T(8,128)(2,1)S(1)} %get-tuple-element.91, bf16[1024,2048]{1,0:T(8,128)(2,1)} %constant_dynamic-update-slice_fusion.2), kind=kOutput, calls=%fused_computation.10 | convolution fusion | flops 5908463616 | bytes 12845056 | tf_op jit(solution)/shard_map/dot_general | solution.py:398
  291.3 14.3 %multiply_convert_fusion = (bf16[1024,1408]{1,0:T(8,128)(2,1)S(1)}, bf16[1024,1408]{1,0:T(8,128)(2,1)S(1)}) fusion(f32[1024,1408]{1,0:T(8,128)} %copy-done.42, f32[1024,1408]{1,0:T(8,128)} %get-tuple-element.182, bf16[1024,2048]{1,0:T(8,128)(2,1)} %constant_dynamic-update-slice_fusion.2, bf16[1408,2048]{1,0:T(8,128)(2,1)} %all-gather.9.cloned.1.call-done), kind=kOutput, calls=%fused_computation.18 | convolution fusion | flops 5924323328 | bytes 27262976 | tf_op jit(solution)/shard_map/dot_general | solution.py:403
  305.7 9.7 %fusion.14 = f32[512,2048]{1,0:T(8,128)} fusion(bf16[2,2048,1408]{2,1,0:T(8,128)(2,1)} %all-gather.7.cloned.1.call-done, bf16[1024,1408]{1,0:T(8,128)(2,1)S(1)} %get-tuple-element.152), kind=kOutput, calls=%fused_computation.27 | convolution fusion | flops 2952790016 | bytes 11403264 | tf_op jit(solution)/shard_map/dot_general | solution.py:412
  346.0 11.5 %collective-permute-done.16 = bf16[256,2048]{1,0:T(8,128)(2,1)} collective-permute-done((bf16[256,2048]{1,0:T(8,128)(2,1)}, bf16[256,2048]{1,0:T(8,128)(2,1)}, u32[]{:S(2)}, u32[]{:S(2)}) %collective-permute-start.16) | collective-permute-done | bytes 1048608 | tf_op jit(solution)/shard_map/ppermute | solution.py:58
  362.9 17.8 %convert_bitcast_fusion = bf16[2,2048,1408]{1,2,0:T(8,128)(2,1)} fusion(bf16[1,1024,1408]{2,1,0:T(8,128)(2,1)S(1)} %bitcast.132, bf16[1,1024,1408]{2,1,0:T(8,128)(2,1)S(1)} %bitcast.133, bf16[1024,2048]{1,0:T(8,128)(2,1)} %constant_dynamic-update-slice_fusion.4), kind=kOutput, calls=%fused_computation | convolution fusion | flops 11819810816 | bytes 21495808 | tf_op jit(solution)/shard_map/rd,crk->cdk/dot_general | solution.py:419
  389.0 9.2 %collective-permute-done.21 = bf16[128,2048]{1,0:T(8,128)(2,1)S(1)} collective-permute-done((bf16[128,2048]{1,0:T(8,128)(2,1)S(1)}, bf16[128,2048]{1,0:T(8,128)(2,1)S(1)}, u32[]{:S(2)}, u32[]{:S(2)}) %collective-permute-start.21) | collective-permute-done | bytes 524320 | tf_op jit(solution)/shard_map/ppermute | solution.py:58
  403.0 8.3 %convolution_convert_fusion.1 = bf16[1024,2048]{1,0:T(8,128)(2,1)} fusion(bf16[1024,1408]{1,0:T(8,128)(2,1)S(1)} %copy-done.41, bf16[1408,2048]{1,0:T(8,128)(2,1)S(1)} %bitcast.131), kind=kOutput, calls=%fused_computation.40 | convolution fusion | flops 5907677184 | bytes 12845056 | tf_op jit(solution)/shard_map/dot_general | solution.py:434
  427.2 20.4 %attend_back.1 = (bf16[3,1024,512]{2,1,0:T(8,128)(2,1)}, f32[2,3,512]{2,1,0:T(4,128)}) custom-call(s32[8]{0:T(128)} %stack.57.offs_ref, bf16[3,2,512,512]{3,2,1,0:T(8,128)(2,1)} %get-tuple-element.70.refs_0_, bf16[1024,512]{1,0:T(8,128)(2,1)} %get-tuple-element.71.refs_1_, bf16[1024,512]{1,0:T(8,128)(2,1)} %fusion.42.refs_2_, ...), custom_call_target="tpu_custom_call" | custom-call | tf_op jit(solution)/shard_map/attend_back/pallas_call | solution.py:318
  452.5 11.8 %convert_bitcast_fusion.1 = bf16[3,2048,512]{1,2,0:T(8,128)(2,1)} fusion(bf16[3,1024,512]{2,1,0:T(8,128)(2,1)S(1)} %copy-done.32, bf16[1024,2048]{1,0:T(8,128)(2,1)} %constant_dynamic-update-slice_fusion, f32[2048]{0:T(1024)S(1)} %bitcast.121, f32[2048]{0:T(1024)S(1)} %bitcast.115, f32[1024]{0:T(1024)S(1)} %copy-done.25, f32[1024]{0:T(1024)S(1)} %copy-done.19), kind=kOutput, calls=%fused_computation.11 | convolution fusion | flops 6458179584 | bytes 13656064 | tf_op jit(solution)/shard_map/rd,crk->cdk/dot_general | solution.py:440
  475.4 20.5 %collective-permute-done.24 = bf16[256,2048]{1,0:T(8,128)(2,1)S(1)} collective-permute-done((bf16[256,2048]{1,0:T(8,128)(2,1)S(1)}, bf16[256,2048]{1,0:T(8,128)(2,1)S(1)}, u32[]{:S(2)}, u32[]{:S(2)}) %collective-permute-start.24) | collective-permute-done | bytes 1048608 | tf_op jit(solution)/shard_map/ppermute | solution.py:58
  520.1 13.9 %collective-permute-done.29 = bf16[256,2048]{1,0:T(8,128)(2,1)S(1)} collective-permute-done((bf16[256,2048]{1,0:T(8,128)(2,1)S(1)}, bf16[256,2048]{1,0:T(8,128)(2,1)S(1)}, u32[]{:S(2)}, u32[]{:S(2)}) %collective-permute-start.29) | collective-permute-done | bytes 1048608 | tf_op jit(solution)/shard_map/ppermute | solution.py:58
  580.5 98.0 %reduce-scatter.6.cloned.1.call-done = bf16[2,256,1408]{1,2,0:T(8,128)(2,1)} async-done(((bf16[2,2048,1408]{1,2,0:T(8,128)(2,1)}), bf16[2,256,1408]{1,2,0:T(8,128)(2,1)}) %reduce-scatter.6.cloned.1.call-update) | async-done | bytes 1441808 | tf_op jit(solution)/shard_map/reduce_scatter | solution.py:425
  (328 shorter events, 226.2 us)
Async XLA Ops:
  7.2 130.8 %all-gather.5.cloned.1.call-start = ((), (), s32[]{:S(2)}) async-start(), calls=%async_computation.3 | async-start | bytes 9437184 | tf_op jit(solution)/shard_map/all_gather | solution.py:357
  10.8 245.9 %all-gather.7.cloned.1.call-start = ((), (), s32[]{:S(2)}) async-start(), calls=%async_computation.4 | async-start | bytes 12976128 | tf_op jit(solution)/shard_map/all_gather | solution.py:359
  11.6 279.8 %all-gather.9.cloned.1.call-start = ((), (), s32[]{:S(2)}) async-start(), calls=%async_computation.5 | async-start | bytes 6488064 | tf_op jit(solution)/shard_map/all_gather | solution.py:360
  28.2 24.0 %collective-permute-start.3 = (bf16[256,2048]{1,0:T(8,128)(2,1)S(1)}, bf16[256,2048]{1,0:T(8,128)(2,1)}, u32[]{:S(2)}, u32[]{:S(2)}) collective-permute-start(bf16[256,2048]{1,0:T(8,128)(2,1)S(1)} %pad_maximum_fusion.13), channel_id=1, source_target_pairs={{0,1},{1,0},{2,3},{3,2},{4,5},{5,4},{6,7},{7,6},{8,9},{9,8},{10,11... | collective-permute-start | bytes 3145736 | tf_op jit(solution)/shard_map/ppermute | solution.py:58
  29.8 23.9 %collective-permute-start.2 = (bf16[256,2048]{1,0:T(8,128)(2,1)S(1)}, bf16[256,2048]{1,0:T(8,128)(2,1)}, u32[]{:S(2)}, u32[]{:S(2)}) collective-permute-start(bf16[256,2048]{1,0:T(8,128)(2,1)S(1)} %pad_maximum_fusion.12), channel_id=1, source_target_pairs={{0,2},{1,3},{2,0},{3,1},{4,6},{5,7},{6,4},{7,5},{8,10},{9,11},{10,... | collective-permute-start | bytes 3145736 | tf_op jit(solution)/shard_map/ppermute | solution.py:58
  58.4 46.2 %collective-permute-start.5 = (bf16[128,2048]{1,0:T(8,128)(2,1)S(1)}, bf16[128,2048]{1,0:T(8,128)(2,1)}, u32[]{:S(2)}, u32[]{:S(2)}) collective-permute-start(bf16[128,2048]{1,0:T(8,128)(2,1)S(1)} %get-tuple-element.166), channel_id=1, source_target_pairs={{0,2},{1,3},{2,0},{3,1},{4,6},{5,7},{6,4},{7,5},{8,10},{9,11},{10,... | collective-permute-start | bytes 1572872 | tf_op jit(solution)/shard_map/ppermute | solution.py:58
  64.4 41.4 %collective-permute-start.4 = (bf16[128,2048]{1,0:T(8,128)(2,1)S(1)}, bf16[128,2048]{1,0:T(8,128)(2,1)S(1)}, u32[]{:S(2)}, u32[]{:S(2)}) collective-permute-start(bf16[128,2048]{1,0:T(8,128)(2,1)S(1)} %get-tuple-element.167), channel_id=1, source_target_pairs={{0,1},{1,0},{2,3},{3,2},{4,5},{5,4},{6,7},{7,6},{8,9},{9,8},{10,11... | collective-permute-start | bytes 1572872 | tf_op jit(solution)/shard_map/ppermute | solution.py:58
  105.9 25.0 %collective-permute-start.7 = (bf16[256,2048]{1,0:T(8,128)(2,1)S(1)}, bf16[256,2048]{1,0:T(8,128)(2,1)S(1)}, u32[]{:S(2)}, u32[]{:S(2)}) collective-permute-start(bf16[256,2048]{1,0:T(8,128)(2,1)S(1)} %pad_maximum_fusion.15), channel_id=1, source_target_pairs={{0,1},{1,0},{2,3},{3,2},{4,5},{5,4},{6,7},{7,6},{8,9},{9,8},{10,11... | collective-permute-start | bytes 3145736 | tf_op jit(solution)/shard_map/ppermute | solution.py:58
  109.6 25.0 %collective-permute-start.6 = (bf16[256,2048]{1,0:T(8,128)(2,1)S(1)}, bf16[256,2048]{1,0:T(8,128)(2,1)S(1)}, u32[]{:S(2)}, u32[]{:S(2)}) collective-permute-start(bf16[256,2048]{1,0:T(8,128)(2,1)S(1)} %pad_maximum_fusion.14), channel_id=1, source_target_pairs={{0,2},{1,3},{2,0},{3,1},{4,6},{5,7},{6,4},{7,5},{8,10},{9,11},{10,... | collective-permute-start | bytes 3145736 | tf_op jit(solution)/shard_map/ppermute | solution.py:58
  174.7 24.2 %collective-permute-start.9 = (bf16[256,2048]{1,0:T(8,128)(2,1)S(1)}, bf16[256,2048]{1,0:T(8,128)(2,1)S(1)}, u32[]{:S(2)}, u32[]{:S(2)}) collective-permute-start(bf16[256,2048]{1,0:T(8,128)(2,1)S(1)} %slice.288), channel_id=1, source_target_pairs={{0,1},{1,0},{2,3},{3,2},{4,5},{5,4},{6,7},{7,6},{8,9},{9,8},{10,11... | collective-permute-start | bytes 3145736 | tf_op jit(solution)/shard_map/ppermute | solution.py:58
  179.5 23.8 %collective-permute-start.8 = (bf16[256,2048]{1,0:T(8,128)(2,1)S(1)}, bf16[256,2048]{1,0:T(8,128)(2,1)S(1)}, u32[]{:S(2)}, u32[]{:S(2)}) collective-permute-start(bf16[256,2048]{1,0:T(8,128)(2,1)S(1)} %slice.286), channel_id=1, source_target_pairs={{0,2},{1,3},{2,0},{3,1},{4,6},{5,7},{6,4},{7,5},{8,10},{9,11},{10,... | collective-permute-start | bytes 3145736 | tf_op jit(solution)/shard_map/ppermute | solution.py:58
  220.1 354.2 %reduce-scatter.8.cloned.1.call-start = ((), (), s32[]{:S(2)}) async-start(), calls=%async_computation.8 | async-start | bytes 6488064 | tf_op jit(solution)/shard_map/reduce_scatter | solution.py:401
  231.2 21.8 %collective-permute-start.15 = (bf16[256,2048]{1,0:T(8,128)(2,1)S(1)}, bf16[256,2048]{1,0:T(8,128)(2,1)S(1)}, u32[]{:S(2)}, u32[]{:S(2)}) collective-permute-start(bf16[256,2048]{1,0:T(8,128)(2,1)S(1)} %pad_maximum_fusion.17), channel_id=1, source_target_pairs={{0,1},{1,0},{2,3},{3,2},{4,5},{5,4},{6,7},{7,6},{8,9},{9,8},{10,11... | collective-permute-start | bytes 3145736 | tf_op jit(solution)/shard_map/ppermute | solution.py:58
  231.8 21.4 %collective-permute-start.14 = (bf16[256,2048]{1,0:T(8,128)(2,1)S(1)}, bf16[256,2048]{1,0:T(8,128)(2,1)S(1)}, u32[]{:S(2)}, u32[]{:S(2)}) collective-permute-start(bf16[256,2048]{1,0:T(8,128)(2,1)S(1)} %pad_maximum_fusion.16), channel_id=1, source_target_pairs={{0,2},{1,3},{2,0},{3,1},{4,6},{5,7},{6,4},{7,5},{8,10},{9,11},{10,... | collective-permute-start | bytes 3145736 | tf_op jit(solution)/shard_map/ppermute | solution.py:58
  322.6 21.3 %collective-permute-start.17 = (bf16[256,2048]{1,0:T(8,128)(2,1)S(1)}, bf16[256,2048]{1,0:T(8,128)(2,1)}, u32[]{:S(2)}, u32[]{:S(2)}) collective-permute-start(bf16[256,2048]{1,0:T(8,128)(2,1)S(1)} %slice.302), channel_id=1, source_target_pairs={{0,1},{1,0},{2,3},{3,2},{4,5},{5,4},{6,7},{7,6},{8,9},{9,8},{10,11... | collective-permute-start | bytes 3145736 | tf_op jit(solution)/shard_map/ppermute | solution.py:58
  336.3 21.2 %collective-permute-start.16 = (bf16[256,2048]{1,0:T(8,128)(2,1)}, bf16[256,2048]{1,0:T(8,128)(2,1)}, u32[]{:S(2)}, u32[]{:S(2)}) collective-permute-start(bf16[256,2048]{1,0:T(8,128)(2,1)} %slice.298), channel_id=1, source_target_pairs={{0,2},{1,3},{2,0},{3,1},{4,6},{5,7},{6,4},{7,5},{8,10},{9,11},{10,... | collective-permute-start | bytes 3145736 | tf_op jit(solution)/shard_map/ppermute | solution.py:58
  337.1 239.4 %reduce-scatter.4.cloned.1.call-start = ((), (), s32[]{:S(2)}) async-start(), calls=%async_computation.6 | async-start | bytes 9437184 | tf_op jit(solution)/shard_map/reduce_scatter | solution.py:447
  360.1 20.6 %collective-permute-start.19 = (bf16[128,2048]{1,0:T(8,128)(2,1)}, bf16[128,2048]{1,0:T(8,128)(2,1)}, u32[]{:S(2)}, u32[]{:S(2)}) collective-permute-start(bf16[128,2048]{1,0:T(8,128)(2,1)} %slice.251), channel_id=1, source_target_pairs={{0,2},{1,3},{2,0},{3,1},{4,6},{5,7},{6,4},{7,5},{8,10},{9,11},{10,... | collective-permute-start | bytes 1572872 | tf_op jit(solution)/shard_map/ppermute | solution.py:58
  361.7 20.2 %collective-permute-start.18 = (bf16[128,2048]{1,0:T(8,128)(2,1)}, bf16[128,2048]{1,0:T(8,128)(2,1)}, u32[]{:S(2)}, u32[]{:S(2)}) collective-permute-start(bf16[128,2048]{1,0:T(8,128)(2,1)} %slice.249), channel_id=1, source_target_pairs={{0,1},{1,0},{2,3},{3,2},{4,5},{5,4},{6,7},{7,6},{8,9},{9,8},{10,11... | collective-permute-start | bytes 1572872 | tf_op jit(solution)/shard_map/ppermute | solution.py:58
  471.1 207.5 %reduce-scatter.6.cloned.1.call-start = ((), (), s32[]{:S(2)}) async-start(), calls=%async_computation.7 | async-start | bytes 12976128 | tf_op jit(solution)/shard_map/reduce_scatter | solution.py:425
  473.6 22.2 %collective-permute-start.24 = (bf16[256,2048]{1,0:T(8,128)(2,1)S(1)}, bf16[256,2048]{1,0:T(8,128)(2,1)S(1)}, u32[]{:S(2)}, u32[]{:S(2)}) collective-permute-start(bf16[256,2048]{1,0:T(8,128)(2,1)S(1)} %get-tuple-element.156), channel_id=1, source_target_pairs={{0,2},{1,3},{2,0},{3,1},{4,6},{5,7},{6,4},{7,5},{8,10},{9,11},{10,... | collective-permute-start | bytes 3145736 | tf_op jit(solution)/shard_map/ppermute | solution.py:58
  474.6 21.3 %collective-permute-start.25 = (bf16[256,2048]{1,0:T(8,128)(2,1)S(1)}, bf16[256,2048]{1,0:T(8,128)(2,1)S(1)}, u32[]{:S(2)}, u32[]{:S(2)}) collective-permute-start(bf16[256,2048]{1,0:T(8,128)(2,1)S(1)} %get-tuple-element.155), channel_id=1, source_target_pairs={{0,1},{1,0},{2,3},{3,2},{4,5},{5,4},{6,7},{7,6},{8,9},{9,8},{10,11... | collective-permute-start | bytes 3145736 | tf_op jit(solution)/shard_map/ppermute | solution.py:58
  515.5 18.5 %collective-permute-start.29 = (bf16[256,2048]{1,0:T(8,128)(2,1)S(1)}, bf16[256,2048]{1,0:T(8,128)(2,1)S(1)}, u32[]{:S(2)}, u32[]{:S(2)}) collective-permute-start(bf16[256,2048]{1,0:T(8,128)(2,1)S(1)} %slice.309), channel_id=1, source_target_pairs={{0,1},{1,0},{2,3},{3,2},{4,5},{5,4},{6,7},{7,6},{8,9},{9,8},{10,11... | collective-permute-start | bytes 3145736 | tf_op jit(solution)/shard_map/ppermute | solution.py:58
  520.1 20.5 %collective-permute-start.28 = (bf16[256,2048]{1,0:T(8,128)(2,1)S(1)}, bf16[256,2048]{1,0:T(8,128)(2,1)S(1)}, u32[]{:S(2)}, u32[]{:S(2)}) collective-permute-start(bf16[256,2048]{1,0:T(8,128)(2,1)S(1)} %slice.307), channel_id=1, source_target_pairs={{0,2},{1,3},{2,0},{3,1},{4,6},{5,7},{6,4},{7,5},{8,10},{9,11},{10,... | collective-permute-start | bytes 3145736 | tf_op jit(solution)/shard_map/ppermute | solution.py:58
  (69 other events, 793.4 us)
Sparse Core Ops, SparseCore 0:
  10.9 85.5 all-gather.4
  98.1 106.3 all-gather.6
  220.2 57.3 all-gather.8
  337.3 62.3 reduce-scatter.7
  471.2 86.4 reduce-scatter.3
  559.8 118.6 reduce-scatter.5

commit v5 on v4

--- a/solution.py
+++ b/solution.py
@@ -85,7 +85,9 @@
     plan = part_plan(block.shape[0])
     held = [block[lo:hi] for lo, hi, _ in plan]
     for j in range(len(plan)):
-        got = [swap(h, "tensor", order[j]) for h, (_, _, order) in zip(held, plan)]
+        got = []
+        for h, (_, _, order) in zip(held, plan):
+            got.append(swap(h, "tensor", order[j]))
         held = together(jnp.concatenate([h, g], axis=0) for h, g in zip(held, got))
     return jnp.concatenate(held, axis=0)
 
@@ -132,6 +134,48 @@
     return jnp.stack(places).astype(jnp.int32)
 
 
+def ring_step(value):
+    count = lax.axis_size("dp")
+    return lax.ppermute(value, "dp", [(i, (i + 2) % count) for i in range(count)])
+
+
+def ring_owners():
+    count = lax.axis_size("dp")
+    here = lax.axis_index("dp")
+    return [(here - 2 * k) % count for k in range(count // 2)]
+
+
+def ring_gather(shard):
+    count = lax.axis_size("dp")
+    size = shard.shape[0]
+    full = jnp.zeros((size * count,) + shard.shape[1:], shard.dtype)
+    held = shard
+    for k, owner in enumerate(ring_owners()):
+        if k:
+            held = ring_step(held)
+        full = lax.dynamic_update_slice_in_dim(full, held, owner * size, 0)
+        full = lax.dynamic_update_slice_in_dim(full, swap(held, "dp", 1), (owner ^ 1) * size, 0)
+    return full
+
+
+def ring_reduce(grad):
+    size = grad.shape[1] // lax.axis_size("dp")
+    owners = ring_owners()
+
+    def columns(owner):
+        return lax.dynamic_slice_in_dim(grad, owner * size, size, 1)
+
+    other = swap(jnp.stack([columns(owner ^ 1) for owner in owners]), "dp", 1)
+
+    def block(k):
+        return columns(owners[k]).astype(F32) + other[k].astype(F32)
+
+    total = block(1)
+    for k in list(range(2, len(owners))) + [0]:
+        total = block(k) + ring_step(total.astype(BF16)).astype(F32)
+    return total
+
+
 def after(value, *others):
     return lax.optimization_barrier((value,) + others)[0]
 
@@ -164,9 +208,11 @@
 
 
 def masked(scores, start):
-    rows = lax.broadcasted_iota(jnp.int32, scores.shape, 0) + start
-    cols = lax.broadcasted_iota(jnp.int32, scores.shape, 1)
-    return jnp.where(rows >= cols, scores, -jnp.inf)
+    own = scores[:, start:]
+    rows = lax.broadcasted_iota(jnp.int32, own.shape, 0)
+    cols = lax.broadcasted_iota(jnp.int32, own.shape, 1)
+    own = jnp.where(rows >= cols, own, -jnp.inf)
+    return jnp.concatenate([scores[:, :start], own], axis=1) if start else own
 
 
 def attend_kernel(offs_ref, pre_ref, keep_ref, low_ref, high_ref, qkv_ref, ctx_ref, lse_ref, *, runs):
@@ -196,7 +242,7 @@
             q = qkv_ref[0, seq, start:end, cols]
             k = qkv_ref[1, seq, :end, cols]
             v = qkv_ref[2, seq, :end, cols]
-            s = lax.dot_general(q, k, NT, preferred_element_type=F32) * scale
+            s = lax.dot_general(q * scale, k, NT, preferred_element_type=F32)
             s = masked(s, start)
             top = jnp.max(s, axis=-1, keepdims=True)
             e = jnp.exp(s - top)
@@ -249,10 +295,10 @@
             g = gctx[start:end, cols]
             lse = lse_ref[seq, start:end, h * HEAD_DIM : h * HEAD_DIM + 1]
             delta = jnp.sum(prod[start:end, cols], axis=-1, keepdims=True)
-            s = lax.dot_general(q, k, NT, preferred_element_type=F32) * scale
+            s = lax.dot_general(q * scale, k, NT, preferred_element_type=F32)
             p = jnp.exp(masked(s, start) - lse)
             dp = lax.dot_general(g, v, NT, preferred_element_type=F32)
-            ds = (p * (dp - delta) * scale).astype(BF16)
+            ds = (p * (dp - delta)).astype(BF16)
             p_low = p.astype(BF16)
             dq_parts.append(jnp.dot(ds, k, preferred_element_type=F32))
             dk_i = lax.dot_general(ds, q, TN, preferred_element_type=F32)
@@ -261,8 +307,8 @@
                 part = slice(j * CHUNK, (j + 1) * CHUNK)
                 dk[j] = dk_i[part] if dk[j] is None else dk[j] + dk_i[part]
                 dv[j] = dv_i[part] if dv[j] is None else dv[j] + dv_i[part]
-        gq.append(jnp.concatenate(dq_parts, axis=0))
-        gk.append(jnp.concatenate(dk, axis=0))
+        gq.append(jnp.concatenate(dq_parts, axis=0) * scale)
+        gk.append(jnp.concatenate(dk, axis=0) * scale)
         gv.append(jnp.concatenate(dv, axis=0))
     keep, low, high = keep_ref[...], low_ref[...], high_ref[...]
     for c, parts in enumerate((gq, gk, gv)):
@@ -353,18 +399,16 @@
     runs = sequence_runs(rows)
     tables = rotary_lanes()
 
-    attn_shard = jnp.concatenate([qkv_weight, out_weight.T[None]], axis=0)
-    attn_local = lax.all_gather(attn_shard, "dp", axis=1, tiled=True)
-    qkv_local, out_turned = attn_local[:3], attn_local[3]
+    qkv_local = lax.all_gather(qkv_weight, "dp", axis=1, tiled=True)
     gate_up_local = lax.all_gather(gate_up_weight, "dp", axis=1, tiled=True)
     down_local = lax.all_gather(down_weight, "dp", axis=1, tiled=True)
 
+    packed = jnp.concatenate(
+        [norm1_gain, norm1_bias, norm2_gain, norm2_bias, qkv_bias.reshape(-1)]
+    )
+    packed = lax.all_gather(packed, "dp", axis=0, tiled=False)
     x_rows = collect_rows(layer_input)
     cot_rows = collect_rows(after(out_cotangent, x_rows))
-    packed = jnp.concatenate(
-        [norm1_gain, norm1_bias, norm2_gain, norm2_bias, qkv_bias.reshape(-1)]
-    )
-    packed = lax.all_gather(after(packed, x_rows), "dp", axis=0, tiled=False)
     gain_one, bias_one, gain_two, bias_two = (
         packed[:, k * part : (k + 1) * part].reshape(width).astype(F32) for k in range(4)
     )
@@ -374,12 +418,13 @@
 
     x_float = layer_input.astype(F32)
     hat_one, inv_one = layer_norm(x_float)
+    out_turned = ring_gather(out_weight.T)
     rows_one = (layer_norm(x_rows.astype(F32))[0] * gain_one + bias_one).astype(BF16)
     pre = (
         jnp.einsum("rd,cdk->crk", rows_one, qkv_local, preferred_element_type=F32)
         + bias_local[:, None, :]
     )
-    qkv_heads, context, lse = attend(offs, after(pre, cot_rows), tables, runs)
+    qkv_heads, context, lse = attend(offs, pre, tables, runs)
     parts = part_slices(rows)
     attn_terms = [
         lax.dot_general(context[at], out_turned, NT, preferred_element_type=F32).astype(BF16)
@@ -440,14 +485,9 @@
     grad_wqkv = jnp.einsum(
         "rd,crk->cdk", rows_one, grad_pre, preferred_element_type=F32
     ).astype(BF16)
-    grad_wout = lax.dot_general(
-        resid_rows, context, TN, preferred_element_type=F32
-    ).astype(BF16)
-    grad_wattn = jnp.concatenate([grad_wqkv, grad_wout[None]], axis=0)
-    share_attn = lax.psum_scatter(grad_wattn, "dp", scatter_dimension=1, tiled=True)
-    share_attn = share_attn.astype(F32)
-    layer_output = (residual + spread_rows([mlp_terms[at] for at in parts], rows)).astype(BF16)
-    late_pre, layer_output = lax.optimization_barrier((grad_pre, layer_output, grad_wattn))[:2]
+    share_qkv = lax.psum_scatter(grad_wqkv, "dp", scatter_dimension=1, tiled=True)
+    share_qkv = share_qkv.astype(F32)
+    late_pre = after(grad_pre, grad_wqkv)
     qkv_terms = [
         jnp.einsum(
             "crk,cdk->rd", late_pre[:, at], qkv_local, preferred_element_type=F32
@@ -455,7 +495,13 @@
         for at in parts
     ]
     grad_normed_one = spread_rows(qkv_terms, rows)
+    grad_wout = lax.dot_general(
+        after(context, *qkv_terms), resid_rows, TN, preferred_element_type=F32
+    ).astype(BF16)
+    share_out = ring_reduce(grad_wout)
     grad_input = grad_resid + norm_back(grad_normed_one * gain_one, hat_one, inv_one)
+    mlp_terms = after(mlp_terms, grad_normed_one)
+    layer_output = (residual + spread_rows([mlp_terms[at] for at in parts], rows)).astype(BF16)
 
     norm_sums = jnp.stack(
         [
@@ -478,9 +524,9 @@
         grad_input,
         share_norm[0],
         share_norm[1],
-        share_attn[:3],
+        share_qkv,
         share_bias,
-        share_attn[3].T,
+        share_out,
         share_norm[2],
         share_norm[3],
         share_gate_up,

time: 694 us -> 676 us (0.974)
  waiting for transfers between devices: 325 us -> 301 us
  local copies, waits for them, and re-layouts: 36.1 us -> 47 us
  blocking collectives: 38.2 us -> 29.2 us
    ppermute x37 -> x42, waiting for transfers between devices: 226 us -> 175 us  [swap(): lax.ppermute(value, axis, [(i, i ^ bit) for i in range(lax.axis_size(axis...]
    ppermute x0 -> x6, waiting for transfers between devices: none -> 33.8 us  [ring_step(): lax.ppermute(value, 'dp', [(i, (i + 2) % count) for i in range(count)])]
    dynamic_update_slice x0 -> x8, local copies, waits for them, and re-layouts: none -> 9.84 us  [the longest x4 5.04 us: ring_gather(): full = lax.dynamic_update_slice_in_dim(full, held, owner * size, 0)]
    unnamed x1, blocking collectives: 38.2 us -> 29.2 us
    concatenate x2 -> x0, other arithmetic: 8.77 us -> none  [the longest x1 6.76 us: shards(): grad_wattn = jnp.concatenate([grad_wqkv, grad_wout[None]], axis=0)]
    reduce_scatter x1, waiting for transfers between devices: 98 us -> 90.4 us  [shards(): lax.psum_scatter(grad_wgate_up, 'dp', scatter_dimension=1, tiled=True)]
    unnamed x119 -> x142, local copies, waits for them, and re-layouts: 17.7 us -> 18.3 us
    ppermute x37 -> x42, starting transfers between devices: 32.6 us -> 32.9 us  [swap(): lax.ppermute(value, axis, [(i, i ^ bit) for i in range(lax.axis_size(axis...]
  transfers between devices with their start and end apart: 43 -> 54, of which waited for: 29 -> 29; matrix products, arithmetic and copies ran while one was open for 28% -> 30% of each run, Pallas kernels for 6% -> 6%
where the time goes in v5:
time: 676 us; the launch traced here: 668 us
  waiting for transfers between devices  301 us (45%)
  matrix products  148 us (22%)
  local copies, waits for them, and re-layouts  47 us (7%)
  other arithmetic  46.8 us (7%)
  Pallas kernels  41.6 us (6%)
  starting transfers between devices  39 us (6%)
  blocking collectives  29.2 us (4%)
  between operations  16.4 us (2%)
    ppermute x42, waiting for transfers between devices, swap(): lax.ppermute(value, axis, [(i, i ^ bit) for i in range(lax.axis_size(axis...  175 us
    reduce_scatter x1, waiting for transfers between devices, shards(): lax.psum_scatter(grad_wgate_up, 'dp', scatter_dimension=1, tiled=True)  90.4 us
    ppermute x6, waiting for transfers between devices, ring_step(): lax.ppermute(value, 'dp', [(i, (i + 2) % count) for i in range(count)])  33.8 us
    ppermute x42, starting transfers between devices, swap(): lax.ppermute(value, axis, [(i, i ^ bit) for i in range(lax.axis_size(axis...  32.9 us
    unnamed x1, blocking collectives  29.2 us
    pallas_call x1, Pallas kernels, attend(): pl.pallas_call(functools.partial(attend_kernel, runs=runs), out_shape=(ja...  20.8 us
    pallas_call x1, Pallas kernels, attend_back(): pl.pallas_call(functools.partial(attend_back_kernel, runs=runs), out_shap...  20.8 us
    unnamed x142, local copies, waits for them, and re-layouts  18.3 us
  transfers between devices with their start and end apart: 54, of which 29 were waited for; matrix products, arithmetic and copies ran while one was open for 30% of the time, Pallas kernels for 6%

profile of v5, /device:TPU:0, one launch (start us, length us, event | category | flops | bytes accessed | tf_op | source)
XLA Modules:
  0.0 668.5 jit_solution(13532311962272138363)
XLA Ops:
  17.6 29.2 %all-reduce = bf16[9728]{0:T(1024)(128)(2,1)S(1)} all-reduce(bf16[9728]{0:T(1024)(128)(2,1)S(1)} %dynamic-update-slice), channel_id=2, replica_groups=mesh['dp'=8,'tensor'=4] {'dp'}, use_global_device_ids=true, to_apply=%add | all-reduce | flops 9728 | bytes 38912
  71.2 11.5 %collective-permute-done.9 = bf16[256,512]{0,1:T(8,128)(2,1)S(1)} collective-permute-done((bf16[256,512]{0,1:T(8,128)(2,1)}, bf16[256,512]{0,1:T(8,128)(2,1)S(1)}, u32[]{:S(2)}, u32[]{:S(2)}) %collective-permute-start.9) | collective-permute-done | bytes 262176 | tf_op jit(solution)/shard_map/ppermute | solution.py:139
  92.1 13.3 %add_bitcast_fusion.pre_ref = f32[3,1024,512]{2,1,0:T(8,128)} fusion(f32[3,512]{1,0:T(4,128)S(1)} %reshape.171, bf16[3,2048,512]{2,1,0:T(8,128)(2,1)} %all-gather.5.cloned.1.call-done, bf16[1024,2048]{1,0:T(8,128)(2,1)} %copy-done, f32[2048]{0:T(1024)S(1)} %bitcast.138, f32[2048]{0:T(1024)S(1)} %bitcast.132, f32[1024]{0:T(1024)S(1)} %add_rsqrt_fusion, ...), kind=kOutput, calls=%fused_computation.11 | convolution fusion | flops 6456606720 | bytes 16807936 | tf_op jit(solution)/shard_map/rd,cdk->crk/dot_general | solution.py:424
  105.4 20.8 %attend.1 = (bf16[3,2,512,512]{3,2,1,0:T(8,128)(2,1)}, bf16[1024,512]{1,0:T(8,128)(2,1)}, f32[2,512,512]{2,1,0:T(8,128)}) custom-call(s32[8]{0:T(128)} %stack.72.offs_ref, f32[3,1024,512]{2,1,0:T(8,128)} %add_bitcast_fusion.pre_ref, f32[512,128]{1,0:T(8,128)} %concatenate.93.keep_ref.refs_4_, f32[512,128]{1,0:T(8,128)} %concatenate.94.low_ref.refs_5_, ...), custom_call_target="tpu_custom_call" | custom-call | tf_op jit(solution)/shard_map/attend/pallas_call | solution.py:343
  134.6 20.1 %collective-permute-done.12 = bf16[256,2048]{1,0:T(8,128)(2,1)S(1)} collective-permute-done((bf16[256,2048]{1,0:T(8,128)(2,1)S(1)}, bf16[256,2048]{1,0:T(8,128)(2,1)S(1)}, u32[]{:S(2)}, u32[]{:S(2)}) %collective-permute-start.12) | collective-permute-done | bytes 1048608 | tf_op jit(solution)/shard_map/ppermute | solution.py:58
  170.5 8.8 %collective-permute-done.14 = bf16[128,2048]{1,0:T(8,128)(2,1)S(1)} collective-permute-done((bf16[128,2048]{1,0:T(8,128)(2,1)S(1)}, bf16[128,2048]{1,0:T(8,128)(2,1)S(1)}, u32[]{:S(2)}, u32[]{:S(2)}) %collective-permute-start.14) | collective-permute-done | bytes 524320 | tf_op jit(solution)/shard_map/ppermute | solution.py:58
  187.2 12.6 %collective-permute-done.20 = bf16[128,2048]{1,0:T(8,128)(2,1)} collective-permute-done((bf16[128,2048]{1,0:T(8,128)(2,1)}, bf16[128,2048]{1,0:T(8,128)(2,1)}, u32[]{:S(2)}, u32[]{:S(2)}) %collective-permute-start.20) | collective-permute-done | bytes 524320 | tf_op jit(solution)/shard_map/ppermute | solution.py:58
  201.2 12.9 %collective-permute-done.19 = bf16[128,2048]{1,0:T(8,128)(2,1)S(1)} collective-permute-done((bf16[128,2048]{1,0:T(8,128)(2,1)}, bf16[128,2048]{1,0:T(8,128)(2,1)S(1)}, u32[]{:S(2)}, u32[]{:S(2)}) %collective-permute-start.19) | collective-permute-done | bytes 524320 | tf_op jit(solution)/shard_map/ppermute | solution.py:58
  220.8 17.5 %collective-permute-done.22 = bf16[256,2048]{1,0:T(8,128)(2,1)S(1)} collective-permute-done((bf16[256,2048]{1,0:T(8,128)(2,1)S(1)}, bf16[256,2048]{1,0:T(8,128)(2,1)S(1)}, u32[]{:S(2)}, u32[]{:S(2)}) %collective-permute-start.22) | collective-permute-done | bytes 1048608 | tf_op jit(solution)/shard_map/ppermute | solution.py:58
  245.1 12.3 %fusion.12 = f32[1024,1408]{1,0:T(8,128)} fusion(bf16[1024,2048]{1,0:T(8,128)(2,1)} %constant_dynamic-update-slice_fusion.4, bf16[2,2048,1408]{2,1,0:T(8,128)(2,1)} %all-gather.7.cloned.1.call-done), kind=kOutput, calls=%fused_computation.24 | convolution fusion | flops 5905580032 | bytes 15728640 | tf_op jit(solution)/shard_map/dot_general | solution.py:437
  257.4 11.9 %multiply_convert_fusion.2 = (bf16[1024,1408]{1,0:T(8,128)(2,1)S(1)}, f32[1024,1408]{1,0:T(8,128)}) fusion(f32[1024,1408]{1,0:T(8,128)} %fusion.12, bf16[1024,2048]{1,0:T(8,128)(2,1)} %constant_dynamic-update-slice_fusion.4, bf16[2,2048,1408]{2,1,0:T(8,128)(2,1)S(1)} %copy-done.47), kind=kOutput, calls=%fused_computation.19 | convolution fusion | flops 5914230784 | bytes 24379392 | tf_op jit(solution)/shard_map/dot_general | solution.py:438
  279.0 14.1 %multiply_convert_fusion = (bf16[1024,1408]{1,0:T(8,128)(2,1)S(1)}, bf16[1024,1408]{1,0:T(8,128)(2,1)S(1)}) fusion(f32[1024,1408]{1,0:T(8,128)} %fusion.12, f32[1024,1408]{1,0:T(8,128)} %get-tuple-element.184, bf16[1024,2048]{1,0:T(8,128)(2,1)} %copy-done.26, bf16[1408,2048]{1,0:T(8,128)(2,1)} %all-gather.9.cloned.1.call-done), kind=kOutput, calls=%fused_computation.17 | convolution fusion | flops 5924323328 | bytes 27262976 | tf_op jit(solution)/shard_map/dot_general | solution.py:448
  293.1 9.7 %fusion.10 = f32[512,2048]{1,0:T(8,128)} fusion(bf16[2,2048,1408]{2,1,0:T(8,128)(2,1)} %all-gather.7.cloned.1.call-done, bf16[1024,1408]{1,0:T(8,128)(2,1)S(1)} %get-tuple-element.150), kind=kOutput, calls=%fused_computation.22 | convolution fusion | flops 2952790016 | bytes 11403264 | tf_op jit(solution)/shard_map/dot_general | solution.py:457
  324.5 10.3 %collective-permute-done.24 = bf16[256,2048]{1,0:T(8,128)(2,1)} collective-permute-done((bf16[256,2048]{1,0:T(8,128)(2,1)S(1)}, bf16[256,2048]{1,0:T(8,128)(2,1)}, u32[]{:S(2)}, u32[]{:S(2)}) %collective-permute-start.24) | collective-permute-done | bytes 1048608 | tf_op jit(solution)/shard_map/ppermute | solution.py:58
  336.9 10.9 %collective-permute-done.23 = bf16[256,2048]{1,0:T(8,128)(2,1)} collective-permute-done((bf16[256,2048]{1,0:T(8,128)(2,1)}, bf16[256,2048]{1,0:T(8,128)(2,1)}, u32[]{:S(2)}, u32[]{:S(2)}) %collective-permute-start.23) | collective-permute-done | bytes 1048608 | tf_op jit(solution)/shard_map/ppermute | solution.py:58
  353.5 17.4 %convert_bitcast_fusion = bf16[2,2048,1408]{1,2,0:T(8,128)(2,1)} fusion(bf16[1,1024,1408]{2,1,0:T(8,128)(2,1)S(1)} %bitcast.148, bf16[1,1024,1408]{2,1,0:T(8,128)(2,1)S(1)} %bitcast.149, bf16[1024,2048]{1,0:T(8,128)(2,1)} %constant_dynamic-update-slice_fusion.4), kind=kOutput, calls=%fused_computation | convolution fusion | flops 11819810816 | bytes 21495808 | tf_op jit(solution)/shard_map/rd,crk->cdk/dot_general | solution.py:464
  379.1 9.7 %collective-permute-done.28 = bf16[128,2048]{1,0:T(8,128)(2,1)S(1)} collective-permute-done((bf16[128,2048]{1,0:T(8,128)(2,1)S(1)}, bf16[128,2048]{1,0:T(8,128)(2,1)S(1)}, u32[]{:S(2)}, u32[]{:S(2)}) %collective-permute-start.28) | collective-permute-done | bytes 524320 | tf_op jit(solution)/shard_map/ppermute | solution.py:58
  391.6 8.4 %convolution_convert_fusion.1 = bf16[1024,2048]{1,0:T(8,128)(2,1)} fusion(bf16[1024,1408]{1,0:T(8,128)(2,1)S(1)} %copy-done.56, bf16[1408,2048]{1,0:T(8,128)(2,1)S(1)} %bitcast.147), kind=kOutput, calls=%fused_computation.35 | convolution fusion | flops 5907677184 | bytes 12845056 | tf_op jit(solution)/shard_map/dot_general | solution.py:479
  400.0 12.1 %collective-permute-done.30 = bf16[256,2048]{1,0:T(8,128)(2,1)S(1)} collective-permute-done((bf16[256,2048]{1,0:T(8,128)(2,1)S(1)}, bf16[256,2048]{1,0:T(8,128)(2,1)S(1)}, u32[]{:S(2)}, u32[]{:S(2)}) %collective-permute-start.30) | collective-permute-done | bytes 1048608 | tf_op jit(solution)/shard_map/ppermute | solution.py:58
  417.6 20.8 %attend_back.1 = (bf16[3,1024,512]{2,1,0:T(8,128)(2,1)}, f32[2,3,512]{2,1,0:T(4,128)}) custom-call(s32[8]{0:T(128)} %stack.72.offs_ref, bf16[3,2,512,512]{3,2,1,0:T(8,128)(2,1)} %get-tuple-element.89.refs_0_, bf16[1024,512]{1,0:T(8,128)(2,1)} %get-tuple-element.104.refs_1_, bf16[1024,512]{1,0:T(8,128)(2,1)} %convolution_convert_fusion.5.refs_2_, ...), custom_call_target="tpu_custom_call" | custom-call | tf_op jit(solution)/shard_map/attend_back/pallas_call | solution.py:364
  438.4 11.8 %convert_bitcast_fusion.1 = bf16[3,2048,512]{1,2,0:T(8,128)(2,1)} fusion(bf16[3,1024,512]{2,1,0:T(8,128)(2,1)} %get-tuple-element.93, bf16[1024,2048]{1,0:T(8,128)(2,1)} %copy-done, f32[2048]{0:T(1024)S(1)} %bitcast.139, f32[2048]{0:T(1024)S(1)} %bitcast.133, f32[1024]{0:T(1024)S(1)} %copy-done.41, f32[1024]{0:T(1024)S(1)} %copy-done.35), kind=kOutput, calls=%fused_computation.10 | convolution fusion | flops 6458179584 | bytes 13656064 | tf_op jit(solution)/shard_map/rd,crk->cdk/dot_general | solution.py:485
  469.6 8.7 %collective-permute-done.32 = bf16[256,2048]{1,0:T(8,128)(2,1)S(1)} collective-permute-done((bf16[256,2048]{1,0:T(8,128)(2,1)S(1)}, bf16[256,2048]{1,0:T(8,128)(2,1)S(1)}, u32[]{:S(2)}, u32[]{:S(2)}) %collective-permute-start.32) | collective-permute-done | bytes 1048608 | tf_op jit(solution)/shard_map/ppermute | solution.py:58
  495.6 11.5 %collective-permute-done.45 = bf16[512,256]{1,0:T(8,128)(2,1)S(1)} collective-permute-done((bf16[512,256]{1,0:T(8,128)(2,1)}, bf16[512,256]{1,0:T(8,128)(2,1)S(1)}, u32[]{:S(2)}, u32[]{:S(2)}) %collective-permute-start.45) | collective-permute-done | bytes 262176 | tf_op jit(solution)/shard_map/ppermute | solution.py:139
  568.0 90.4 %reduce-scatter.6.cloned.1.call-done = bf16[2,256,1408]{1,2,0:T(8,128)(2,1)} async-done(((bf16[2,2048,1408]{1,2,0:T(8,128)(2,1)}), bf16[2,256,1408]{1,2,0:T(8,128)(2,1)}) %reduce-scatter.6.cloned.1.call-update) | async-done | bytes 1441808 | tf_op jit(solution)/shard_map/reduce_scatter | solution.py:470
  (382 shorter events, 245.2 us)
Async XLA Ops:
  7.2 84.9 %all-gather.5.cloned.1.call-start = ((), (), s32[]{:S(2)}) async-start(), calls=%async_computation.3 | async-start | bytes 7077888 | tf_op jit(solution)/shard_map/all_gather | solution.py:402
  7.9 237.2 %all-gather.7.cloned.1.call-start = ((), (), s32[]{:S(2)}) async-start(), calls=%async_computation.4 | async-start | bytes 12976128 | tf_op jit(solution)/shard_map/all_gather | solution.py:403
  8.7 270.3 %all-gather.9.cloned.1.call-start = ((), (), s32[]{:S(2)}) async-start(), calls=%async_computation.5 | async-start | bytes 6488064 | tf_op jit(solution)/shard_map/all_gather | solution.py:404
  8.7 57.5 %collective-permute-start.4 = (bf16[256,512]{0,1:T(8,128)(2,1)}, bf16[256,512]{0,1:T(8,128)(2,1)}, u32[]{:S(2)}, u32[]{:S(2)}) collective-permute-start(bf16[256,512]{0,1:T(8,128)(2,1)} %bitcast.12), channel_id=1, source_target_pairs={{0,4},{4,0},{8,12},{12,8},{16,20},{20,16},{24,28},{28,24},{1,5},{5... | collective-permute-start | bytes 786440 | tf_op jit(solution)/shard_map/ppermute | solution.py:58
  9.3 39.9 %collective-permute-start.5 = (bf16[256,512]{0,1:T(8,128)(2,1)}, bf16[256,512]{0,1:T(8,128)(2,1)}, u32[]{:S(2)}, u32[]{:S(2)}) collective-permute-start(bf16[256,512]{0,1:T(8,128)(2,1)} %bitcast.12), channel_id=1, source_target_pairs={{0,8},{4,12},{8,16},{12,20},{16,24},{20,28},{24,0},{28,4},{1,9},{5... | collective-permute-start | bytes 786440 | tf_op jit(solution)/shard_map/ppermute | solution.py:139
  12.0 37.4 %collective-permute-start = (bf16[128,2048]{1,0:T(8,128)(2,1)S(1)}, bf16[128,2048]{1,0:T(8,128)(2,1)}, u32[]{:S(2)}, u32[]{:S(2)}) collective-permute-start(bf16[128,2048]{1,0:T(8,128)(2,1)S(1)} %get-tuple-element.171), channel_id=1, source_target_pairs={{0,1},{1,0},{2,3},{3,2},{4,5},{5,4},{6,7},{7,6},{8,9},{9,8},{10,11... | collective-permute-start | bytes 1572872 | tf_op jit(solution)/shard_map/ppermute | solution.py:58
  13.6 37.1 %collective-permute-start.1 = (bf16[128,2048]{1,0:T(8,128)(2,1)S(1)}, bf16[128,2048]{1,0:T(8,128)(2,1)}, u32[]{:S(2)}, u32[]{:S(2)}) collective-permute-start(bf16[128,2048]{1,0:T(8,128)(2,1)S(1)} %get-tuple-element.170), channel_id=1, source_target_pairs={{0,2},{1,3},{2,0},{3,1},{4,6},{5,7},{6,4},{7,5},{8,10},{9,11},{10,... | collective-permute-start | bytes 1572872 | tf_op jit(solution)/shard_map/ppermute | solution.py:58
  52.8 33.8 %collective-permute-start.2 = (bf16[256,2048]{1,0:T(8,128)(2,1)S(1)}, bf16[256,2048]{1,0:T(8,128)(2,1)}, u32[]{:S(2)}, u32[]{:S(2)}) collective-permute-start(bf16[256,2048]{1,0:T(8,128)(2,1)S(1)} %pad_maximum_fusion.10), channel_id=1, source_target_pairs={{0,2},{1,3},{2,0},{3,1},{4,6},{5,7},{6,4},{7,5},{8,10},{9,11},{10,... | collective-permute-start | bytes 3145736 | tf_op jit(solution)/shard_map/ppermute | solution.py:58
  59.3 28.7 %collective-permute-start.3 = (bf16[256,2048]{1,0:T(8,128)(2,1)S(1)}, bf16[256,2048]{1,0:T(8,128)(2,1)S(1)}, u32[]{:S(2)}, u32[]{:S(2)}) collective-permute-start(bf16[256,2048]{1,0:T(8,128)(2,1)S(1)} %copy-done.12), channel_id=1, source_target_pairs={{0,1},{1,0},{2,3},{3,2},{4,5},{5,4},{6,7},{7,6},{8,9},{9,8},{10,11... | collective-permute-start | bytes 3145736 | tf_op jit(solution)/shard_map/ppermute | solution.py:58
  128.6 26.1 %collective-permute-start.12 = (bf16[256,2048]{1,0:T(8,128)(2,1)S(1)}, bf16[256,2048]{1,0:T(8,128)(2,1)S(1)}, u32[]{:S(2)}, u32[]{:S(2)}) collective-permute-start(bf16[256,2048]{1,0:T(8,128)(2,1)S(1)} %slice.287), channel_id=1, source_target_pairs={{0,1},{1,0},{2,3},{3,2},{4,5},{5,4},{6,7},{7,6},{8,9},{9,8},{10,11... | collective-permute-start | bytes 3145736 | tf_op jit(solution)/shard_map/ppermute | solution.py:58
  131.2 26.1 %collective-permute-start.11 = (bf16[256,2048]{1,0:T(8,128)(2,1)S(1)}, bf16[256,2048]{1,0:T(8,128)(2,1)S(1)}, u32[]{:S(2)}, u32[]{:S(2)}) collective-permute-start(bf16[256,2048]{1,0:T(8,128)(2,1)S(1)} %slice.285), channel_id=1, source_target_pairs={{0,2},{1,3},{2,0},{3,1},{4,6},{5,7},{6,4},{7,5},{8,10},{9,11},{10,... | collective-permute-start | bytes 3145736 | tf_op jit(solution)/shard_map/ppermute | solution.py:58
  132.4 33.2 %collective-permute-start.15 = (bf16[128,2048]{1,0:T(8,128)(2,1)S(1)}, bf16[128,2048]{1,0:T(8,128)(2,1)S(1)}, u32[]{:S(2)}, u32[]{:S(2)}) collective-permute-start(bf16[128,2048]{1,0:T(8,128)(2,1)S(1)} %get-tuple-element.167), channel_id=1, source_target_pairs={{0,1},{1,0},{2,3},{3,2},{4,5},{5,4},{6,7},{7,6},{8,9},{9,8},{10,11... | collective-permute-start | bytes 1572872 | tf_op jit(solution)/shard_map/ppermute | solution.py:58
  133.4 35.1 %collective-permute-start.16 = (bf16[128,2048]{1,0:T(8,128)(2,1)S(1)}, bf16[128,2048]{1,0:T(8,128)(2,1)S(1)}, u32[]{:S(2)}, u32[]{:S(2)}) collective-permute-start(bf16[128,2048]{1,0:T(8,128)(2,1)S(1)} %get-tuple-element.166), channel_id=1, source_target_pairs={{0,2},{1,3},{2,0},{3,1},{4,6},{5,7},{6,4},{7,5},{8,10},{9,11},{10,... | collective-permute-start | bytes 1572872 | tf_op jit(solution)/shard_map/ppermute | solution.py:58
  169.6 45.2 %collective-permute-start.18 = (bf16[256,2048]{1,0:T(8,128)(2,1)}, bf16[256,2048]{1,0:T(8,128)(2,1)}, u32[]{:S(2)}, u32[]{:S(2)}) collective-permute-start(bf16[256,2048]{1,0:T(8,128)(2,1)} %pad_maximum_fusion.13), channel_id=1, source_target_pairs={{0,1},{1,0},{2,3},{3,2},{4,5},{5,4},{6,7},{7,6},{8,9},{9,8},{10,11... | collective-permute-start | bytes 3145736 | tf_op jit(solution)/shard_map/ppermute | solution.py:58
  184.8 378.3 %reduce-scatter.8.cloned.1.call-start = ((), (), s32[]{:S(2)}) async-start(), calls=%async_computation.8 | async-start | bytes 6488064 | tf_op jit(solution)/shard_map/reduce_scatter | solution.py:446
  184.8 29.2 %collective-permute-start.19 = (bf16[128,2048]{1,0:T(8,128)(2,1)}, bf16[128,2048]{1,0:T(8,128)(2,1)S(1)}, u32[]{:S(2)}, u32[]{:S(2)}) collective-permute-start(bf16[128,2048]{1,0:T(8,128)(2,1)} %get-tuple-element.169), channel_id=1, source_target_pairs={{0,1},{1,0},{2,3},{3,2},{4,5},{5,4},{6,7},{7,6},{8,9},{9,8},{10,11... | collective-permute-start | bytes 1572872 | tf_op jit(solution)/shard_map/ppermute | solution.py:58
  185.3 34.7 %collective-permute-start.17 = (bf16[256,2048]{1,0:T(8,128)(2,1)S(1)}, bf16[256,2048]{1,0:T(8,128)(2,1)S(1)}, u32[]{:S(2)}, u32[]{:S(2)}) collective-permute-start(bf16[256,2048]{1,0:T(8,128)(2,1)S(1)} %copy-done.13), channel_id=1, source_target_pairs={{0,2},{1,3},{2,0},{3,1},{4,6},{5,7},{6,4},{7,5},{8,10},{9,11},{10,... | collective-permute-start | bytes 3145736 | tf_op jit(solution)/shard_map/ppermute | solution.py:58
  216.6 25.1 %collective-permute-start.21 = (bf16[256,2048]{1,0:T(8,128)(2,1)S(1)}, bf16[256,2048]{1,0:T(8,128)(2,1)S(1)}, u32[]{:S(2)}, u32[]{:S(2)}) collective-permute-start(bf16[256,2048]{1,0:T(8,128)(2,1)S(1)} %pad_maximum_fusion.14), channel_id=1, source_target_pairs={{0,2},{1,3},{2,0},{3,1},{4,6},{5,7},{6,4},{7,5},{8,10},{9,11},{10,... | collective-permute-start | bytes 3145736 | tf_op jit(solution)/shard_map/ppermute | solution.py:58
  310.5 24.3 %collective-permute-start.24 = (bf16[256,2048]{1,0:T(8,128)(2,1)S(1)}, bf16[256,2048]{1,0:T(8,128)(2,1)}, u32[]{:S(2)}, u32[]{:S(2)}) collective-permute-start(bf16[256,2048]{1,0:T(8,128)(2,1)S(1)} %slice.301), channel_id=1, source_target_pairs={{0,1},{1,0},{2,3},{3,2},{4,5},{5,4},{6,7},{7,6},{8,9},{9,8},{10,11... | collective-permute-start | bytes 3145736 | tf_op jit(solution)/shard_map/ppermute | solution.py:58
  324.5 240.9 %reduce-scatter.4.cloned.1.call-start = ((), (), s32[]{:S(2)}) async-start(), calls=%async_computation.6 | async-start | bytes 7077888 | tf_op jit(solution)/shard_map/reduce_scatter | solution.py:488
  450.1 208.3 %reduce-scatter.6.cloned.1.call-start = ((), (), s32[]{:S(2)}) async-start(), calls=%async_computation.7 | async-start | bytes 12976128 | tf_op jit(solution)/shard_map/reduce_scatter | solution.py:470
  513.8 26.2 %collective-permute-start.35 = (bf16[256,2048]{1,0:T(8,128)(2,1)S(1)}, bf16[256,2048]{1,0:T(8,128)(2,1)S(1)}, u32[]{:S(2)}, u32[]{:S(2)}) collective-permute-start(bf16[256,2048]{1,0:T(8,128)(2,1)S(1)} %get-tuple-element.154), channel_id=1, source_target_pairs={{0,2},{1,3},{2,0},{3,1},{4,6},{5,7},{6,4},{7,5},{8,10},{9,11},{10,... | collective-permute-start | bytes 3145736 | tf_op jit(solution)/shard_map/ppermute | solution.py:58
  514.6 25.4 %collective-permute-start.36 = (bf16[256,2048]{1,0:T(8,128)(2,1)S(1)}, bf16[256,2048]{1,0:T(8,128)(2,1)S(1)}, u32[]{:S(2)}, u32[]{:S(2)}) collective-permute-start(bf16[256,2048]{1,0:T(8,128)(2,1)S(1)} %get-tuple-element.153), channel_id=1, source_target_pairs={{0,1},{1,0},{2,3},{3,2},{4,5},{5,4},{6,7},{7,6},{8,9},{9,8},{10,11... | collective-permute-start | bytes 3145736 | tf_op jit(solution)/shard_map/ppermute | solution.py:58
  524.5 26.2 %collective-permute-start.47 = (bf16[512,256]{1,0:T(8,128)(2,1)}, bf16[512,256]{1,0:T(8,128)(2,1)S(1)}, u32[]{:S(2)}, u32[]{:S(2)}) collective-permute-start(bf16[512,256]{1,0:T(8,128)(2,1)} %fusion.42), channel_id=1, source_target_pairs={{0,8},{4,12},{8,16},{12,20},{16,24},{20,28},{24,0},{28,4},{1,9},{5... | collective-permute-start | bytes 786440 | tf_op jit(solution)/shard_map/ppermute | solution.py:139
  (92 other events, 1204.9 us)
Sparse Core Ops, SparseCore 0:
  9.6 78.9 all-gather.4
  90.2 106.5 all-gather.6
  198.4 59.0 all-gather.8
  324.6 67.8 reduce-scatter.7
  450.3 88.0 reduce-scatter.3
  540.5 117.8 reduce-scatter.5

commit v6 on v5

--- a/solution.py
+++ b/solution.py
@@ -174,6 +174,24 @@
     for k in list(range(2, len(owners))) + [0]:
         total = block(k) + ring_step(total.astype(BF16)).astype(F32)
     return total
+
+
+def core_halves(grad):
+    count = lax.axis_size("dp")
+    size = grad.shape[1] // count
+    core = lax.axis_index("dp") % 2
+
+    def half(which):
+        return jnp.concatenate(
+            [
+                lax.dynamic_slice_in_dim(grad, (2 * z + which) * size, size, 1)
+                for z in range(count // 2)
+            ],
+            axis=1,
+        )
+
+    got = swap(half(1 - core), "dp", 1)
+    return (half(core).astype(F32) + got.astype(F32)).astype(BF16)
 
 
 def after(value, *others):
@@ -483,11 +501,19 @@
     grad_context = jnp.dot(resid_rows, out_turned, preferred_element_type=F32).astype(BF16)
     grad_pre, bias_sums = attend_back(offs, qkv_heads, context, grad_context, lse, tables, runs)
     grad_wqkv = jnp.einsum(
-        "rd,crk->cdk", rows_one, grad_pre, preferred_element_type=F32
+        "crk,rd->ckd", grad_pre, rows_one, preferred_element_type=F32
     ).astype(BF16)
-    share_qkv = lax.psum_scatter(grad_wqkv, "dp", scatter_dimension=1, tiled=True)
-    share_qkv = share_qkv.astype(F32)
-    late_pre = after(grad_pre, grad_wqkv)
+    wqkv_half = core_halves(grad_wqkv.reshape(3 * head_cols, width))
+    share_qkv = lax.psum_scatter(
+        wqkv_half,
+        "dp",
+        scatter_dimension=1,
+        tiled=True,
+        axis_index_groups=[list(range(c, dp_count, 2)) for c in range(2)],
+    )
+    share_qkv = share_qkv.astype(F32).reshape(3, head_cols, part).transpose(0, 2, 1)
+    layer_output = (residual + spread_rows([mlp_terms[at] for at in parts], rows)).astype(BF16)
+    late_pre, layer_output = lax.optimization_barrier((grad_pre, layer_output, grad_wqkv))[:2]
     qkv_terms = [
         jnp.einsum(
             "crk,cdk->rd", late_pre[:, at], qkv_local, preferred_element_type=F32
@@ -500,8 +526,6 @@
     ).astype(BF16)
     share_out = ring_reduce(grad_wout)
     grad_input = grad_resid + norm_back(grad_normed_one * gain_one, hat_one, inv_one)
-    mlp_terms = after(mlp_terms, grad_normed_one)
-    layer_output = (residual + spread_rows([mlp_terms[at] for at in parts], rows)).astype(BF16)
 
     norm_sums = jnp.stack(
         [
@@ -511,7 +535,10 @@
             jnp.sum(grad_normed_two, axis=0),
         ]
     )
-    norm_total = total_over(norm_sums, "tensor").reshape(-1)
+    norm_total, share_gate_up, share_down = lax.optimization_barrier(
+        (total_over(norm_sums, "tensor"), share_gate_up, share_down)
+    )
+    norm_total = norm_total.reshape(-1)
     bias_total = jnp.sum(bias_sums, axis=0).reshape(-1)
     totals = total_over(jnp.concatenate([norm_total, bias_total]), "dp")
     norm_total = totals[: 4 * width].reshape(4, width)

time: 676 us -> 586 us (0.87)
  waiting for transfers between devices: 301 us -> 203 us
  starting transfers between devices: 39 us -> 59.4 us
  matrix products: 148 us -> 139 us
  local copies, waits for them, and re-layouts: 47 us -> 38.6 us
    reduce_scatter x1, waiting for transfers between devices: 90.4 us -> 0.01 us  [shards(): lax.psum_scatter(grad_wgate_up, 'dp', scatter_dimension=1, tiled=True)]
    ppermute x42 -> x43, starting transfers between devices: 32.9 us -> 44.8 us  [swap(): lax.ppermute(value, axis, [(i, i ^ bit) for i in range(lax.axis_size(axis...]
    ppermute x42 -> x43, waiting for transfers between devices: 175 us -> 167 us  [swap(): lax.ppermute(value, axis, [(i, i ^ bit) for i in range(lax.axis_size(axis...]
    ppermute x6, starting transfers between devices: 5.59 us -> 13.7 us  [ring_step(): lax.ppermute(value, 'dp', [(i, (i + 2) % count) for i in range(count)])]
    unnamed x142 -> x128, local copies, waits for them, and re-layouts: 18.3 us -> 13.4 us
  transfers between devices with their start and end apart: 54 -> 55, of which waited for: 29 -> 28; matrix products, arithmetic and copies ran while one was open for 30% -> 39% of each run, Pallas kernels for 6% -> 7%
where the time goes in v6:
time: 586 us; the launch traced here: 579 us
  waiting for transfers between devices  203 us (35%)
  matrix products  139 us (24%)
  starting transfers between devices  59.4 us (10%)
  other arithmetic  52.2 us (9%)
  Pallas kernels  41.6 us (7%)
  local copies, waits for them, and re-layouts  38.6 us (7%)
  blocking collectives  29.2 us (5%)
  between operations  16.3 us (3%)
    ppermute x43, waiting for transfers between devices, swap(): lax.ppermute(value, axis, [(i, i ^ bit) for i in range(lax.axis_size(axis...  167 us
    ppermute x43, starting transfers between devices, swap(): lax.ppermute(value, axis, [(i, i ^ bit) for i in range(lax.axis_size(axis...  44.8 us
    ppermute x6, waiting for transfers between devices, ring_step(): lax.ppermute(value, 'dp', [(i, (i + 2) % count) for i in range(count)])  34.6 us
    unnamed x1, blocking collectives  29.2 us
    pallas_call x1, Pallas kernels, attend_back(): pl.pallas_call(functools.partial(attend_back_kernel, runs=runs), out_shap...  20.8 us
    pallas_call x1, Pallas kernels, attend(): pl.pallas_call(functools.partial(attend_kernel, runs=runs), out_shape=(ja...  20.8 us
    dot_general x1, matrix products, shards(): jnp.einsum('rd,crk->cdk', after(rows_two, *back_terms), grad_gate_up, pre...  17.6 us
    concatenate x16, other arithmetic, collect_rows(): jnp.concatenate([h, g], axis=0)  14.7 us
  transfers between devices with their start and end apart: 55, of which 28 were waited for; matrix products, arithmetic and copies ran while one was open for 39% of the time, Pallas kernels for 7%

profile of v6, /device:TPU:0, one launch (start us, length us, event | category | flops | bytes accessed | tf_op | source)
XLA Modules:
  0.0 578.6 jit_solution(12488175560874980922)
XLA Ops:
  17.7 29.2 %all-reduce = bf16[9728]{0:T(1024)(128)(2,1)S(1)} all-reduce(bf16[9728]{0:T(1024)(128)(2,1)S(1)} %dynamic-update-slice), channel_id=2, replica_groups=mesh['dp'=8,'tensor'=4] {'dp'}, use_global_device_ids=true, to_apply=%add | all-reduce | flops 9728 | bytes 38912
  57.2 8.1 %collective-permute-done.7 = bf16[256,512]{0,1:T(8,128)(2,1)} collective-permute-done((bf16[256,512]{0,1:T(8,128)(2,1)}, bf16[256,512]{0,1:T(8,128)(2,1)}, u32[]{:S(2)}, u32[]{:S(2)}) %collective-permute-start.7) | collective-permute-done | bytes 262176 | tf_op jit(solution)/shard_map/ppermute | solution.py:139
  70.5 11.3 %collective-permute-done.9 = bf16[256,512]{0,1:T(8,128)(2,1)S(1)} collective-permute-done((bf16[256,512]{0,1:T(8,128)(2,1)}, bf16[256,512]{0,1:T(8,128)(2,1)S(1)}, u32[]{:S(2)}, u32[]{:S(2)}) %collective-permute-start.9) | collective-permute-done | bytes 262176 | tf_op jit(solution)/shard_map/ppermute | solution.py:139
  89.8 12.5 %add_bitcast_fusion.pre_ref = f32[3,1024,512]{2,1,0:T(8,128)} fusion(f32[3,512]{1,0:T(4,128)S(1)} %reshape.180, bf16[3,2048,512]{2,1,0:T(8,128)(2,1)} %all-gather.5.cloned.1.call-done, bf16[1024,2048]{1,0:T(8,128)(2,1)} %copy-done, f32[2048]{0:T(1024)S(1)} %bitcast.145, f32[2048]{0:T(1024)S(1)} %bitcast.139, f32[1024]{0:T(1024)S(1)} %add_rsqrt_fusion, ...), kind=kOutput, calls=%fused_computation.11 | convolution fusion | flops 6456606720 | bytes 16807936 | tf_op jit(solution)/shard_map/rd,cdk->crk/dot_general | solution.py:442
  102.3 20.8 %attend.1 = (bf16[3,2,512,512]{3,2,1,0:T(8,128)(2,1)}, bf16[1024,512]{1,0:T(8,128)(2,1)}, f32[2,512,512]{2,1,0:T(8,128)}) custom-call(s32[8]{0:T(128)} %stack.72.offs_ref, f32[3,1024,512]{2,1,0:T(8,128)} %add_bitcast_fusion.pre_ref, f32[512,128]{1,0:T(8,128)} %concatenate.99.keep_ref.refs_4_, f32[512,128]{1,0:T(8,128)} %concatenate.100.low_ref.refs_5_, ...), custom_call_target="tpu_custom_call" | custom-call | tf_op jit(solution)/shard_map/attend/pallas_call | solution.py:361
  131.6 20.1 %collective-permute-done.12 = bf16[256,2048]{1,0:T(8,128)(2,1)S(1)} collective-permute-done((bf16[256,2048]{1,0:T(8,128)(2,1)S(1)}, bf16[256,2048]{1,0:T(8,128)(2,1)S(1)}, u32[]{:S(2)}, u32[]{:S(2)}) %collective-permute-start.12) | collective-permute-done | bytes 1048608 | tf_op jit(solution)/shard_map/ppermute | solution.py:58
  167.5 8.0 %collective-permute-done.14 = bf16[128,2048]{1,0:T(8,128)(2,1)S(1)} collective-permute-done((bf16[128,2048]{1,0:T(8,128)(2,1)S(1)}, bf16[128,2048]{1,0:T(8,128)(2,1)S(1)}, u32[]{:S(2)}, u32[]{:S(2)}) %collective-permute-start.14) | collective-permute-done | bytes 524320 | tf_op jit(solution)/shard_map/ppermute | solution.py:58
  184.6 12.2 %collective-permute-done.20 = bf16[128,2048]{1,0:T(8,128)(2,1)} collective-permute-done((bf16[128,2048]{1,0:T(8,128)(2,1)}, bf16[128,2048]{1,0:T(8,128)(2,1)}, u32[]{:S(2)}, u32[]{:S(2)}) %collective-permute-start.20) | collective-permute-done | bytes 524320 | tf_op jit(solution)/shard_map/ppermute | solution.py:58
  198.0 12.8 %collective-permute-done.19 = bf16[128,2048]{1,0:T(8,128)(2,1)S(1)} collective-permute-done((bf16[128,2048]{1,0:T(8,128)(2,1)}, bf16[128,2048]{1,0:T(8,128)(2,1)S(1)}, u32[]{:S(2)}, u32[]{:S(2)}) %collective-permute-start.19) | collective-permute-done | bytes 524320 | tf_op jit(solution)/shard_map/ppermute | solution.py:58
  216.7 19.4 %collective-permute-done.22 = bf16[256,2048]{1,0:T(8,128)(2,1)S(1)} collective-permute-done((bf16[256,2048]{1,0:T(8,128)(2,1)S(1)}, bf16[256,2048]{1,0:T(8,128)(2,1)S(1)}, u32[]{:S(2)}, u32[]{:S(2)}) %collective-permute-start.22) | collective-permute-done | bytes 1048608 | tf_op jit(solution)/shard_map/ppermute | solution.py:58
  241.9 12.1 %fusion.12 = f32[1024,1408]{1,0:T(8,128)} fusion(bf16[1024,2048]{1,0:T(8,128)(2,1)} %constant_dynamic-update-slice_fusion.4, bf16[2,2048,1408]{2,1,0:T(8,128)(2,1)} %all-gather.7.cloned.1.call-done), kind=kOutput, calls=%fused_computation.25 | convolution fusion | flops 5905580032 | bytes 15728640 | tf_op jit(solution)/shard_map/dot_general | solution.py:455
  254.0 11.9 %multiply_convert_fusion.2 = (bf16[1024,1408]{1,0:T(8,128)(2,1)S(1)}, f32[1024,1408]{1,0:T(8,128)}) fusion(f32[1024,1408]{1,0:T(8,128)} %fusion.12, bf16[1024,2048]{1,0:T(8,128)(2,1)} %constant_dynamic-update-slice_fusion.4, bf16[2,2048,1408]{2,1,0:T(8,128)(2,1)S(1)} %copy-done.44), kind=kOutput, calls=%fused_computation.19 | convolution fusion | flops 5914230784 | bytes 24379392 | tf_op jit(solution)/shard_map/dot_general | solution.py:456
  267.5 8.0 %convolution_convert_fusion = bf16[1408,2048]{1,0:T(8,128)(2,1)} fusion(bf16[1024,1408]{1,0:T(8,128)(2,1)S(1)} %get-tuple-element.91, bf16[1024,2048]{1,0:T(8,128)(2,1)S(1)} %copy-done.23), kind=kOutput, calls=%fused_computation.9 | convolution fusion | flops 5908463616 | bytes 12845056 | tf_op jit(solution)/shard_map/dot_general | solution.py:461
  276.0 14.1 %multiply_convert_fusion = (bf16[1024,1408]{1,0:T(8,128)(2,1)S(1)}, bf16[1024,1408]{1,0:T(8,128)(2,1)S(1)}) fusion(f32[1024,1408]{1,0:T(8,128)} %fusion.12, f32[1024,1408]{1,0:T(8,128)} %get-tuple-element.198, bf16[1024,2048]{1,0:T(8,128)(2,1)} %copy-done.22, bf16[1408,2048]{1,0:T(8,128)(2,1)} %all-gather.9.cloned.1.call-done), kind=kOutput, calls=%fused_computation.17 | convolution fusion | flops 5924323328 | bytes 27262976 | tf_op jit(solution)/shard_map/dot_general | solution.py:466
  290.2 7.8 %fusion.10 = f32[512,2048]{1,0:T(8,128)} fusion(bf16[2,2048,1408]{2,1,0:T(8,128)(2,1)} %all-gather.7.cloned.1.call-done, bf16[1024,1408]{1,0:T(8,128)(2,1)S(1)} %get-tuple-element.156), kind=kOutput, calls=%fused_computation.23 | convolution fusion | flops 2952790016 | bytes 11403264 | tf_op jit(solution)/shard_map/dot_general | solution.py:475
  314.7 17.6 %convert_bitcast_fusion = bf16[2,2048,1408]{1,2,0:T(8,128)(2,1)} fusion(bf16[1,1024,1408]{2,1,0:T(8,128)(2,1)S(1)} %bitcast.155, bf16[1,1024,1408]{2,1,0:T(8,128)(2,1)S(1)} %bitcast.156, bf16[1024,2048]{1,0:T(8,128)(2,1)} %constant_dynamic-update-slice_fusion.4), kind=kOutput, calls=%fused_computation | convolution fusion | flops 11819810816 | bytes 21495808 | tf_op jit(solution)/shard_map/rd,crk->cdk/dot_general | solution.py:482
  337.0 20.0 %collective-permute-done.24 = bf16[256,2048]{1,0:T(8,128)(2,1)S(1)} collective-permute-done((bf16[256,2048]{1,0:T(8,128)(2,1)S(1)}, bf16[256,2048]{1,0:T(8,128)(2,1)S(1)}, u32[]{:S(2)}, u32[]{:S(2)}) %collective-permute-start.24) | collective-permute-done | bytes 1048608 | tf_op jit(solution)/shard_map/ppermute | solution.py:58
  361.2 9.5 %collective-permute-done.26 = bf16[128,2048]{1,0:T(8,128)(2,1)S(1)} collective-permute-done((bf16[128,2048]{1,0:T(8,128)(2,1)S(1)}, bf16[128,2048]{1,0:T(8,128)(2,1)S(1)}, u32[]{:S(2)}, u32[]{:S(2)}) %collective-permute-start.26) | collective-permute-done | bytes 524320 | tf_op jit(solution)/shard_map/ppermute | solution.py:58
  390.0 9.0 %convolution_convert_fusion.2 = bf16[1024,2048]{1,0:T(8,128)(2,1)S(1)} fusion(bf16[1024,1408]{1,0:T(8,128)(2,1)S(1)} %copy-done.49, bf16[1408,2048]{1,0:T(8,128)(2,1)} %all-gather.9.cloned.1.call-done), kind=kOutput, calls=%fused_computation.36 | convolution fusion | flops 5907677184 | bytes 12845056 | tf_op jit(solution)/shard_map/dot_general | solution.py:497
  399.0 9.4 %collective-permute-done.30 = bf16[256,2048]{1,0:T(8,128)(2,1)S(1)} collective-permute-done((bf16[256,2048]{1,0:T(8,128)(2,1)S(1)}, bf16[256,2048]{1,0:T(8,128)(2,1)S(1)}, u32[]{:S(2)}, u32[]{:S(2)}) %collective-permute-start.30) | collective-permute-done | bytes 1048608 | tf_op jit(solution)/shard_map/ppermute | solution.py:58
  416.7 20.8 %attend_back.1 = (bf16[3,1024,512]{2,1,0:T(8,128)(2,1)}, f32[2,3,512]{2,1,0:T(4,128)}) custom-call(s32[8]{0:T(128)} %stack.72.offs_ref, bf16[3,2,512,512]{3,2,1,0:T(8,128)(2,1)} %get-tuple-element.65.refs_0_, bf16[1024,512]{1,0:T(8,128)(2,1)} %get-tuple-element.108.refs_1_, bf16[1024,512]{1,0:T(8,128)(2,1)} %convolution_convert_fusion.6.refs_2_, ...), custom_call_target="tpu_custom_call" | custom-call | tf_op jit(solution)/shard_map/attend_back/pallas_call | solution.py:382
  437.5 10.6 %convolution_convert_fusion.1 = bf16[3,512,2048]{2,1,0:T(8,128)(2,1)S(1)} fusion(bf16[3,1024,512]{2,1,0:T(8,128)(2,1)} %get-tuple-element.101, bf16[1024,2048]{1,0:T(8,128)(2,1)} %copy-done, f32[2048]{0:T(1024)S(1)} %bitcast.146, f32[2048]{0:T(1024)S(1)} %bitcast.140, f32[1024]{0:T(1024)S(1)} %copy-done.38, f32[1024]{0:T(1024)S(1)} %copy-done.32), kind=kOutput, calls=%fused_computation.22 | convolution fusion | flops 6458179584 | bytes 13656064 | tf_op jit(solution)/shard_map/crk,rd->ckd/dot_general | solution.py:503
  485.6 16.3 %collective-permute-done.36 = bf16[256,2048]{1,0:T(8,128)(2,1)} collective-permute-done((bf16[256,2048]{1,0:T(8,128)(2,1)S(1)}, bf16[256,2048]{1,0:T(8,128)(2,1)}, u32[]{:S(2)}, u32[]{:S(2)}) %collective-permute-start.36) | collective-permute-done | bytes 1048608 | tf_op jit(solution)/shard_map/ppermute | solution.py:58
  513.0 15.1 %collective-permute-done.47 = bf16[512,256]{1,0:T(8,128)(2,1)} collective-permute-done((bf16[512,256]{1,0:T(8,128)(2,1)S(1)}, bf16[512,256]{1,0:T(8,128)(2,1)}, u32[]{:S(2)}, u32[]{:S(2)}) %collective-permute-start.47) | collective-permute-done | bytes 262176 | tf_op jit(solution)/shard_map/ppermute | solution.py:139
  (375 shorter events, 225.6 us)
Async XLA Ops:
  7.3 82.5 %all-gather.5.cloned.1.call-start = ((), (), s32[]{:S(2)}) async-start(), calls=%async_computation.3 | async-start | bytes 7077888 | tf_op jit(solution)/shard_map/all_gather | solution.py:420
  8.0 233.9 %all-gather.7.cloned.1.call-start = ((), (), s32[]{:S(2)}) async-start(), calls=%async_computation.4 | async-start | bytes 12976128 | tf_op jit(solution)/shard_map/all_gather | solution.py:421
  8.7 267.3 %all-gather.9.cloned.1.call-start = ((), (), s32[]{:S(2)}) async-start(), calls=%async_computation.5 | async-start | bytes 6488064 | tf_op jit(solution)/shard_map/all_gather | solution.py:422
  8.8 56.6 %collective-permute-start.4 = (bf16[256,512]{0,1:T(8,128)(2,1)}, bf16[256,512]{0,1:T(8,128)(2,1)}, u32[]{:S(2)}, u32[]{:S(2)}) collective-permute-start(bf16[256,512]{0,1:T(8,128)(2,1)} %bitcast.120), channel_id=1, source_target_pairs={{0,4},{4,0},{8,12},{12,8},{16,20},{20,16},{24,28},{28,24},{1,5},{5... | collective-permute-start | bytes 786440 | tf_op jit(solution)/shard_map/ppermute | solution.py:58
  9.4 39.0 %collective-permute-start.5 = (bf16[256,512]{0,1:T(8,128)(2,1)}, bf16[256,512]{0,1:T(8,128)(2,1)}, u32[]{:S(2)}, u32[]{:S(2)}) collective-permute-start(bf16[256,512]{0,1:T(8,128)(2,1)} %bitcast.121), channel_id=1, source_target_pairs={{0,8},{4,12},{8,16},{12,20},{16,24},{20,28},{24,0},{28,4},{1,9},{5... | collective-permute-start | bytes 786440 | tf_op jit(solution)/shard_map/ppermute | solution.py:139
  12.1 36.5 %collective-permute-start.1 = (bf16[128,2048]{1,0:T(8,128)(2,1)S(1)}, bf16[128,2048]{1,0:T(8,128)(2,1)}, u32[]{:S(2)}, u32[]{:S(2)}) collective-permute-start(bf16[128,2048]{1,0:T(8,128)(2,1)S(1)} %get-tuple-element.184), channel_id=1, source_target_pairs={{0,2},{1,3},{2,0},{3,1},{4,6},{5,7},{6,4},{7,5},{8,10},{9,11},{10,... | collective-permute-start | bytes 1572872 | tf_op jit(solution)/shard_map/ppermute | solution.py:58
  13.7 36.2 %collective-permute-start = (bf16[128,2048]{1,0:T(8,128)(2,1)S(1)}, bf16[128,2048]{1,0:T(8,128)(2,1)}, u32[]{:S(2)}, u32[]{:S(2)}) collective-permute-start(bf16[128,2048]{1,0:T(8,128)(2,1)S(1)} %get-tuple-element.185), channel_id=1, source_target_pairs={{0,1},{1,0},{2,3},{3,2},{4,5},{5,4},{6,7},{7,6},{8,9},{9,8},{10,11... | collective-permute-start | bytes 1572872 | tf_op jit(solution)/shard_map/ppermute | solution.py:58
  52.0 33.6 %collective-permute-start.3 = (bf16[256,2048]{1,0:T(8,128)(2,1)S(1)}, bf16[256,2048]{1,0:T(8,128)(2,1)}, u32[]{:S(2)}, u32[]{:S(2)}) collective-permute-start(bf16[256,2048]{1,0:T(8,128)(2,1)S(1)} %pad_maximum_fusion.12), channel_id=1, source_target_pairs={{0,1},{1,0},{2,3},{3,2},{4,5},{5,4},{6,7},{7,6},{8,9},{9,8},{10,11... | collective-permute-start | bytes 3145736 | tf_op jit(solution)/shard_map/ppermute | solution.py:58
  56.7 30.3 %collective-permute-start.2 = (bf16[256,2048]{1,0:T(8,128)(2,1)}, bf16[256,2048]{1,0:T(8,128)(2,1)S(1)}, u32[]{:S(2)}, u32[]{:S(2)}) collective-permute-start(bf16[256,2048]{1,0:T(8,128)(2,1)} %pad_maximum_fusion.11), channel_id=1, source_target_pairs={{0,2},{1,3},{2,0},{3,1},{4,6},{5,7},{6,4},{7,5},{8,10},{9,11},{10,... | collective-permute-start | bytes 3145736 | tf_op jit(solution)/shard_map/ppermute | solution.py:58
  127.6 26.1 %collective-permute-start.11 = (bf16[256,2048]{1,0:T(8,128)(2,1)S(1)}, bf16[256,2048]{1,0:T(8,128)(2,1)S(1)}, u32[]{:S(2)}, u32[]{:S(2)}) collective-permute-start(bf16[256,2048]{1,0:T(8,128)(2,1)S(1)} %slice.285), channel_id=1, source_target_pairs={{0,2},{1,3},{2,0},{3,1},{4,6},{5,7},{6,4},{7,5},{8,10},{9,11},{10,... | collective-permute-start | bytes 3145736 | tf_op jit(solution)/shard_map/ppermute | solution.py:58
  129.2 33.2 %collective-permute-start.15 = (bf16[128,2048]{1,0:T(8,128)(2,1)S(1)}, bf16[128,2048]{1,0:T(8,128)(2,1)S(1)}, u32[]{:S(2)}, u32[]{:S(2)}) collective-permute-start(bf16[128,2048]{1,0:T(8,128)(2,1)S(1)} %get-tuple-element.181), channel_id=1, source_target_pairs={{0,1},{1,0},{2,3},{3,2},{4,5},{5,4},{6,7},{7,6},{8,9},{9,8},{10,11... | collective-permute-start | bytes 1572872 | tf_op jit(solution)/shard_map/ppermute | solution.py:58
  130.4 34.6 %collective-permute-start.16 = (bf16[128,2048]{1,0:T(8,128)(2,1)S(1)}, bf16[128,2048]{1,0:T(8,128)(2,1)S(1)}, u32[]{:S(2)}, u32[]{:S(2)}) collective-permute-start(bf16[128,2048]{1,0:T(8,128)(2,1)S(1)} %get-tuple-element.180), channel_id=1, source_target_pairs={{0,2},{1,3},{2,0},{3,1},{4,6},{5,7},{6,4},{7,5},{8,10},{9,11},{10,... | collective-permute-start | bytes 1572872 | tf_op jit(solution)/shard_map/ppermute | solution.py:58
  166.0 46.7 %collective-permute-start.18 = (bf16[256,2048]{1,0:T(8,128)(2,1)}, bf16[256,2048]{1,0:T(8,128)(2,1)}, u32[]{:S(2)}, u32[]{:S(2)}) collective-permute-start(bf16[256,2048]{1,0:T(8,128)(2,1)} %pad_maximum_fusion.14), channel_id=1, source_target_pairs={{0,1},{1,0},{2,3},{3,2},{4,5},{5,4},{6,7},{7,6},{8,9},{9,8},{10,11... | collective-permute-start | bytes 3145736 | tf_op jit(solution)/shard_map/ppermute | solution.py:58
  182.2 362.3 %reduce-scatter.6.cloned.1.call-start = ((), (), s32[]{:S(2)}) async-start(), calls=%async_computation.7 | async-start | bytes 6488064 | tf_op jit(solution)/shard_map/reduce_scatter | solution.py:464
  182.4 28.5 %collective-permute-start.19 = (bf16[128,2048]{1,0:T(8,128)(2,1)}, bf16[128,2048]{1,0:T(8,128)(2,1)S(1)}, u32[]{:S(2)}, u32[]{:S(2)}) collective-permute-start(bf16[128,2048]{1,0:T(8,128)(2,1)} %get-tuple-element.183), channel_id=1, source_target_pairs={{0,1},{1,0},{2,3},{3,2},{4,5},{5,4},{6,7},{7,6},{8,9},{9,8},{10,11... | collective-permute-start | bytes 1572872 | tf_op jit(solution)/shard_map/ppermute | solution.py:58
  183.5 32.6 %collective-permute-start.17 = (bf16[256,2048]{1,0:T(8,128)(2,1)S(1)}, bf16[256,2048]{1,0:T(8,128)(2,1)S(1)}, u32[]{:S(2)}, u32[]{:S(2)}) collective-permute-start(bf16[256,2048]{1,0:T(8,128)(2,1)S(1)} %copy-done.12), channel_id=1, source_target_pairs={{0,2},{1,3},{2,0},{3,1},{4,6},{5,7},{6,4},{7,5},{8,10},{9,11},{10,... | collective-permute-start | bytes 3145736 | tf_op jit(solution)/shard_map/ppermute | solution.py:58
  275.5 271.2 %reduce-scatter.4.cloned.1.call-start = ((), (), s32[]{:S(2)}) async-start(), calls=%async_computation.6 | async-start | bytes 12976128 | tf_op jit(solution)/shard_map/reduce_scatter | solution.py:488
  332.3 230.3 %reduce-scatter.8.cloned.1.call-start = ((), (), s32[]{:S(2)}) async-start(), calls=%async_computation.8 | async-start | bytes 3932160 | tf_op jit(solution)/shard_map/reduce_scatter | solution.py:507
  411.8 36.4 %collective-permute-start.31 = (bf16[256,2048]{1,0:T(8,128)(2,1)}, bf16[256,2048]{1,0:T(8,128)(2,1)S(1)}, u32[]{:S(2)}, u32[]{:S(2)}) collective-permute-start(bf16[256,2048]{1,0:T(8,128)(2,1)} %get-tuple-element.168), channel_id=1, source_target_pairs={{0,2},{1,3},{2,0},{3,1},{4,6},{5,7},{6,4},{7,5},{8,10},{9,11},{10,... | collective-permute-start | bytes 3145736 | tf_op jit(solution)/shard_map/ppermute | solution.py:58
  413.0 35.2 %collective-permute-start.32 = (bf16[256,2048]{1,0:T(8,128)(2,1)}, bf16[256,2048]{1,0:T(8,128)(2,1)}, u32[]{:S(2)}, u32[]{:S(2)}) collective-permute-start(bf16[256,2048]{1,0:T(8,128)(2,1)} %get-tuple-element.167), channel_id=1, source_target_pairs={{0,1},{1,0},{2,3},{3,2},{4,5},{5,4},{6,7},{7,6},{8,9},{9,8},{10,11... | collective-permute-start | bytes 3145736 | tf_op jit(solution)/shard_map/ppermute | solution.py:58
  454.3 28.8 %collective-permute-start.44 = (bf16[1536,1024]{1,0:T(8,128)(2,1)S(1)}, bf16[1536,1024]{1,0:T(8,128)(2,1)S(1)}, u32[]{:S(2)}, u32[]{:S(2)}) collective-permute-start(bf16[1536,1024]{1,0:T(8,128)(2,1)S(1)} %pad_maximum_fusion.1), channel_id=1, source_target_pairs={{0,4},{4,0},{8,12},{12,8},{16,20},{20,16},{24,28},{28,24},{1,5},{5... | collective-permute-start | bytes 9437192 | tf_op jit(solution)/shard_map/ppermute | solution.py:58
  479.7 27.2 %collective-permute-start.46 = (bf16[512,256]{1,0:T(8,128)(2,1)S(1)}, bf16[512,256]{1,0:T(8,128)(2,1)}, u32[]{:S(2)}, u32[]{:S(2)}) collective-permute-start(bf16[512,256]{1,0:T(8,128)(2,1)S(1)} %fusion.38), channel_id=1, source_target_pairs={{0,8},{4,12},{8,16},{12,20},{16,24},{20,28},{24,0},{28,4},{1,9},{5... | collective-permute-start | bytes 786440 | tf_op jit(solution)/shard_map/ppermute | solution.py:139
  505.8 28.3 %collective-permute-start.38 = (bf16[128,2048]{1,0:T(8,128)(2,1)S(1)}, bf16[128,2048]{1,0:T(8,128)(2,1)S(1)}, u32[]{:S(2)}, u32[]{:S(2)}) collective-permute-start(bf16[128,2048]{1,0:T(8,128)(2,1)S(1)} %slice.269), channel_id=1, source_target_pairs={{0,2},{1,3},{2,0},{3,1},{4,6},{5,7},{6,4},{7,5},{8,10},{9,11},{10,... | collective-permute-start | bytes 1572872 | tf_op jit(solution)/shard_map/ppermute | solution.py:58
  530.1 27.3 %collective-permute-start.48 = (bf16[512,256]{1,0:T(8,128)(2,1)}, bf16[512,256]{1,0:T(8,128)(2,1)S(1)}, u32[]{:S(2)}, u32[]{:S(2)}) collective-permute-start(bf16[512,256]{1,0:T(8,128)(2,1)} %fusion.42), channel_id=1, source_target_pairs={{0,8},{4,12},{8,16},{12,20},{16,24},{20,28},{24,0},{28,4},{1,9},{5... | collective-permute-start | bytes 786440 | tf_op jit(solution)/shard_map/ppermute | solution.py:139
  (86 other events, 1120.1 us)
Sparse Core Ops, SparseCore 0:
  9.7 78.9 all-gather.4
  90.3 106.6 all-gather.6
  198.5 59.0 all-gather.8
  275.6 68.8 reduce-scatter.5
  346.7 117.6 reduce-scatter.3
  485.7 73.1 reduce-scatter.7

commit v7 on v6

--- a/solution.py
+++ b/solution.py
@@ -190,7 +190,8 @@
             axis=1,
         )
 
-    got = swap(half(1 - core), "dp", 1)
+    other = half(1 - core)
+    got = swap(other, "dp", 1)
     return (half(core).astype(F32) + got.astype(F32)).astype(BF16)
 
 
@@ -511,9 +512,8 @@
         tiled=True,
         axis_index_groups=[list(range(c, dp_count, 2)) for c in range(2)],
     )
-    share_qkv = share_qkv.astype(F32).reshape(3, head_cols, part).transpose(0, 2, 1)
     layer_output = (residual + spread_rows([mlp_terms[at] for at in parts], rows)).astype(BF16)
-    late_pre, layer_output = lax.optimization_barrier((grad_pre, layer_output, grad_wqkv))[:2]
+    late_pre = after(grad_pre, grad_wqkv)
     qkv_terms = [
         jnp.einsum(
             "crk,cdk->rd", late_pre[:, at], qkv_local, preferred_element_type=F32
@@ -522,7 +522,7 @@
     ]
     grad_normed_one = spread_rows(qkv_terms, rows)
     grad_wout = lax.dot_general(
-        after(context, *qkv_terms), resid_rows, TN, preferred_element_type=F32
+        after(context, grad_wqkv), resid_rows, TN, preferred_element_type=F32
     ).astype(BF16)
     share_out = ring_reduce(grad_wout)
     grad_input = grad_resid + norm_back(grad_normed_one * gain_one, hat_one, inv_one)
@@ -541,6 +541,8 @@
     norm_total = norm_total.reshape(-1)
     bias_total = jnp.sum(bias_sums, axis=0).reshape(-1)
     totals = total_over(jnp.concatenate([norm_total, bias_total]), "dp")
+    share_qkv = after(share_qkv, totals)
+    share_qkv = share_qkv.astype(F32).reshape(3, head_cols, part).transpose(0, 2, 1)
     norm_total = totals[: 4 * width].reshape(4, width)
     bias_total = totals[4 * width :].reshape(3, head_cols)
     share_norm = lax.dynamic_slice_in_dim(norm_total, dp_here * part, part, axis=1)

time: 586 us -> 616 us (1.051)
  waiting for transfers between devices: 203 us -> 226 us
  starting transfers between devices: 59.4 us -> 50.1 us
  local copies, waits for them, and re-layouts: 38.6 us -> 47.5 us
  other arithmetic: 52.2 us -> 58.7 us
    reduce_scatter x1, waiting for transfers between devices: 0.01 us -> 27 us  [shards(): lax.psum_scatter(wqkv_half, 'dp', scatter_dimension=1, tiled=True, axis_i...]
    ppermute x6, waiting for transfers between devices: 34.6 us -> 24.6 us  [ring_step(): lax.ppermute(value, 'dp', [(i, (i + 2) % count) for i in range(count)])]
    ppermute x43, waiting for transfers between devices: 167 us -> 173 us  [swap(): lax.ppermute(value, axis, [(i, i ^ bit) for i in range(lax.axis_size(axis...]
    unnamed x128 -> x146, local copies, waits for them, and re-layouts: 13.4 us -> 16.4 us
  transfers between devices with their start and end apart: 55 -> 55, of which waited for: 28 -> 28; matrix products, arithmetic and copies ran while one was open for 39% -> 38% of each run, Pallas kernels for 7% -> 7%
where the time goes in v7:
time: 616 us; the launch traced here: 609 us
  waiting for transfers between devices  226 us (37%)
  matrix products  139 us (23%)
  other arithmetic  58.7 us (10%)
  starting transfers between devices  50.1 us (8%)
  local copies, waits for them, and re-layouts  47.5 us (8%)
  Pallas kernels  41.5 us (7%)
  blocking collectives  29.2 us (5%)
  between operations  16.3 us (3%)
    ppermute x43, waiting for transfers between devices, swap(): lax.ppermute(value, axis, [(i, i ^ bit) for i in range(lax.axis_size(axis...  173 us
    ppermute x43, starting transfers between devices, swap(): lax.ppermute(value, axis, [(i, i ^ bit) for i in range(lax.axis_size(axis...  39.5 us
    unnamed x1, blocking collectives  29.2 us
    reduce_scatter x1, waiting for transfers between devices, shards(): lax.psum_scatter(wqkv_half, 'dp', scatter_dimension=1, tiled=True, axis_i...  27 us
    ppermute x6, waiting for transfers between devices, ring_step(): lax.ppermute(value, 'dp', [(i, (i + 2) % count) for i in range(count)])  24.6 us
    pallas_call x1, Pallas kernels, attend(): pl.pallas_call(functools.partial(attend_kernel, runs=runs), out_shape=(ja...  20.8 us
    pallas_call x1, Pallas kernels, attend_back(): pl.pallas_call(functools.partial(attend_back_kernel, runs=runs), out_shap...  20.7 us
    dot_general x1, matrix products, shards(): jnp.einsum('rd,crk->cdk', after(rows_two, *back_terms), grad_gate_up, pre...  17.6 us
  transfers between devices with their start and end apart: 55, of which 28 were waited for; matrix products, arithmetic and copies ran while one was open for 38% of the time, Pallas kernels for 7%

profile of v7, /device:TPU:0, one launch (start us, length us, event | category | flops | bytes accessed | tf_op | source)
XLA Modules:
  0.0 608.9 jit_solution(13533920020425524341)
XLA Ops:
  17.7 29.2 %all-reduce = bf16[9728]{0:T(1024)(128)(2,1)S(1)} all-reduce(bf16[9728]{0:T(1024)(128)(2,1)S(1)} %dynamic-update-slice), channel_id=2, replica_groups=mesh['dp'=8,'tensor'=4] {'dp'}, use_global_device_ids=true, to_apply=%add | all-reduce | flops 9728 | bytes 38912
  57.2 8.1 %collective-permute-done.7 = bf16[256,512]{0,1:T(8,128)(2,1)} collective-permute-done((bf16[256,512]{0,1:T(8,128)(2,1)}, bf16[256,512]{0,1:T(8,128)(2,1)}, u32[]{:S(2)}, u32[]{:S(2)}) %collective-permute-start.7) | collective-permute-done | bytes 262176 | tf_op jit(solution)/shard_map/ppermute | solution.py:139
  70.5 11.3 %collective-permute-done.9 = bf16[256,512]{0,1:T(8,128)(2,1)S(1)} collective-permute-done((bf16[256,512]{0,1:T(8,128)(2,1)}, bf16[256,512]{0,1:T(8,128)(2,1)S(1)}, u32[]{:S(2)}, u32[]{:S(2)}) %collective-permute-start.9) | collective-permute-done | bytes 262176 | tf_op jit(solution)/shard_map/ppermute | solution.py:139
  89.7 12.6 %add_bitcast_fusion.pre_ref = f32[3,1024,512]{2,1,0:T(8,128)} fusion(f32[3,512]{1,0:T(4,128)S(1)} %reshape.180, bf16[3,2048,512]{2,1,0:T(8,128)(2,1)} %all-gather.5.cloned.1.call-done, bf16[1024,2048]{1,0:T(8,128)(2,1)} %copy-done, f32[2048]{0:T(1024)S(1)} %bitcast.145, f32[2048]{0:T(1024)S(1)} %bitcast.139, f32[1024]{0:T(1024)S(1)} %add_rsqrt_fusion, ...), kind=kOutput, calls=%fused_computation.11 | convolution fusion | flops 6456606720 | bytes 16807936 | tf_op jit(solution)/shard_map/rd,cdk->crk/dot_general | solution.py:443
  102.3 20.8 %attend.1 = (bf16[3,2,512,512]{3,2,1,0:T(8,128)(2,1)}, bf16[1024,512]{1,0:T(8,128)(2,1)}, f32[2,512,512]{2,1,0:T(8,128)}) custom-call(s32[8]{0:T(128)} %stack.72.offs_ref, f32[3,1024,512]{2,1,0:T(8,128)} %add_bitcast_fusion.pre_ref, f32[512,128]{1,0:T(8,128)} %concatenate.99.keep_ref.refs_4_, f32[512,128]{1,0:T(8,128)} %concatenate.100.low_ref.refs_5_, ...), custom_call_target="tpu_custom_call" | custom-call | tf_op jit(solution)/shard_map/attend/pallas_call | solution.py:362
  131.6 20.1 %collective-permute-done.12 = bf16[256,2048]{1,0:T(8,128)(2,1)S(1)} collective-permute-done((bf16[256,2048]{1,0:T(8,128)(2,1)S(1)}, bf16[256,2048]{1,0:T(8,128)(2,1)S(1)}, u32[]{:S(2)}, u32[]{:S(2)}) %collective-permute-start.12) | collective-permute-done | bytes 1048608 | tf_op jit(solution)/shard_map/ppermute | solution.py:58
  167.5 8.0 %collective-permute-done.14 = bf16[128,2048]{1,0:T(8,128)(2,1)S(1)} collective-permute-done((bf16[128,2048]{1,0:T(8,128)(2,1)S(1)}, bf16[128,2048]{1,0:T(8,128)(2,1)S(1)}, u32[]{:S(2)}, u32[]{:S(2)}) %collective-permute-start.14) | collective-permute-done | bytes 524320 | tf_op jit(solution)/shard_map/ppermute | solution.py:58
  184.0 12.2 %collective-permute-done.20 = bf16[128,2048]{1,0:T(8,128)(2,1)} collective-permute-done((bf16[128,2048]{1,0:T(8,128)(2,1)}, bf16[128,2048]{1,0:T(8,128)(2,1)}, u32[]{:S(2)}, u32[]{:S(2)}) %collective-permute-start.20) | collective-permute-done | bytes 524320 | tf_op jit(solution)/shard_map/ppermute | solution.py:58
  197.5 13.4 %collective-permute-done.19 = bf16[128,2048]{1,0:T(8,128)(2,1)S(1)} collective-permute-done((bf16[128,2048]{1,0:T(8,128)(2,1)}, bf16[128,2048]{1,0:T(8,128)(2,1)S(1)}, u32[]{:S(2)}, u32[]{:S(2)}) %collective-permute-start.19) | collective-permute-done | bytes 524320 | tf_op jit(solution)/shard_map/ppermute | solution.py:58
  216.1 20.1 %collective-permute-done.22 = bf16[256,2048]{1,0:T(8,128)(2,1)S(1)} collective-permute-done((bf16[256,2048]{1,0:T(8,128)(2,1)S(1)}, bf16[256,2048]{1,0:T(8,128)(2,1)S(1)}, u32[]{:S(2)}, u32[]{:S(2)}) %collective-permute-start.22) | collective-permute-done | bytes 1048608 | tf_op jit(solution)/shard_map/ppermute | solution.py:58
  241.7 12.1 %fusion.12 = f32[1024,1408]{1,0:T(8,128)} fusion(bf16[1024,2048]{1,0:T(8,128)(2,1)} %constant_dynamic-update-slice_fusion.4, bf16[2,2048,1408]{2,1,0:T(8,128)(2,1)} %all-gather.7.cloned.1.call-done), kind=kOutput, calls=%fused_computation.25 | convolution fusion | flops 5905580032 | bytes 15728640 | tf_op jit(solution)/shard_map/dot_general | solution.py:456
  253.8 11.9 %multiply_convert_fusion.2 = (bf16[1024,1408]{1,0:T(8,128)(2,1)S(1)}, f32[1024,1408]{1,0:T(8,128)}) fusion(f32[1024,1408]{1,0:T(8,128)} %fusion.12, bf16[1024,2048]{1,0:T(8,128)(2,1)} %constant_dynamic-update-slice_fusion.4, bf16[2,2048,1408]{2,1,0:T(8,128)(2,1)S(1)} %copy-done.53), kind=kOutput, calls=%fused_computation.19 | convolution fusion | flops 5914230784 | bytes 24379392 | tf_op jit(solution)/shard_map/dot_general | solution.py:457
  267.3 8.0 %convolution_convert_fusion = bf16[1408,2048]{1,0:T(8,128)(2,1)} fusion(bf16[1024,1408]{1,0:T(8,128)(2,1)S(1)} %get-tuple-element.90, bf16[1024,2048]{1,0:T(8,128)(2,1)S(1)} %copy-done.34), kind=kOutput, calls=%fused_computation.9 | convolution fusion | flops 5908463616 | bytes 12845056 | tf_op jit(solution)/shard_map/dot_general | solution.py:462
  275.8 14.1 %multiply_convert_fusion = (bf16[1024,1408]{1,0:T(8,128)(2,1)S(1)}, bf16[1024,1408]{1,0:T(8,128)(2,1)S(1)}) fusion(f32[1024,1408]{1,0:T(8,128)} %fusion.12, f32[1024,1408]{1,0:T(8,128)} %get-tuple-element.198, bf16[1024,2048]{1,0:T(8,128)(2,1)} %copy-done.33, bf16[1408,2048]{1,0:T(8,128)(2,1)} %all-gather.9.cloned.1.call-done), kind=kOutput, calls=%fused_computation.17 | convolution fusion | flops 5924323328 | bytes 27262976 | tf_op jit(solution)/shard_map/dot_general | solution.py:467
  289.9 7.8 %fusion.10 = f32[512,2048]{1,0:T(8,128)} fusion(bf16[2,2048,1408]{2,1,0:T(8,128)(2,1)} %all-gather.7.cloned.1.call-done, bf16[1024,1408]{1,0:T(8,128)(2,1)S(1)} %get-tuple-element.156), kind=kOutput, calls=%fused_computation.23 | convolution fusion | flops 2952790016 | bytes 11403264 | tf_op jit(solution)/shard_map/dot_general | solution.py:476
  314.4 17.6 %convert_bitcast_fusion = bf16[2,2048,1408]{1,2,0:T(8,128)(2,1)} fusion(bf16[1,1024,1408]{2,1,0:T(8,128)(2,1)S(1)} %bitcast.155, bf16[1,1024,1408]{2,1,0:T(8,128)(2,1)S(1)} %bitcast.156, bf16[1024,2048]{1,0:T(8,128)(2,1)} %constant_dynamic-update-slice_fusion.4), kind=kOutput, calls=%fused_computation | convolution fusion | flops 11819810816 | bytes 21495808 | tf_op jit(solution)/shard_map/rd,crk->cdk/dot_general | solution.py:483
  336.8 19.8 %collective-permute-done.24 = bf16[256,2048]{1,0:T(8,128)(2,1)S(1)} collective-permute-done((bf16[256,2048]{1,0:T(8,128)(2,1)S(1)}, bf16[256,2048]{1,0:T(8,128)(2,1)S(1)}, u32[]{:S(2)}, u32[]{:S(2)}) %collective-permute-start.24) | collective-permute-done | bytes 1048608 | tf_op jit(solution)/shard_map/ppermute | solution.py:58
  360.9 9.6 %collective-permute-done.26 = bf16[128,2048]{1,0:T(8,128)(2,1)S(1)} collective-permute-done((bf16[128,2048]{1,0:T(8,128)(2,1)S(1)}, bf16[128,2048]{1,0:T(8,128)(2,1)S(1)}, u32[]{:S(2)}, u32[]{:S(2)}) %collective-permute-start.26) | collective-permute-done | bytes 524320 | tf_op jit(solution)/shard_map/ppermute | solution.py:58
  389.6 11.1 %convolution_convert_fusion.2 = bf16[1024,2048]{1,0:T(8,128)(2,1)} fusion(bf16[1024,1408]{1,0:T(8,128)(2,1)S(1)} %copy-done.58, bf16[1408,2048]{1,0:T(8,128)(2,1)} %all-gather.9.cloned.1.call-done), kind=kOutput, calls=%fused_computation.36 | convolution fusion | flops 5907677184 | bytes 12845056 | tf_op jit(solution)/shard_map/dot_general | solution.py:498
  413.7 20.7 %attend_back.1 = (bf16[3,1024,512]{2,1,0:T(8,128)(2,1)}, f32[2,3,512]{2,1,0:T(4,128)}) custom-call(s32[8]{0:T(128)} %stack.72.offs_ref, bf16[3,2,512,512]{3,2,1,0:T(8,128)(2,1)} %get-tuple-element.96.refs_0_, bf16[1024,512]{1,0:T(8,128)(2,1)} %get-tuple-element.108.refs_1_, bf16[1024,512]{1,0:T(8,128)(2,1)} %convolution_convert_fusion.6.refs_2_, ...), custom_call_target="tpu_custom_call" | custom-call | tf_op jit(solution)/shard_map/attend_back/pallas_call | solution.py:383
  434.5 10.7 %convolution_convert_fusion.1 = bf16[3,512,2048]{2,1,0:T(8,128)(2,1)S(1)} fusion(bf16[3,1024,512]{2,1,0:T(8,128)(2,1)} %get-tuple-element.100, bf16[1024,2048]{1,0:T(8,128)(2,1)} %copy-done, f32[2048]{0:T(1024)S(1)} %bitcast.146, f32[2048]{0:T(1024)S(1)} %bitcast.140, f32[1024]{0:T(1024)S(1)} %copy-done.48, f32[1024]{0:T(1024)S(1)} %copy-done.42), kind=kOutput, calls=%fused_computation.22 | convolution fusion | flops 6458179584 | bytes 13656064 | tf_op jit(solution)/shard_map/crk,rd->ckd/dot_general | solution.py:504
  473.7 13.1 %collective-permute-done.36 = bf16[256,2048]{1,0:T(8,128)(2,1)S(1)} collective-permute-done((bf16[256,2048]{1,0:T(8,128)(2,1)}, bf16[256,2048]{1,0:T(8,128)(2,1)S(1)}, u32[]{:S(2)}, u32[]{:S(2)}) %collective-permute-start.36) | collective-permute-done | bytes 1048608 | tf_op jit(solution)/shard_map/ppermute | solution.py:58
  498.4 17.9 %collective-permute-done.31 = bf16[256,2048]{1,0:T(8,128)(2,1)S(1)} collective-permute-done((bf16[256,2048]{1,0:T(8,128)(2,1)S(1)}, bf16[256,2048]{1,0:T(8,128)(2,1)S(1)}, u32[]{:S(2)}, u32[]{:S(2)}) %collective-permute-start.31) | collective-permute-done | bytes 1048608 | tf_op jit(solution)/shard_map/ppermute | solution.py:58
  570.7 27.0 %reduce-scatter.8.cloned.1.call-done = bf16[1536,256]{1,0:T(8,128)(2,1)} async-done(((bf16[1536,1024]{1,0:T(8,128)(2,1)}), bf16[1536,256]{1,0:T(8,128)(2,1)}) %reduce-scatter.8.cloned.1.call-update) | async-done | bytes 786448 | tf_op jit(solution)/shard_map/reduce_scatter | solution.py:508
  (393 shorter events, 235.5 us)
Async XLA Ops:
  7.3 82.5 %all-gather.5.cloned.1.call-start = ((), (), s32[]{:S(2)}) async-start(), calls=%async_computation.3 | async-start | bytes 7077888 | tf_op jit(solution)/shard_map/all_gather | solution.py:421
  8.0 233.7 %all-gather.7.cloned.1.call-start = ((), (), s32[]{:S(2)}) async-start(), calls=%async_computation.4 | async-start | bytes 12976128 | tf_op jit(solution)/shard_map/all_gather | solution.py:422
  8.7 267.0 %all-gather.9.cloned.1.call-start = ((), (), s32[]{:S(2)}) async-start(), calls=%async_computation.5 | async-start | bytes 6488064 | tf_op jit(solution)/shard_map/all_gather | solution.py:423
  8.8 56.6 %collective-permute-start.4 = (bf16[256,512]{0,1:T(8,128)(2,1)}, bf16[256,512]{0,1:T(8,128)(2,1)}, u32[]{:S(2)}, u32[]{:S(2)}) collective-permute-start(bf16[256,512]{0,1:T(8,128)(2,1)} %bitcast.120), channel_id=1, source_target_pairs={{0,4},{4,0},{8,12},{12,8},{16,20},{20,16},{24,28},{28,24},{1,5},{5... | collective-permute-start | bytes 786440 | tf_op jit(solution)/shard_map/ppermute | solution.py:58
  9.4 39.0 %collective-permute-start.5 = (bf16[256,512]{0,1:T(8,128)(2,1)}, bf16[256,512]{0,1:T(8,128)(2,1)}, u32[]{:S(2)}, u32[]{:S(2)}) collective-permute-start(bf16[256,512]{0,1:T(8,128)(2,1)} %bitcast.121), channel_id=1, source_target_pairs={{0,8},{4,12},{8,16},{12,20},{16,24},{20,28},{24,0},{28,4},{1,9},{5... | collective-permute-start | bytes 786440 | tf_op jit(solution)/shard_map/ppermute | solution.py:139
  12.1 36.5 %collective-permute-start = (bf16[128,2048]{1,0:T(8,128)(2,1)S(1)}, bf16[128,2048]{1,0:T(8,128)(2,1)}, u32[]{:S(2)}, u32[]{:S(2)}) collective-permute-start(bf16[128,2048]{1,0:T(8,128)(2,1)S(1)} %get-tuple-element.185), channel_id=1, source_target_pairs={{0,1},{1,0},{2,3},{3,2},{4,5},{5,4},{6,7},{7,6},{8,9},{9,8},{10,11... | collective-permute-start | bytes 1572872 | tf_op jit(solution)/shard_map/ppermute | solution.py:58
  13.7 36.2 %collective-permute-start.1 = (bf16[128,2048]{1,0:T(8,128)(2,1)S(1)}, bf16[128,2048]{1,0:T(8,128)(2,1)}, u32[]{:S(2)}, u32[]{:S(2)}) collective-permute-start(bf16[128,2048]{1,0:T(8,128)(2,1)S(1)} %get-tuple-element.184), channel_id=1, source_target_pairs={{0,2},{1,3},{2,0},{3,1},{4,6},{5,7},{6,4},{7,5},{8,10},{9,11},{10,... | collective-permute-start | bytes 1572872 | tf_op jit(solution)/shard_map/ppermute | solution.py:58
  52.0 33.6 %collective-permute-start.2 = (bf16[256,2048]{1,0:T(8,128)(2,1)S(1)}, bf16[256,2048]{1,0:T(8,128)(2,1)}, u32[]{:S(2)}, u32[]{:S(2)}) collective-permute-start(bf16[256,2048]{1,0:T(8,128)(2,1)S(1)} %pad_maximum_fusion.11), channel_id=1, source_target_pairs={{0,2},{1,3},{2,0},{3,1},{4,6},{5,7},{6,4},{7,5},{8,10},{9,11},{10,... | collective-permute-start | bytes 3145736 | tf_op jit(solution)/shard_map/ppermute | solution.py:58
  56.6 30.4 %collective-permute-start.3 = (bf16[256,2048]{1,0:T(8,128)(2,1)}, bf16[256,2048]{1,0:T(8,128)(2,1)S(1)}, u32[]{:S(2)}, u32[]{:S(2)}) collective-permute-start(bf16[256,2048]{1,0:T(8,128)(2,1)} %pad_maximum_fusion.12), channel_id=1, source_target_pairs={{0,1},{1,0},{2,3},{3,2},{4,5},{5,4},{6,7},{7,6},{8,9},{9,8},{10,11... | collective-permute-start | bytes 3145736 | tf_op jit(solution)/shard_map/ppermute | solution.py:58
  129.3 33.2 %collective-permute-start.15 = (bf16[128,2048]{1,0:T(8,128)(2,1)S(1)}, bf16[128,2048]{1,0:T(8,128)(2,1)S(1)}, u32[]{:S(2)}, u32[]{:S(2)}) collective-permute-start(bf16[128,2048]{1,0:T(8,128)(2,1)S(1)} %get-tuple-element.181), channel_id=1, source_target_pairs={{0,1},{1,0},{2,3},{3,2},{4,5},{5,4},{6,7},{7,6},{8,9},{9,8},{10,11... | collective-permute-start | bytes 1572872 | tf_op jit(solution)/shard_map/ppermute | solution.py:58
  130.4 34.6 %collective-permute-start.16 = (bf16[128,2048]{1,0:T(8,128)(2,1)S(1)}, bf16[128,2048]{1,0:T(8,128)(2,1)S(1)}, u32[]{:S(2)}, u32[]{:S(2)}) collective-permute-start(bf16[128,2048]{1,0:T(8,128)(2,1)S(1)} %get-tuple-element.180), channel_id=1, source_target_pairs={{0,2},{1,3},{2,0},{3,1},{4,6},{5,7},{6,4},{7,5},{8,10},{9,11},{10,... | collective-permute-start | bytes 1572872 | tf_op jit(solution)/shard_map/ppermute | solution.py:58
  166.0 46.6 %collective-permute-start.18 = (bf16[256,2048]{1,0:T(8,128)(2,1)}, bf16[256,2048]{1,0:T(8,128)(2,1)}, u32[]{:S(2)}, u32[]{:S(2)}) collective-permute-start(bf16[256,2048]{1,0:T(8,128)(2,1)} %pad_maximum_fusion.14), channel_id=1, source_target_pairs={{0,1},{1,0},{2,3},{3,2},{4,5},{5,4},{6,7},{7,6},{8,9},{9,8},{10,11... | collective-permute-start | bytes 3145736 | tf_op jit(solution)/shard_map/ppermute | solution.py:58
  181.6 367.6 %reduce-scatter.6.cloned.1.call-start = ((), (), s32[]{:S(2)}) async-start(), calls=%async_computation.7 | async-start | bytes 6488064 | tf_op jit(solution)/shard_map/reduce_scatter | solution.py:465
  181.9 29.0 %collective-permute-start.19 = (bf16[128,2048]{1,0:T(8,128)(2,1)}, bf16[128,2048]{1,0:T(8,128)(2,1)S(1)}, u32[]{:S(2)}, u32[]{:S(2)}) collective-permute-start(bf16[128,2048]{1,0:T(8,128)(2,1)} %get-tuple-element.183), channel_id=1, source_target_pairs={{0,1},{1,0},{2,3},{3,2},{4,5},{5,4},{6,7},{7,6},{8,9},{9,8},{10,11... | collective-permute-start | bytes 1572872 | tf_op jit(solution)/shard_map/ppermute | solution.py:58
  183.0 32.4 %collective-permute-start.17 = (bf16[256,2048]{1,0:T(8,128)(2,1)S(1)}, bf16[256,2048]{1,0:T(8,128)(2,1)S(1)}, u32[]{:S(2)}, u32[]{:S(2)}) collective-permute-start(bf16[256,2048]{1,0:T(8,128)(2,1)S(1)} %copy-done.12), channel_id=1, source_target_pairs={{0,2},{1,3},{2,0},{3,1},{4,6},{5,7},{6,4},{7,5},{8,10},{9,11},{10,... | collective-permute-start | bytes 3145736 | tf_op jit(solution)/shard_map/ppermute | solution.py:58
  275.3 276.3 %reduce-scatter.4.cloned.1.call-start = ((), (), s32[]{:S(2)}) async-start(), calls=%async_computation.6 | async-start | bytes 12976128 | tf_op jit(solution)/shard_map/reduce_scatter | solution.py:489
  332.0 265.7 %reduce-scatter.8.cloned.1.call-start = ((), (), s32[]{:S(2)}) async-start(), calls=%async_computation.8 | async-start | bytes 3932160 | tf_op jit(solution)/shard_map/reduce_scatter | solution.py:508
  453.6 69.3 %collective-permute-start.44 = (bf16[1536,1024]{1,0:T(8,128)(2,1)}, bf16[1536,1024]{1,0:T(8,128)(2,1)}, u32[]{:S(2)}, u32[]{:S(2)}) collective-permute-start(bf16[1536,1024]{1,0:T(8,128)(2,1)} %pad_maximum_fusion.1), channel_id=1, source_target_pairs={{0,4},{4,0},{8,12},{12,8},{16,20},{20,16},{24,28},{28,24},{1,5},{5... | collective-permute-start | bytes 9437192 | tf_op jit(solution)/shard_map/ppermute | solution.py:58
  470.3 46.0 %collective-permute-start.31 = (bf16[256,2048]{1,0:T(8,128)(2,1)S(1)}, bf16[256,2048]{1,0:T(8,128)(2,1)S(1)}, u32[]{:S(2)}, u32[]{:S(2)}) collective-permute-start(bf16[256,2048]{1,0:T(8,128)(2,1)S(1)} %get-tuple-element.168), channel_id=1, source_target_pairs={{0,2},{1,3},{2,0},{3,1},{4,6},{5,7},{6,4},{7,5},{8,10},{9,11},{10,... | collective-permute-start | bytes 3145736 | tf_op jit(solution)/shard_map/ppermute | solution.py:58
  471.6 45.8 %collective-permute-start.32 = (bf16[256,2048]{1,0:T(8,128)(2,1)S(1)}, bf16[256,2048]{1,0:T(8,128)(2,1)S(1)}, u32[]{:S(2)}, u32[]{:S(2)}) collective-permute-start(bf16[256,2048]{1,0:T(8,128)(2,1)S(1)} %get-tuple-element.167), channel_id=1, source_target_pairs={{0,1},{1,0},{2,3},{3,2},{4,5},{5,4},{6,7},{7,6},{8,9},{9,8},{10,11... | collective-permute-start | bytes 3145736 | tf_op jit(solution)/shard_map/ppermute | solution.py:58
  487.8 33.1 %collective-permute-start.46 = (bf16[512,256]{1,0:T(8,128)(2,1)S(1)}, bf16[512,256]{1,0:T(8,128)(2,1)S(1)}, u32[]{:S(2)}, u32[]{:S(2)}) collective-permute-start(bf16[512,256]{1,0:T(8,128)(2,1)S(1)} %fusion.38), channel_id=1, source_target_pairs={{0,8},{4,12},{8,16},{12,20},{16,24},{20,28},{24,0},{28,4},{1,9},{5... | collective-permute-start | bytes 786440 | tf_op jit(solution)/shard_map/ppermute | solution.py:139
  496.5 40.7 %collective-permute-start.38 = (bf16[128,2048]{1,0:T(8,128)(2,1)}, bf16[128,2048]{1,0:T(8,128)(2,1)}, u32[]{:S(2)}, u32[]{:S(2)}) collective-permute-start(bf16[128,2048]{1,0:T(8,128)(2,1)} %slice.269), channel_id=1, source_target_pairs={{0,2},{1,3},{2,0},{3,1},{4,6},{5,7},{6,4},{7,5},{8,10},{9,11},{10,... | collective-permute-start | bytes 1572872 | tf_op jit(solution)/shard_map/ppermute | solution.py:58
  519.2 27.6 %collective-permute-start.34 = (bf16[128,2048]{1,0:T(8,128)(2,1)}, bf16[128,2048]{1,0:T(8,128)(2,1)}, u32[]{:S(2)}, u32[]{:S(2)}) collective-permute-start(bf16[128,2048]{1,0:T(8,128)(2,1)} %slice.259), channel_id=1, source_target_pairs={{0,2},{1,3},{2,0},{3,1},{4,6},{5,7},{6,4},{7,5},{8,10},{9,11},{10,... | collective-permute-start | bytes 1572872 | tf_op jit(solution)/shard_map/ppermute | solution.py:58
  520.9 34.0 %collective-permute-start.33 = (bf16[128,2048]{1,0:T(8,128)(2,1)}, bf16[128,2048]{1,0:T(8,128)(2,1)}, u32[]{:S(2)}, u32[]{:S(2)}) collective-permute-start(bf16[128,2048]{1,0:T(8,128)(2,1)} %slice.257), channel_id=1, source_target_pairs={{0,1},{1,0},{2,3},{3,2},{4,5},{5,4},{6,7},{7,6},{8,9},{9,8},{10,11... | collective-permute-start | bytes 1572872 | tf_op jit(solution)/shard_map/ppermute | solution.py:58
  (95 other events, 1226.6 us)
Sparse Core Ops, SparseCore 0:
  9.7 78.9 all-gather.4
  90.3 106.6 all-gather.6
  198.5 59.0 all-gather.8
  275.4 68.9 reduce-scatter.5
  346.5 117.6 reduce-scatter.3
  530.3 67.3 reduce-scatter.7

commit v8 on v7

--- a/solution.py
+++ b/solution.py
@@ -171,9 +171,9 @@
         return columns(owners[k]).astype(F32) + other[k].astype(F32)
 
     total = block(1)
-    for k in list(range(2, len(owners))) + [0]:
+    for k in range(2, len(owners)):
         total = block(k) + ring_step(total.astype(BF16)).astype(F32)
-    return total
+    return block(0), ring_step(total.astype(BF16))
 
 
 def core_halves(grad):
@@ -524,7 +524,7 @@
     grad_wout = lax.dot_general(
         after(context, grad_wqkv), resid_rows, TN, preferred_element_type=F32
     ).astype(BF16)
-    share_out = ring_reduce(grad_wout)
+    own_out, got_out = ring_reduce(grad_wout)
     grad_input = grad_resid + norm_back(grad_normed_one * gain_one, hat_one, inv_one)
 
     norm_sums = jnp.stack(
@@ -542,6 +542,7 @@
     bias_total = jnp.sum(bias_sums, axis=0).reshape(-1)
     totals = total_over(jnp.concatenate([norm_total, bias_total]), "dp")
     share_qkv = after(share_qkv, totals)
+    share_out = own_out + after(got_out, totals).astype(F32)
     share_qkv = share_qkv.astype(F32).reshape(3, head_cols, part).transpose(0, 2, 1)
     norm_total = totals[: 4 * width].reshape(4, width)
     bias_total = totals[4 * width :].reshape(3, head_cols)

time: 616 us -> 598 us (0.971)
  waiting for transfers between devices: 226 us -> 200 us
    reduce_scatter x1, waiting for transfers between devices: 27 us -> 12.6 us  [shards(): lax.psum_scatter(wqkv_half, 'dp', scatter_dimension=1, tiled=True, axis_i...]
    ppermute x43, waiting for transfers between devices: 173 us -> 164 us  [swap(): lax.ppermute(value, axis, [(i, i ^ bit) for i in range(lax.axis_size(axis...]
    unnamed x146 -> x144, local copies, waits for them, and re-layouts: 16.4 us -> 16.4 us
  transfers between devices with their start and end apart: 55 -> 55, of which waited for: 28 -> 28; matrix products, arithmetic and copies ran while one was open for 38% -> 40% of each run, Pallas kernels for 7% -> 7%
where the time goes in v8:
time: 598 us; the launch traced here: 591 us
  waiting for transfers between devices  200 us (33%)
  matrix products  139 us (23%)
  other arithmetic  61.2 us (10%)
  starting transfers between devices  54.1 us (9%)
  local copies, waits for them, and re-layouts  49 us (8%)
  Pallas kernels  41.5 us (7%)
  blocking collectives  29.2 us (5%)
  between operations  16.3 us (3%)
    ppermute x43, waiting for transfers between devices, swap(): lax.ppermute(value, axis, [(i, i ^ bit) for i in range(lax.axis_size(axis...  164 us
    ppermute x43, starting transfers between devices, swap(): lax.ppermute(value, axis, [(i, i ^ bit) for i in range(lax.axis_size(axis...  43.7 us
    unnamed x1, blocking collectives  29.2 us
    ppermute x6, waiting for transfers between devices, ring_step(): lax.ppermute(value, 'dp', [(i, (i + 2) % count) for i in range(count)])  22 us
    pallas_call x1, Pallas kernels, attend(): pl.pallas_call(functools.partial(attend_kernel, runs=runs), out_shape=(ja...  20.8 us
    pallas_call x1, Pallas kernels, attend_back(): pl.pallas_call(functools.partial(attend_back_kernel, runs=runs), out_shap...  20.8 us
    dot_general x1, matrix products, shards(): jnp.einsum('rd,crk->cdk', after(rows_two, *back_terms), grad_gate_up, pre...  17.6 us
    unnamed x144, local copies, waits for them, and re-layouts  16.4 us
  transfers between devices with their start and end apart: 55, of which 28 were waited for; matrix products, arithmetic and copies ran while one was open for 40% of the time, Pallas kernels for 7%

profile of v8, /device:TPU:0, one launch (start us, length us, event | category | flops | bytes accessed | tf_op | source)
XLA Modules:
  0.0 590.9 jit_solution(9118475638641796201)
XLA Ops:
  17.7 29.2 %all-reduce = bf16[9728]{0:T(1024)(128)(2,1)S(1)} all-reduce(bf16[9728]{0:T(1024)(128)(2,1)S(1)} %dynamic-update-slice), channel_id=2, replica_groups=mesh['dp'=8,'tensor'=4] {'dp'}, use_global_device_ids=true, to_apply=%add | all-reduce | flops 9728 | bytes 38912
  57.3 8.0 %collective-permute-done.7 = bf16[256,512]{0,1:T(8,128)(2,1)} collective-permute-done((bf16[256,512]{0,1:T(8,128)(2,1)}, bf16[256,512]{0,1:T(8,128)(2,1)}, u32[]{:S(2)}, u32[]{:S(2)}) %collective-permute-start.7) | collective-permute-done | bytes 262176 | tf_op jit(solution)/shard_map/ppermute | solution.py:139
  70.5 11.3 %collective-permute-done.9 = bf16[256,512]{0,1:T(8,128)(2,1)S(1)} collective-permute-done((bf16[256,512]{0,1:T(8,128)(2,1)}, bf16[256,512]{0,1:T(8,128)(2,1)S(1)}, u32[]{:S(2)}, u32[]{:S(2)}) %collective-permute-start.9) | collective-permute-done | bytes 262176 | tf_op jit(solution)/shard_map/ppermute | solution.py:139
  89.7 12.6 %add_bitcast_fusion.pre_ref = f32[3,1024,512]{2,1,0:T(8,128)} fusion(f32[3,512]{1,0:T(4,128)S(1)} %reshape.180, bf16[3,2048,512]{2,1,0:T(8,128)(2,1)} %all-gather.5.cloned.1.call-done, bf16[1024,2048]{1,0:T(8,128)(2,1)} %copy-done, f32[2048]{0:T(1024)S(1)} %bitcast.145, f32[2048]{0:T(1024)S(1)} %bitcast.139, f32[1024]{0:T(1024)S(1)} %add_rsqrt_fusion, ...), kind=kOutput, calls=%fused_computation.11 | convolution fusion | flops 6456606720 | bytes 16807936 | tf_op jit(solution)/shard_map/rd,cdk->crk/dot_general | solution.py:443
  102.3 20.8 %attend.1 = (bf16[3,2,512,512]{3,2,1,0:T(8,128)(2,1)}, bf16[1024,512]{1,0:T(8,128)(2,1)}, f32[2,512,512]{2,1,0:T(8,128)}) custom-call(s32[8]{0:T(128)} %stack.72.offs_ref, f32[3,1024,512]{2,1,0:T(8,128)} %add_bitcast_fusion.pre_ref, f32[512,128]{1,0:T(8,128)} %concatenate.99.keep_ref.refs_4_, f32[512,128]{1,0:T(8,128)} %concatenate.100.low_ref.refs_5_, ...), custom_call_target="tpu_custom_call" | custom-call | tf_op jit(solution)/shard_map/attend/pallas_call | solution.py:362
  131.6 20.1 %collective-permute-done.12 = bf16[256,2048]{1,0:T(8,128)(2,1)S(1)} collective-permute-done((bf16[256,2048]{1,0:T(8,128)(2,1)S(1)}, bf16[256,2048]{1,0:T(8,128)(2,1)S(1)}, u32[]{:S(2)}, u32[]{:S(2)}) %collective-permute-start.12) | collective-permute-done | bytes 1048608 | tf_op jit(solution)/shard_map/ppermute | solution.py:58
  167.5 8.0 %collective-permute-done.14 = bf16[128,2048]{1,0:T(8,128)(2,1)S(1)} collective-permute-done((bf16[128,2048]{1,0:T(8,128)(2,1)S(1)}, bf16[128,2048]{1,0:T(8,128)(2,1)S(1)}, u32[]{:S(2)}, u32[]{:S(2)}) %collective-permute-start.14) | collective-permute-done | bytes 524320 | tf_op jit(solution)/shard_map/ppermute | solution.py:58
  184.0 12.2 %collective-permute-done.20 = bf16[128,2048]{1,0:T(8,128)(2,1)} collective-permute-done((bf16[128,2048]{1,0:T(8,128)(2,1)}, bf16[128,2048]{1,0:T(8,128)(2,1)}, u32[]{:S(2)}, u32[]{:S(2)}) %collective-permute-start.20) | collective-permute-done | bytes 524320 | tf_op jit(solution)/shard_map/ppermute | solution.py:58
  197.5 13.4 %collective-permute-done.19 = bf16[128,2048]{1,0:T(8,128)(2,1)S(1)} collective-permute-done((bf16[128,2048]{1,0:T(8,128)(2,1)}, bf16[128,2048]{1,0:T(8,128)(2,1)S(1)}, u32[]{:S(2)}, u32[]{:S(2)}) %collective-permute-start.19) | collective-permute-done | bytes 524320 | tf_op jit(solution)/shard_map/ppermute | solution.py:58
  216.1 20.1 %collective-permute-done.22 = bf16[256,2048]{1,0:T(8,128)(2,1)S(1)} collective-permute-done((bf16[256,2048]{1,0:T(8,128)(2,1)S(1)}, bf16[256,2048]{1,0:T(8,128)(2,1)S(1)}, u32[]{:S(2)}, u32[]{:S(2)}) %collective-permute-start.22) | collective-permute-done | bytes 1048608 | tf_op jit(solution)/shard_map/ppermute | solution.py:58
  241.7 12.1 %fusion.12 = f32[1024,1408]{1,0:T(8,128)} fusion(bf16[1024,2048]{1,0:T(8,128)(2,1)} %constant_dynamic-update-slice_fusion.4, bf16[2,2048,1408]{2,1,0:T(8,128)(2,1)} %all-gather.7.cloned.1.call-done), kind=kOutput, calls=%fused_computation.25 | convolution fusion | flops 5905580032 | bytes 15728640 | tf_op jit(solution)/shard_map/dot_general | solution.py:456
  253.8 11.9 %multiply_convert_fusion.2 = (bf16[1024,1408]{1,0:T(8,128)(2,1)S(1)}, f32[1024,1408]{1,0:T(8,128)}) fusion(f32[1024,1408]{1,0:T(8,128)} %fusion.12, bf16[1024,2048]{1,0:T(8,128)(2,1)} %constant_dynamic-update-slice_fusion.4, bf16[2,2048,1408]{2,1,0:T(8,128)(2,1)S(1)} %copy-done.52), kind=kOutput, calls=%fused_computation.19 | convolution fusion | flops 5914230784 | bytes 24379392 | tf_op jit(solution)/shard_map/dot_general | solution.py:457
  267.3 8.0 %convolution_convert_fusion = bf16[1408,2048]{1,0:T(8,128)(2,1)} fusion(bf16[1024,1408]{1,0:T(8,128)(2,1)S(1)} %get-tuple-element.91, bf16[1024,2048]{1,0:T(8,128)(2,1)S(1)} %copy-done.33), kind=kOutput, calls=%fused_computation.9 | convolution fusion | flops 5908463616 | bytes 12845056 | tf_op jit(solution)/shard_map/dot_general | solution.py:462
  275.8 14.1 %multiply_convert_fusion = (bf16[1024,1408]{1,0:T(8,128)(2,1)S(1)}, bf16[1024,1408]{1,0:T(8,128)(2,1)S(1)}) fusion(f32[1024,1408]{1,0:T(8,128)} %fusion.12, f32[1024,1408]{1,0:T(8,128)} %get-tuple-element.200, bf16[1024,2048]{1,0:T(8,128)(2,1)} %copy-done.32, bf16[1408,2048]{1,0:T(8,128)(2,1)} %all-gather.9.cloned.1.call-done), kind=kOutput, calls=%fused_computation.17 | convolution fusion | flops 5924323328 | bytes 27262976 | tf_op jit(solution)/shard_map/dot_general | solution.py:467
  289.9 7.8 %fusion.10 = f32[512,2048]{1,0:T(8,128)} fusion(bf16[2,2048,1408]{2,1,0:T(8,128)(2,1)} %all-gather.7.cloned.1.call-done, bf16[1024,1408]{1,0:T(8,128)(2,1)S(1)} %get-tuple-element.158), kind=kOutput, calls=%fused_computation.23 | convolution fusion | flops 2952790016 | bytes 11403264 | tf_op jit(solution)/shard_map/dot_general | solution.py:476
  314.4 17.6 %convert_bitcast_fusion = bf16[2,2048,1408]{1,2,0:T(8,128)(2,1)} fusion(bf16[1,1024,1408]{2,1,0:T(8,128)(2,1)S(1)} %bitcast.155, bf16[1,1024,1408]{2,1,0:T(8,128)(2,1)S(1)} %bitcast.156, bf16[1024,2048]{1,0:T(8,128)(2,1)} %constant_dynamic-update-slice_fusion.4), kind=kOutput, calls=%fused_computation | convolution fusion | flops 11819810816 | bytes 21495808 | tf_op jit(solution)/shard_map/rd,crk->cdk/dot_general | solution.py:483
  336.9 19.8 %collective-permute-done.24 = bf16[256,2048]{1,0:T(8,128)(2,1)S(1)} collective-permute-done((bf16[256,2048]{1,0:T(8,128)(2,1)S(1)}, bf16[256,2048]{1,0:T(8,128)(2,1)S(1)}, u32[]{:S(2)}, u32[]{:S(2)}) %collective-permute-start.24) | collective-permute-done | bytes 1048608 | tf_op jit(solution)/shard_map/ppermute | solution.py:58
  360.9 9.6 %collective-permute-done.26 = bf16[128,2048]{1,0:T(8,128)(2,1)S(1)} collective-permute-done((bf16[128,2048]{1,0:T(8,128)(2,1)S(1)}, bf16[128,2048]{1,0:T(8,128)(2,1)S(1)}, u32[]{:S(2)}, u32[]{:S(2)}) %collective-permute-start.26) | collective-permute-done | bytes 524320 | tf_op jit(solution)/shard_map/ppermute | solution.py:58
  389.7 11.1 %convolution_convert_fusion.2 = bf16[1024,2048]{1,0:T(8,128)(2,1)} fusion(bf16[1024,1408]{1,0:T(8,128)(2,1)S(1)} %copy-done.57, bf16[1408,2048]{1,0:T(8,128)(2,1)} %all-gather.9.cloned.1.call-done), kind=kOutput, calls=%fused_computation.36 | convolution fusion | flops 5907677184 | bytes 12845056 | tf_op jit(solution)/shard_map/dot_general | solution.py:498
  413.8 20.8 %attend_back.1 = (bf16[3,1024,512]{2,1,0:T(8,128)(2,1)}, f32[2,3,512]{2,1,0:T(4,128)}) custom-call(s32[8]{0:T(128)} %stack.72.offs_ref, bf16[3,2,512,512]{3,2,1,0:T(8,128)(2,1)} %get-tuple-element.97.refs_0_, bf16[1024,512]{1,0:T(8,128)(2,1)} %get-tuple-element.109.refs_1_, bf16[1024,512]{1,0:T(8,128)(2,1)} %convolution_convert_fusion.6.refs_2_, ...), custom_call_target="tpu_custom_call" | custom-call | tf_op jit(solution)/shard_map/attend_back/pallas_call | solution.py:383
  434.6 10.7 %convolution_convert_fusion.1 = bf16[3,512,2048]{2,1,0:T(8,128)(2,1)S(1)} fusion(bf16[3,1024,512]{2,1,0:T(8,128)(2,1)} %get-tuple-element.101, bf16[1024,2048]{1,0:T(8,128)(2,1)} %copy-done, f32[2048]{0:T(1024)S(1)} %bitcast.146, f32[2048]{0:T(1024)S(1)} %bitcast.140, f32[1024]{0:T(1024)S(1)} %copy-done.47, f32[1024]{0:T(1024)S(1)} %copy-done.41), kind=kOutput, calls=%fused_computation.22 | convolution fusion | flops 6458179584 | bytes 13656064 | tf_op jit(solution)/shard_map/crk,rd->ckd/dot_general | solution.py:504
  475.1 11.8 %collective-permute-done.36 = bf16[256,2048]{1,0:T(8,128)(2,1)S(1)} collective-permute-done((bf16[256,2048]{1,0:T(8,128)(2,1)}, bf16[256,2048]{1,0:T(8,128)(2,1)S(1)}, u32[]{:S(2)}, u32[]{:S(2)}) %collective-permute-start.36) | collective-permute-done | bytes 1048608 | tf_op jit(solution)/shard_map/ppermute | solution.py:58
  508.1 8.4 %collective-permute-done.31 = bf16[256,2048]{1,0:T(8,128)(2,1)} collective-permute-done((bf16[256,2048]{1,0:T(8,128)(2,1)}, bf16[256,2048]{1,0:T(8,128)(2,1)}, u32[]{:S(2)}, u32[]{:S(2)}) %collective-permute-start.31) | collective-permute-done | bytes 1048608 | tf_op jit(solution)/shard_map/ppermute | solution.py:58
  565.1 12.6 %reduce-scatter.8.cloned.1.call-done = bf16[1536,256]{1,0:T(8,128)(2,1)} async-done(((bf16[1536,1024]{1,0:T(8,128)(2,1)}), bf16[1536,256]{1,0:T(8,128)(2,1)}) %reduce-scatter.8.cloned.1.call-update) | async-done | bytes 786448 | tf_op jit(solution)/shard_map/reduce_scatter | solution.py:508
  (391 shorter events, 242.7 us)
Async XLA Ops:
  7.3 82.5 %all-gather.5.cloned.1.call-start = ((), (), s32[]{:S(2)}) async-start(), calls=%async_computation.3 | async-start | bytes 7077888 | tf_op jit(solution)/shard_map/all_gather | solution.py:421
  8.0 233.7 %all-gather.7.cloned.1.call-start = ((), (), s32[]{:S(2)}) async-start(), calls=%async_computation.4 | async-start | bytes 12976128 | tf_op jit(solution)/shard_map/all_gather | solution.py:422
  8.7 267.0 %all-gather.9.cloned.1.call-start = ((), (), s32[]{:S(2)}) async-start(), calls=%async_computation.5 | async-start | bytes 6488064 | tf_op jit(solution)/shard_map/all_gather | solution.py:423
  8.8 56.6 %collective-permute-start.4 = (bf16[256,512]{0,1:T(8,128)(2,1)}, bf16[256,512]{0,1:T(8,128)(2,1)}, u32[]{:S(2)}, u32[]{:S(2)}) collective-permute-start(bf16[256,512]{0,1:T(8,128)(2,1)} %bitcast.120), channel_id=1, source_target_pairs={{0,4},{4,0},{8,12},{12,8},{16,20},{20,16},{24,28},{28,24},{1,5},{5... | collective-permute-start | bytes 786440 | tf_op jit(solution)/shard_map/ppermute | solution.py:58
  9.4 39.0 %collective-permute-start.5 = (bf16[256,512]{0,1:T(8,128)(2,1)}, bf16[256,512]{0,1:T(8,128)(2,1)}, u32[]{:S(2)}, u32[]{:S(2)}) collective-permute-start(bf16[256,512]{0,1:T(8,128)(2,1)} %bitcast.121), channel_id=1, source_target_pairs={{0,8},{4,12},{8,16},{12,20},{16,24},{20,28},{24,0},{28,4},{1,9},{5... | collective-permute-start | bytes 786440 | tf_op jit(solution)/shard_map/ppermute | solution.py:139
  12.1 36.5 %collective-permute-start = (bf16[128,2048]{1,0:T(8,128)(2,1)S(1)}, bf16[128,2048]{1,0:T(8,128)(2,1)}, u32[]{:S(2)}, u32[]{:S(2)}) collective-permute-start(bf16[128,2048]{1,0:T(8,128)(2,1)S(1)} %get-tuple-element.187), channel_id=1, source_target_pairs={{0,1},{1,0},{2,3},{3,2},{4,5},{5,4},{6,7},{7,6},{8,9},{9,8},{10,11... | collective-permute-start | bytes 1572872 | tf_op jit(solution)/shard_map/ppermute | solution.py:58
  13.7 36.2 %collective-permute-start.1 = (bf16[128,2048]{1,0:T(8,128)(2,1)S(1)}, bf16[128,2048]{1,0:T(8,128)(2,1)}, u32[]{:S(2)}, u32[]{:S(2)}) collective-permute-start(bf16[128,2048]{1,0:T(8,128)(2,1)S(1)} %get-tuple-element.186), channel_id=1, source_target_pairs={{0,2},{1,3},{2,0},{3,1},{4,6},{5,7},{6,4},{7,5},{8,10},{9,11},{10,... | collective-permute-start | bytes 1572872 | tf_op jit(solution)/shard_map/ppermute | solution.py:58
  52.0 33.6 %collective-permute-start.2 = (bf16[256,2048]{1,0:T(8,128)(2,1)S(1)}, bf16[256,2048]{1,0:T(8,128)(2,1)}, u32[]{:S(2)}, u32[]{:S(2)}) collective-permute-start(bf16[256,2048]{1,0:T(8,128)(2,1)S(1)} %pad_maximum_fusion.11), channel_id=1, source_target_pairs={{0,2},{1,3},{2,0},{3,1},{4,6},{5,7},{6,4},{7,5},{8,10},{9,11},{10,... | collective-permute-start | bytes 3145736 | tf_op jit(solution)/shard_map/ppermute | solution.py:58
  56.7 30.3 %collective-permute-start.3 = (bf16[256,2048]{1,0:T(8,128)(2,1)}, bf16[256,2048]{1,0:T(8,128)(2,1)S(1)}, u32[]{:S(2)}, u32[]{:S(2)}) collective-permute-start(bf16[256,2048]{1,0:T(8,128)(2,1)} %pad_maximum_fusion.12), channel_id=1, source_target_pairs={{0,1},{1,0},{2,3},{3,2},{4,5},{5,4},{6,7},{7,6},{8,9},{9,8},{10,11... | collective-permute-start | bytes 3145736 | tf_op jit(solution)/shard_map/ppermute | solution.py:58
  129.3 33.2 %collective-permute-start.15 = (bf16[128,2048]{1,0:T(8,128)(2,1)S(1)}, bf16[128,2048]{1,0:T(8,128)(2,1)S(1)}, u32[]{:S(2)}, u32[]{:S(2)}) collective-permute-start(bf16[128,2048]{1,0:T(8,128)(2,1)S(1)} %get-tuple-element.183), channel_id=1, source_target_pairs={{0,1},{1,0},{2,3},{3,2},{4,5},{5,4},{6,7},{7,6},{8,9},{9,8},{10,11... | collective-permute-start | bytes 1572872 | tf_op jit(solution)/shard_map/ppermute | solution.py:58
  130.4 34.6 %collective-permute-start.16 = (bf16[128,2048]{1,0:T(8,128)(2,1)S(1)}, bf16[128,2048]{1,0:T(8,128)(2,1)S(1)}, u32[]{:S(2)}, u32[]{:S(2)}) collective-permute-start(bf16[128,2048]{1,0:T(8,128)(2,1)S(1)} %get-tuple-element.182), channel_id=1, source_target_pairs={{0,2},{1,3},{2,0},{3,1},{4,6},{5,7},{6,4},{7,5},{8,10},{9,11},{10,... | collective-permute-start | bytes 1572872 | tf_op jit(solution)/shard_map/ppermute | solution.py:58
  166.0 46.6 %collective-permute-start.18 = (bf16[256,2048]{1,0:T(8,128)(2,1)}, bf16[256,2048]{1,0:T(8,128)(2,1)}, u32[]{:S(2)}, u32[]{:S(2)}) collective-permute-start(bf16[256,2048]{1,0:T(8,128)(2,1)} %pad_maximum_fusion.14), channel_id=1, source_target_pairs={{0,1},{1,0},{2,3},{3,2},{4,5},{5,4},{6,7},{7,6},{8,9},{9,8},{10,11... | collective-permute-start | bytes 3145736 | tf_op jit(solution)/shard_map/ppermute | solution.py:58
  181.6 359.0 %reduce-scatter.6.cloned.1.call-start = ((), (), s32[]{:S(2)}) async-start(), calls=%async_computation.7 | async-start | bytes 6488064 | tf_op jit(solution)/shard_map/reduce_scatter | solution.py:465
  181.9 29.0 %collective-permute-start.19 = (bf16[128,2048]{1,0:T(8,128)(2,1)}, bf16[128,2048]{1,0:T(8,128)(2,1)S(1)}, u32[]{:S(2)}, u32[]{:S(2)}) collective-permute-start(bf16[128,2048]{1,0:T(8,128)(2,1)} %get-tuple-element.185), channel_id=1, source_target_pairs={{0,1},{1,0},{2,3},{3,2},{4,5},{5,4},{6,7},{7,6},{8,9},{9,8},{10,11... | collective-permute-start | bytes 1572872 | tf_op jit(solution)/shard_map/ppermute | solution.py:58
  183.0 32.4 %collective-permute-start.17 = (bf16[256,2048]{1,0:T(8,128)(2,1)S(1)}, bf16[256,2048]{1,0:T(8,128)(2,1)S(1)}, u32[]{:S(2)}, u32[]{:S(2)}) collective-permute-start(bf16[256,2048]{1,0:T(8,128)(2,1)S(1)} %copy-done.11), channel_id=1, source_target_pairs={{0,2},{1,3},{2,0},{3,1},{4,6},{5,7},{6,4},{7,5},{8,10},{9,11},{10,... | collective-permute-start | bytes 3145736 | tf_op jit(solution)/shard_map/ppermute | solution.py:58
  275.3 267.6 %reduce-scatter.4.cloned.1.call-start = ((), (), s32[]{:S(2)}) async-start(), calls=%async_computation.6 | async-start | bytes 12976128 | tf_op jit(solution)/shard_map/reduce_scatter | solution.py:489
  332.0 245.7 %reduce-scatter.8.cloned.1.call-start = ((), (), s32[]{:S(2)}) async-start(), calls=%async_computation.8 | async-start | bytes 3932160 | tf_op jit(solution)/shard_map/reduce_scatter | solution.py:508
  453.7 49.9 %collective-permute-start.44 = (bf16[1536,1024]{1,0:T(8,128)(2,1)}, bf16[1536,1024]{1,0:T(8,128)(2,1)}, u32[]{:S(2)}, u32[]{:S(2)}) collective-permute-start(bf16[1536,1024]{1,0:T(8,128)(2,1)} %pad_maximum_fusion.1), channel_id=1, source_target_pairs={{0,4},{4,0},{8,12},{12,8},{16,20},{20,16},{24,28},{28,24},{1,5},{5... | collective-permute-start | bytes 9437192 | tf_op jit(solution)/shard_map/ppermute | solution.py:58
  471.7 44.7 %collective-permute-start.31 = (bf16[256,2048]{1,0:T(8,128)(2,1)}, bf16[256,2048]{1,0:T(8,128)(2,1)}, u32[]{:S(2)}, u32[]{:S(2)}) collective-permute-start(bf16[256,2048]{1,0:T(8,128)(2,1)} %get-tuple-element.170), channel_id=1, source_target_pairs={{0,2},{1,3},{2,0},{3,1},{4,6},{5,7},{6,4},{7,5},{8,10},{9,11},{10,... | collective-permute-start | bytes 3145736 | tf_op jit(solution)/shard_map/ppermute | solution.py:58
  473.0 43.5 %collective-permute-start.32 = (bf16[256,2048]{1,0:T(8,128)(2,1)}, bf16[256,2048]{1,0:T(8,128)(2,1)}, u32[]{:S(2)}, u32[]{:S(2)}) collective-permute-start(bf16[256,2048]{1,0:T(8,128)(2,1)} %get-tuple-element.169), channel_id=1, source_target_pairs={{0,1},{1,0},{2,3},{3,2},{4,5},{5,4},{6,7},{7,6},{8,9},{9,8},{10,11... | collective-permute-start | bytes 3145736 | tf_op jit(solution)/shard_map/ppermute | solution.py:58
  496.5 32.3 %collective-permute-start.38 = (bf16[128,2048]{1,0:T(8,128)(2,1)}, bf16[128,2048]{1,0:T(8,128)(2,1)}, u32[]{:S(2)}, u32[]{:S(2)}) collective-permute-start(bf16[128,2048]{1,0:T(8,128)(2,1)} %slice.269), channel_id=1, source_target_pairs={{0,2},{1,3},{2,0},{3,1},{4,6},{5,7},{6,4},{7,5},{8,10},{9,11},{10,... | collective-permute-start | bytes 1572872 | tf_op jit(solution)/shard_map/ppermute | solution.py:58
  501.0 29.0 %collective-permute-start.37 = (bf16[128,2048]{1,0:T(8,128)(2,1)}, bf16[128,2048]{1,0:T(8,128)(2,1)}, u32[]{:S(2)}, u32[]{:S(2)}) collective-permute-start(bf16[128,2048]{1,0:T(8,128)(2,1)} %slice.267), channel_id=1, source_target_pairs={{0,1},{1,0},{2,3},{3,2},{4,5},{5,4},{6,7},{7,6},{8,9},{9,8},{10,11... | collective-permute-start | bytes 1572872 | tf_op jit(solution)/shard_map/ppermute | solution.py:58
  522.5 28.7 %collective-permute-start.33 = (bf16[128,2048]{1,0:T(8,128)(2,1)}, bf16[128,2048]{1,0:T(8,128)(2,1)}, u32[]{:S(2)}, u32[]{:S(2)}) collective-permute-start(bf16[128,2048]{1,0:T(8,128)(2,1)} %slice.257), channel_id=1, source_target_pairs={{0,1},{1,0},{2,3},{3,2},{4,5},{5,4},{6,7},{7,6},{8,9},{9,8},{10,11... | collective-permute-start | bytes 1572872 | tf_op jit(solution)/shard_map/ppermute | solution.py:58
  525.8 39.3 %collective-permute-start.48 = (bf16[512,256]{1,0:T(8,128)(2,1)}, bf16[512,256]{1,0:T(8,128)(2,1)S(1)}, u32[]{:S(2)}, u32[]{:S(2)}) collective-permute-start(bf16[512,256]{1,0:T(8,128)(2,1)} %fusion.42), channel_id=1, source_target_pairs={{0,8},{4,12},{8,16},{12,20},{16,24},{20,28},{24,0},{28,4},{1,9},{5... | collective-permute-start | bytes 786440 | tf_op jit(solution)/shard_map/ppermute | solution.py:139
  (94 other events, 1240.5 us)
Sparse Core Ops, SparseCore 0:
  9.7 78.9 all-gather.4
  90.3 106.6 all-gather.6
  198.5 59.0 all-gather.8
  275.4 68.9 reduce-scatter.5
  346.5 117.6 reduce-scatter.3
  508.2 69.4 reduce-scatter.7
